TPU v7x, 32 devices: a whole 2x2x4 slice. The times are simulated.
32 devices in a mesh: ctx: 4 (over y, core), exp: 8 (over z, x).
Axes of the slice: x: 2, y: 2, z: 4, core: 2. Of those that a mesh axis runs over, the one named last changes fastest.
Arguments:
- layer_input: bfloat16 [8, 1536, 2048], P('exp', 'ctx'), may hold values from -30 to 30
- block_ids: int32 [8, 8], P('exp'), may hold values from 0 to 7, as said below
- routes: int32 [8, 1536, 8], P('exp', 'ctx'), may hold values from 0 to 15, all different within a row
- w_query: bfloat16 [2048, 2048], P('exp'), may hold values from -0.125 to 0.125
- w_key: bfloat16 [2048, 2048], P('exp'), may hold values from -0.125 to 0.125
- w_value: bfloat16 [2048, 2048], P('exp'), may hold values from -0.125 to 0.125
- w_output: bfloat16 [2048, 2048], P('exp'), may hold values from -2 to 2
- w_router: bfloat16 [2048, 16], P('exp'), may hold values from -0.0625 to 0.0625
- norm_gains: bfloat16 [2048, 4], P('exp'), may hold values from 0.25 to 1.75
- w_gate_up: bfloat16 [16, 4096, 1024], P('exp', None, 'ctx'), may hold values from -0.125 to 0.125
- w_down: bfloat16 [16, 2048, 1024], P('exp', None, 'ctx'), may hold values from -4 to 4
- d_out: bfloat16 [8, 1536, 2048], P('exp', 'ctx'), may hold values from -6 to 6
Outputs:
- output: bfloat16 [8, 1536, 2048], P('exp', 'ctx')
- d_x: float32 [8, 1536, 2048], P('exp', 'ctx')
- g_query: float32 [2048, 2048], P('exp')
- g_key: float32 [2048, 2048], P('exp')
- g_value: float32 [2048, 2048], P('exp')
- g_output: float32 [2048, 2048], P('exp')
- g_router: float32 [2048, 16], P('exp')
- g_gains: float32 [2048, 4], P('exp')
- g_gate_up: float32 [16, 4096, 1024], P('exp', None, 'ctx')
- g_down: float32 [16, 2048, 1024], P('exp', None, 'ctx')
Inputs may be any that keep to these rules, and one draw needn't show every extreme that they name: `block_ids`: each row holds each block number once; the two blocks of one device add up to 7. `routes`: each token names 8 different experts.
All inputs are finite; a program needn't handle non-finite values.
Results may differ from a plain program's by a relative error of at most 0.025.
Values may be sent and summed in bfloat16 or wider, within the bound.
A program may use at most 448 MiB of HBM per device.

v0:
```python
import jax
import jax.numpy as jnp
from jax import lax
from jax.sharding import PartitionSpec as P

HEAD_DIM = 128


epsilon = 1e-05
rope_theta = 10000.0


def rms_scale(matrix, gain):
    return matrix * lax.rsqrt(jnp.mean(matrix * matrix, axis=-1, keepdims=True) + epsilon) * gain


def angle_tables(positions, head_width):
    half_width = head_width // 2
    inverse = rope_theta ** (-(jnp.arange(half_width, dtype=jnp.float32) * 2.0) / head_width)
    angles = positions.astype(jnp.float32)[:, None] * inverse[None, :]
    angles = jnp.concatenate([angles, angles], axis=-1)
    return (jnp.cos(angles), jnp.sin(angles))


def rotate(matrix, cosine, sine, head_count, head_width):
    row_count = matrix.shape[0]
    split_heads = matrix.reshape(row_count, head_count, head_width)
    half_width = head_width // 2
    turned = jnp.concatenate(
        [-split_heads[..., half_width:], split_heads[..., :half_width]], axis=-1
    )
    result = split_heads * cosine[:, None, :] + turned * sine[:, None, :]
    return result.reshape(row_count, head_count * head_width)


def all_positions(block_row, half_rows):
    offsets = jnp.arange(half_rows, dtype=jnp.int32)
    return (block_row[:, None] * half_rows + offsets[None, :]).reshape(-1)


def slot_table(route_rows, expert_count, capacity):
    flat_routes = route_rows.reshape(-1)
    onehot = (flat_routes[:, None] == jnp.arange(expert_count, dtype=jnp.int32)[None, :]).astype(
        jnp.int32
    )
    rank_of = jnp.sum(jnp.cumsum(onehot, axis=0) * onehot, axis=1) - 1
    kept_mask = rank_of < capacity
    pair_slot = jnp.where(kept_mask, flat_routes * capacity + rank_of, expert_count * capacity)
    return (pair_slot, kept_mask)


def per_device(
    layer_input,
    block_ids,
    routes,
    w_query,
    w_key,
    w_value,
    w_output,
    w_router,
    norm_gains,
    w_gate_up,
    w_down,
    d_out,
):
    query_full, key_full, value_full, output_full, router_full, gains_bf = (
        lax.all_gather(w_query, "exp", axis=0, tiled=True),
        lax.all_gather(w_key, "exp", axis=0, tiled=True),
        lax.all_gather(w_value, "exp", axis=0, tiled=True),
        lax.all_gather(w_output, "exp", axis=0, tiled=True),
        lax.all_gather(w_router, "exp", axis=0, tiled=True),
        lax.all_gather(norm_gains, "exp", axis=0, tiled=True),
    )
    gain_table = gains_bf.astype(jnp.float32)
    tokens = layer_input[0].astype(jnp.float32)
    row_count, model_width = tokens.shape
    head_width = HEAD_DIM
    head_count = model_width // head_width
    half_rows = row_count // 2
    key_positions = all_positions(block_ids[0], half_rows)
    device_index = lax.axis_index("ctx")
    query_positions = lax.dynamic_slice_in_dim(key_positions, device_index * row_count, row_count)
    cosine, sine = angle_tables(query_positions, head_width)
    score_scale = head_width ** (-0.5)

    def norm_rope(projected, gain):
        return rotate(rms_scale(projected, gain), cosine, sine, head_count, head_width)

    first_norm = rms_scale(tokens, gain_table[:, 0]).astype(jnp.bfloat16)
    query_pre = jnp.dot(first_norm, query_full, preferred_element_type=jnp.float32)
    key_pre = jnp.dot(first_norm, key_full, preferred_element_type=jnp.float32)
    own_values = jnp.dot(first_norm, value_full, preferred_element_type=jnp.float32).astype(
        jnp.bfloat16
    )
    query = norm_rope(query_pre, gain_table[:, 1]).astype(jnp.bfloat16)
    own_keys = norm_rope(key_pre, gain_table[:, 2]).astype(jnp.bfloat16)
    all_keys, all_values = (
        lax.all_gather(own_keys, "ctx", axis=0, tiled=True),
        lax.all_gather(own_values, "ctx", axis=0, tiled=True),
    )
    seq_length = all_keys.shape[0]
    query_heads = query.reshape(row_count, head_count, head_width)
    key_heads = all_keys.reshape(seq_length, head_count, head_width)
    value_heads = all_values.reshape(seq_length, head_count, head_width)
    visible = key_positions[None, :] <= query_positions[:, None]

    def scores_of():
        raw_scores = (
            jnp.einsum("qhd,khd->hqk", query_heads, key_heads, preferred_element_type=jnp.float32)
            * score_scale
        )
        return jnp.where(visible[None], raw_scores, -1e30)

    scores = scores_of()
    top_score = jnp.max(scores, axis=-1, keepdims=True)
    log_total = top_score + jnp.log(jnp.sum(jnp.exp(scores - top_score), axis=-1, keepdims=True))
    probs_low = jnp.exp(scores - log_total).astype(jnp.bfloat16)
    attended = (
        jnp.einsum("hqk,khd->qhd", probs_low, value_heads, preferred_element_type=jnp.float32)
        .reshape(row_count, model_width)
        .astype(jnp.bfloat16)
    )
    hidden = tokens + jnp.dot(attended, output_full, preferred_element_type=jnp.float32)
    second_norm = rms_scale(hidden, gain_table[:, 3]).astype(jnp.bfloat16)
    logits = jnp.dot(second_norm, router_full, preferred_element_type=jnp.float32)
    router_probs = jax.nn.softmax(logits, axis=-1)
    expert_count = router_full.shape[1]
    route_rows = routes[0]
    top_count = route_rows.shape[1]
    chosen_mask = (
        route_rows[..., None] == jnp.arange(expert_count, dtype=jnp.int32)[None, None, :]
    ).astype(jnp.float32)
    gates = jnp.sum(chosen_mask * router_probs[:, None, :], axis=-1)
    capacity = (5 * row_count * top_count + 4 * expert_count - 1) // (4 * expert_count)
    pair_slot, kept_mask = slot_table(route_rows, expert_count, capacity)
    slot_total = expert_count * capacity
    pair_rows = jnp.repeat(second_norm, top_count, axis=0)
    send_rows = jnp.zeros((slot_total + 1, model_width), jnp.bfloat16).at[pair_slot].set(pair_rows)
    send_rows = send_rows[:slot_total].reshape(expert_count, capacity, model_width)
    arrived = lax.all_to_all(send_rows, "exp", split_axis=0, concat_axis=1, tiled=True)
    gate_up_full, down_full = (
        lax.all_gather(w_gate_up, "ctx", axis=2, tiled=True),
        lax.all_gather(w_down, "ctx", axis=2, tiled=True),
    )
    gate_full = gate_up_full[:, :model_width]
    up_full = gate_up_full[:, model_width:]
    gate_pre = jnp.einsum("erd,edf->erf", arrived, gate_full, preferred_element_type=jnp.float32)
    up_pre = jnp.einsum("erd,edf->erf", arrived, up_full, preferred_element_type=jnp.float32)
    activated = jax.nn.silu(gate_pre)
    inner = (activated * up_pre).astype(jnp.bfloat16)
    expert_out = jnp.einsum(
        "erf,edf->erd", inner, down_full, preferred_element_type=jnp.float32
    ).astype(jnp.bfloat16)
    returned = lax.all_to_all(expert_out, "exp", split_axis=1, concat_axis=0, tiled=True)
    padded_out = jnp.concatenate(
        [returned.reshape(slot_total, model_width), jnp.zeros((1, model_width), jnp.bfloat16)],
        axis=0,
    )
    pair_out = padded_out[pair_slot].astype(jnp.float32).reshape(row_count, top_count, model_width)
    mixture = jnp.sum(gates[..., None] * pair_out, axis=1)
    output = (hidden + mixture).astype(jnp.bfloat16)[None]
    grad_out = d_out[0].astype(jnp.float32)
    pair_weight = jnp.where(kept_mask, gates.reshape(-1), 0.0)
    pair_grad = (pair_weight[:, None] * jnp.repeat(grad_out, top_count, axis=0)).astype(
        jnp.bfloat16
    )
    send_grad = jnp.zeros((slot_total + 1, model_width), jnp.bfloat16).at[pair_slot].set(pair_grad)
    send_grad = send_grad[:slot_total].reshape(expert_count, capacity, model_width)
    gate_grad = jnp.sum(pair_out * grad_out[:, None, :], axis=-1)
    out_grad = lax.all_to_all(send_grad, "exp", split_axis=0, concat_axis=1, tiled=True)
    gate_up_again, down_back = (
        lax.all_gather(w_gate_up, "ctx", axis=2, tiled=True),
        lax.all_gather(w_down, "ctx", axis=2, tiled=True),
    )
    gate_back = gate_up_again[:, :model_width]
    up_back = gate_up_again[:, model_width:]
    inner_grad = jnp.einsum("erd,edf->erf", out_grad, down_back, preferred_element_type=jnp.float32)
    sigmoid_gate = jax.nn.sigmoid(gate_pre)
    gate_pre_grad = (
        inner_grad * up_pre * sigmoid_gate * (1.0 + gate_pre * (1.0 - sigmoid_gate))
    ).astype(jnp.bfloat16)
    up_pre_grad = (inner_grad * activated).astype(jnp.bfloat16)
    down_grad = jnp.einsum("erd,erf->edf", out_grad, inner, preferred_element_type=jnp.float32)
    gate_w_grad = jnp.einsum(
        "erd,erf->edf", arrived, gate_pre_grad, preferred_element_type=jnp.float32
    )
    up_w_grad = jnp.einsum("erd,erf->edf", arrived, up_pre_grad, preferred_element_type=jnp.float32)
    arrived_grad = jnp.einsum(
        "erf,edf->erd", gate_pre_grad, gate_back, preferred_element_type=jnp.float32
    )
    arrived_grad = (
        arrived_grad
        + jnp.einsum("erf,edf->erd", up_pre_grad, up_back, preferred_element_type=jnp.float32)
    ).astype(jnp.bfloat16)
    gate_up_grad, down_grad_shard = (
        lax.psum_scatter(
            jnp.concatenate([gate_w_grad, up_w_grad], axis=1).astype(jnp.bfloat16),
            "ctx",
            scatter_dimension=2,
            tiled=True,
        ).astype(jnp.float32),
        lax.psum_scatter(
            down_grad.astype(jnp.bfloat16), "ctx", scatter_dimension=2, tiled=True
        ).astype(jnp.float32),
    )
    back_rows = lax.all_to_all(arrived_grad, "exp", split_axis=1, concat_axis=0, tiled=True)
    padded_back = jnp.concatenate(
        [back_rows.reshape(slot_total, model_width), jnp.zeros((1, model_width), jnp.bfloat16)],
        axis=0,
    )
    second_grad = jnp.sum(
        padded_back[pair_slot].astype(jnp.float32).reshape(row_count, top_count, model_width),
        axis=1,
    )
    prob_grad = jnp.sum(chosen_mask * gate_grad[..., None], axis=1)
    logit_grad = (
        router_probs * (prob_grad - jnp.sum(prob_grad * router_probs, axis=-1, keepdims=True))
    ).astype(jnp.bfloat16)
    second_grad = second_grad + jnp.einsum(
        "te,de->td", logit_grad, router_full, preferred_element_type=jnp.float32
    )
    second_value, second_back = jax.vjp(rms_scale, hidden, gain_table[:, 3])
    hidden_part, gain_two_grad = second_back(second_grad)
    hidden_grad = grad_out + hidden_part
    hidden_grad_low = hidden_grad.astype(jnp.bfloat16)
    attended_grad = jnp.einsum(
        "tf,df->td", hidden_grad_low, output_full, preferred_element_type=jnp.float32
    ).astype(jnp.bfloat16)
    attended_heads = attended_grad.reshape(row_count, head_count, head_width)
    probs_again = jnp.exp(scores_of() - log_total)
    probs_grad = jnp.einsum(
        "qhd,khd->hqk", attended_heads, value_heads, preferred_element_type=jnp.float32
    )
    row_dot = jnp.sum(probs_again * probs_grad, axis=-1, keepdims=True)
    score_grad = (probs_again * (probs_grad - row_dot)).astype(jnp.bfloat16)
    query_grad = (
        jnp.einsum(
            "hqk,khd->qhd", score_grad, key_heads, preferred_element_type=jnp.float32
        ).reshape(row_count, model_width)
        * score_scale
    )
    key_part = (
        jnp.einsum(
            "hqk,qhd->khd", score_grad, query_heads, preferred_element_type=jnp.float32
        ).reshape(seq_length, model_width)
        * score_scale
    )
    value_part = jnp.einsum(
        "hqk,qhd->khd",
        probs_again.astype(jnp.bfloat16),
        attended_heads,
        preferred_element_type=jnp.float32,
    ).reshape(seq_length, model_width)
    key_grad, value_grad = (
        lax.psum_scatter(
            key_part.astype(jnp.bfloat16), "ctx", scatter_dimension=0, tiled=True
        ).astype(jnp.float32),
        lax.psum_scatter(
            value_part.astype(jnp.bfloat16), "ctx", scatter_dimension=0, tiled=True
        ).astype(jnp.float32),
    )
    query_value, query_back = jax.vjp(norm_rope, query_pre, gain_table[:, 1])
    query_pre_grad, gain_query_grad = query_back(query_grad)
    key_value, key_back = jax.vjp(norm_rope, key_pre, gain_table[:, 2])
    key_pre_grad, gain_key_grad = key_back(key_grad)
    query_low = query_pre_grad.astype(jnp.bfloat16)
    key_low = key_pre_grad.astype(jnp.bfloat16)
    value_low = value_grad.astype(jnp.bfloat16)
    first_grad = jnp.einsum("tf,df->td", query_low, query_full, preferred_element_type=jnp.float32)
    first_grad = first_grad + jnp.einsum(
        "tf,df->td", key_low, key_full, preferred_element_type=jnp.float32
    )
    first_grad = first_grad + jnp.einsum(
        "tf,df->td", value_low, value_full, preferred_element_type=jnp.float32
    )
    first_value, first_back = jax.vjp(rms_scale, tokens, gain_table[:, 0])
    token_part, gain_one_grad = first_back(first_grad)
    input_grad = (hidden_grad + token_part)[None]
    gain_grads = jnp.stack([gain_one_grad, gain_query_grad, gain_key_grad, gain_two_grad], axis=1)
    query_w_grad = jnp.einsum(
        "td,tf->df", first_norm, query_low, preferred_element_type=jnp.float32
    )
    key_w_grad = jnp.einsum("td,tf->df", first_norm, key_low, preferred_element_type=jnp.float32)
    value_w_grad = jnp.einsum(
        "td,tf->df", first_norm, value_low, preferred_element_type=jnp.float32
    )
    output_w_grad = jnp.einsum(
        "td,tf->df", attended, hidden_grad_low, preferred_element_type=jnp.float32
    )
    router_grad = jnp.einsum(
        "td,te->de", second_norm, logit_grad, preferred_element_type=jnp.float32
    )
    query_share, key_share, value_share, output_share, router_share, gain_share = (
        lax.psum_scatter(
            query_w_grad.astype(jnp.bfloat16), "exp", scatter_dimension=0, tiled=True
        ).astype(jnp.float32),
        lax.psum_scatter(
            key_w_grad.astype(jnp.bfloat16), "exp", scatter_dimension=0, tiled=True
        ).astype(jnp.float32),
        lax.psum_scatter(
            value_w_grad.astype(jnp.bfloat16), "exp", scatter_dimension=0, tiled=True
        ).astype(jnp.float32),
        lax.psum_scatter(
            output_w_grad.astype(jnp.bfloat16), "exp", scatter_dimension=0, tiled=True
        ).astype(jnp.float32),
        lax.psum_scatter(
            router_grad.astype(jnp.bfloat16), "exp", scatter_dimension=0, tiled=True
        ).astype(jnp.float32),
        lax.psum_scatter(
            gain_grads.astype(jnp.bfloat16), "exp", scatter_dimension=0, tiled=True
        ).astype(jnp.float32),
    )
    query_sum, key_sum, value_sum, output_sum, router_sum, gain_sum = (
        lax.psum(query_share.astype(jnp.bfloat16), "ctx").astype(jnp.float32),
        lax.psum(key_share.astype(jnp.bfloat16), "ctx").astype(jnp.float32),
        lax.psum(value_share.astype(jnp.bfloat16), "ctx").astype(jnp.float32),
        lax.psum(output_share.astype(jnp.bfloat16), "ctx").astype(jnp.float32),
        lax.psum(router_share.astype(jnp.bfloat16), "ctx").astype(jnp.float32),
        lax.psum(gain_share.astype(jnp.bfloat16), "ctx").astype(jnp.float32),
    )
    return (
        output,
        input_grad,
        query_sum,
        key_sum,
        value_sum,
        output_sum,
        router_sum,
        gain_sum,
        gate_up_grad,
        down_grad_shard,
    )


def solution(mesh):
    in_specs = (
        P("exp", "ctx", None),
        P("exp", None),
        P("exp", "ctx", None),
        P("exp", None),
        P("exp", None),
        P("exp", None),
        P("exp", None),
        P("exp", None),
        P("exp", None),
        P("exp", None, "ctx"),
        P("exp", None, "ctx"),
        P("exp", "ctx", None),
    )
    out_specs = (
        P("exp", "ctx", None),
        P("exp", "ctx", None),
        P("exp", None),
        P("exp", None),
        P("exp", None),
        P("exp", None),
        P("exp", None),
        P("exp", None),
        P("exp", None, "ctx"),
        P("exp", None, "ctx"),
    )
    return jax.shard_map(
        per_device, mesh=mesh, in_specs=in_specs, out_specs=out_specs, check_vma=False
    )
```

profile of v0, /device:TPU:1, one launch (start us, length us, event | category | flops | bytes accessed | tf_op | source)
XLA Modules:
  0.0 3465.5 jit_solution(3763846171016239692)
XLA Ops:
  37.3 99.8 %all-gather.13.cloned.1.call-done = bf16[2048,2048]{1,0:T(8,128)(2,1)} async-done(((bf16[256,2048]{1,0:T(8,128)(2,1)}), bf16[2048,2048]{1,0:T(8,128)(2,1)}) %all-gather.13.cloned.1.call-update) | async-done | bytes 8388624 | tf_op jit(solution)/shard_map/all_gather | solution.py:67
  146.7 115.6 %all-gather.15.cloned.1.call-done = bf16[2048,2048]{1,0:T(8,128)(2,1)} async-done(((bf16[256,2048]{1,0:T(8,128)(2,1)}), bf16[2048,2048]{1,0:T(8,128)(2,1)}) %all-gather.15.cloned.1.call-update) | async-done | bytes 8388624 | tf_op jit(solution)/shard_map/all_gather | solution.py:68
  297.0 90.6 %all-gather.9.cloned.1.call-done = bf16[2048,2048]{1,0:T(8,128)(2,1)} async-done(((bf16[256,2048]{1,0:T(8,128)(2,1)}), bf16[2048,2048]{1,0:T(8,128)(2,1)}) %all-gather.9.cloned.1.call-update) | async-done | bytes 8388624 | tf_op jit(solution)/shard_map/all_gather | solution.py:69
  503.7 105.9 %all-gather.19.cloned.1.call-done = bf16[2048,2048]{1,0:T(8,128)(2,1)} async-done(((bf16[256,2048]{1,0:T(8,128)(2,1)}), bf16[2048,2048]{1,0:T(8,128)(2,1)}) %all-gather.19.cloned.1.call-update) | async-done | bytes 8388624 | tf_op jit(solution)/shard_map/all_gather | solution.py:70
  708.4 297.8 %all-to-all-done.2 = bf16[16,240,2048]{2,1,0:T(8,128)(2,1)} async-done(((bf16[16,240,2048]{2,1,0:T(8,128)(2,1)}), bf16[16,240,2048]{2,1,0:T(8,128)(2,1)}, u32[]{:S(2)}, u32[]{:S(2)}) %all-to-all-start.2) | async-done | bytes 15728672 | tf_op jit(solution)/shard_map/all_to_all | solution.py:170
  1026.6 323.6 %all-to-all-done = bf16[16,240,2048]{2,1,0:T(8,128)(2,1)} async-done(((bf16[16,240,2048]{2,1,0:T(8,128)(2,1)}), bf16[16,240,2048]{2,1,0:T(8,128)(2,1)}, u32[]{:S(2)}, u32[]{:S(2)}) %all-to-all-start) | async-done | bytes 15728672 | tf_op jit(solution)/shard_map/all_to_all | solution.py:140
  1408.5 32.9 multiply_convert_fusion.1
  1464.9 29.1 copy.129
  1551.3 29.1 copy.133
  1580.4 257.3 %all-to-all-done.1 = bf16[2,1920,2048]{2,0,1:T(2,128)(2,1)} async-done(((bf16[2,1920,2048]{2,0,1:T(2,128)(2,1)}), bf16[2,1920,2048]{2,0,1:T(2,128)(2,1)}, u32[]{:S(2)}, u32[]{:S(2)}) %all-to-all-start.1) | async-done | bytes 15728672 | tf_op jit(solution)/shard_map/all_to_all | solution.py:154
  1864.1 31.5 gather_fusion
  1910.4 273.4 %all-to-all-done.3 = bf16[2,1920,2048]{2,0,1:T(2,128)(2,1)} async-done(((bf16[2,1920,2048]{2,0,1:T(2,128)(2,1)}), bf16[2,1920,2048]{2,0,1:T(2,128)(2,1)}, u32[]{:S(2)}, u32[]{:S(2)}) %all-to-all-start.3) | async-done | bytes 15728672 | tf_op jit(solution)/shard_map/all_to_all | solution.py:206
  2202.5 31.3 gather_fusion.1
  2284.9 31.7 multiply_reduce_fusion
  2316.6 32.0 multiply_convert_fusion
  2552.8 30.2 reduce-scatter.23.cloned.1.call-done
  2583.0 152.5 %reduce-scatter.17.cloned.1.call-done = bf16[256,2048]{1,0:T(8,128)(2,1)} async-done(((bf16[2048,2048]{1,0:T(8,128)(2,1)}), bf16[256,2048]{1,0:T(8,128)(2,1)}) %reduce-scatter.17.cloned.1.call-update) | async-done | bytes 1048592 | tf_op jit(solution)/shard_map/reduce_scatter | solution.py:294
  2735.5 151.7 %reduce-scatter.21.cloned.1.call-done = bf16[256,2048]{1,0:T(8,128)(2,1)} async-done(((bf16[2048,2048]{1,0:T(8,128)(2,1)}), bf16[256,2048]{1,0:T(8,128)(2,1)}) %reduce-scatter.21.cloned.1.call-update) | async-done | bytes 1048592 | tf_op jit(solution)/shard_map/reduce_scatter | solution.py:300
  2887.2 152.0 %reduce-scatter.19.cloned.1.call-done = bf16[256,2048]{1,0:T(8,128)(2,1)} async-done(((bf16[2048,2048]{1,0:T(8,128)(2,1)}), bf16[256,2048]{1,0:T(8,128)(2,1)}) %reduce-scatter.19.cloned.1.call-update) | async-done | bytes 1048592 | tf_op jit(solution)/shard_map/reduce_scatter | solution.py:297
  3039.2 73.1 %reduce-scatter.29.cloned.1.call-done = bf16[2,2048,256]{2,1,0:T(8,128)(2,1)} async-done(((bf16[2,2048,1024]{2,1,0:T(8,128)(2,1)}), bf16[2,2048,256]{2,1,0:T(8,128)(2,1)}) %reduce-scatter.29.cloned.1.call-update) | async-done | bytes 2097168 | tf_op jit(solution)/shard_map/reduce_scatter | solution.py:202
  3116.2 124.8 %reduce-scatter.27.cloned.1.call-done = bf16[2,4096,256]{2,1,0:T(8,128)(2,1)} async-done(((bf16[2,4096,1024]{2,1,0:T(8,128)(2,1)}), bf16[2,4096,256]{2,1,0:T(8,128)(2,1)}) %reduce-scatter.27.cloned.1.call-update) | async-done | bytes 4194320 | tf_op jit(solution)/shard_map/reduce_scatter | solution.py:196
  3250.0 54.9 %reduce-scatter.35.cloned.1.call-done = bf16[256,4]{1,0:T(8,128)(2,1)} async-done(((bf16[2048,4]{1,0:T(8,128)(2,1)}), bf16[256,4]{1,0:T(8,128)(2,1)}) %reduce-scatter.35.cloned.1.call-update) | async-done | bytes 2064
  3305.8 55.3 %reduce-scatter.25.cloned.1.call-done = bf16[256,16]{0,1:T(8,128)(2,1)} async-done(((bf16[2048,16]{0,1:T(8,128)(2,1)}), bf16[256,16]{0,1:T(8,128)(2,1)}) %reduce-scatter.25.cloned.1.call-update) | async-done | bytes 8208 | tf_op jit(solution)/shard_map/reduce_scatter | solution.py:306
  3374.9 76.2 %all-reduce.10.cloned.1.call-done = (bf16[256,2048]{1,0:T(8,128)(2,1)}, bf16[256,2048]{1,0:T(8,128)(2,1)}, bf16[256,2048]{1,0:T(8,128)(2,1)}, bf16[256,2048]{1,0:T(8,128)(2,1)}) async-done(((bf16[256,2048]{1,0:T(8,128)(2,1)}, bf16[256,2048]{1,0:T(8,128)(2,1)}, bf16[256,2048]{1,0:T(8,128)(2,1)}, bf16[256,2048]{1,0:T(8,128)(2,1)}), (bf16[256,2048]{1,0:T(8,128)(2,1)}, bf16[256,2048]{1,0:T(8,128)(2,1)}, ...) | async-done | bytes 4194320 | tf_op jit(solution)/shard_map/psum | solution.py:314
  (383 shorter events, 797.7 us)
Async XLA Ops:
  7.2 129.8 %all-gather.13.cloned.1.call-start = ((), (), s32[]{:S(2)}) async-start(), calls=%async_computation.16 | async-start | bytes 9437184 | tf_op jit(solution)/shard_map/all_gather | solution.py:67
  7.9 254.4 %all-gather.15.cloned.1.call-start = ((), (), s32[]{:S(2)}) async-start(), calls=%async_computation.17 | async-start | bytes 9437184 | tf_op jit(solution)/shard_map/all_gather | solution.py:68
  8.7 378.9 %all-gather.9.cloned.1.call-start = ((), (), s32[]{:S(2)}) async-start(), calls=%async_computation.14 | async-start | bytes 9437184 | tf_op jit(solution)/shard_map/all_gather | solution.py:69
  9.4 425.6 %all-gather.17.cloned.1.call-start = ((), (), s32[]{:S(2)}) async-start(), calls=%async_computation.18 | async-start | bytes 7864320 | tf_op jit(solution)/shard_map/all_gather | solution.py:98
  296.7 186.7 %all-gather.11.cloned.1.call-start = ((), (), s32[]{:S(2)}) async-start(), calls=%async_computation.15 | async-start | bytes 7864320 | tf_op jit(solution)/shard_map/all_gather | solution.py:99
  396.1 213.4 %all-gather.19.cloned.1.call-start = ((), (), s32[]{:S(2)}) async-start(), calls=%async_computation.19 | async-start | bytes 9437184 | tf_op jit(solution)/shard_map/all_gather | solution.py:70
  661.1 345.0 %all-to-all-start.2 = ((bf16[16,240,2048]{2,1,0:T(8,128)(2,1)}), bf16[16,240,2048]{2,1,0:T(8,128)(2,1)}, u32[]{:S(2)}, u32[]{:S(2)}) async-start(bf16[16,240,2048]{2,1,0:T(8,128)(2,1)} %bitcast.209), calls=%async_computation.2 | async-start | bytes 31457280 | tf_op jit(solution)/shard_map/all_to_all | solution.py:170
  666.8 697.0 %all-gather.21.cloned.1.call-start = ((), (), s32[]{:S(2)}) async-start(), calls=%async_computation.20 | async-start | bytes 20971520 | tf_op jit(solution)/shard_map/all_gather | solution.py:142
  1006.1 344.1 %all-to-all-start = ((bf16[16,240,2048]{2,1,0:T(8,128)(2,1)}), bf16[16,240,2048]{2,1,0:T(8,128)(2,1)}, u32[]{:S(2)}, u32[]{:S(2)}) async-start(bf16[16,240,2048]{2,1,0:T(8,128)(2,1)} %bitcast.208), calls=%async_computation | async-start | bytes 31457280 | tf_op jit(solution)/shard_map/all_to_all | solution.py:140
  1011.8 396.7 %all-gather.23.cloned.1.call-start = ((), (), s32[]{:S(2)}) async-start(), calls=%async_computation.21 | async-start | bytes 10485760 | tf_op jit(solution)/shard_map/all_gather | solution.py:143
  1494.0 343.8 %all-to-all-start.1 = ((bf16[2,1920,2048]{2,0,1:T(2,128)(2,1)}), bf16[2,1920,2048]{2,0,1:T(2,128)(2,1)}, u32[]{:S(2)}, u32[]{:S(2)}) async-start(bf16[2,1920,2048]{2,0,1:T(2,128)(2,1)} %copy.129), calls=%async_computation.1 | async-start | bytes 31457280 | tf_op jit(solution)/shard_map/all_to_all | solution.py:154
  1837.8 346.0 %all-to-all-start.3 = ((bf16[2,1920,2048]{2,0,1:T(2,128)(2,1)}), bf16[2,1920,2048]{2,0,1:T(2,128)(2,1)}, u32[]{:S(2)}, u32[]{:S(2)}) async-start(bf16[2,1920,2048]{2,0,1:T(2,128)(2,1)} %copy.133), calls=%async_computation.3 | async-start | bytes 31457280 | tf_op jit(solution)/shard_map/all_to_all | solution.py:206
  1845.0 570.5 %reduce-scatter.33.cloned.1.call-start = ((), (), s32[]{:S(2)}) async-start(), calls=%async_computation.30 | async-start | bytes 7864320
  1910.4 334.6 %copy-start.60 = (bf16[384,16]{0,1:T(8,128)(2,1)}, bf16[384,16]{0,1:T(8,128)(2,1)S(1)}, u32[]{:S(2)}) copy-start(bf16[384,16]{0,1:T(8,128)(2,1)S(1)} %multiply_convert_fusion.6) | copy-start | bytes 36868
  2284.8 145.5 %reduce-scatter.31.cloned.1.call-start = ((), (), s32[]{:S(2)}) async-start(), calls=%async_computation.29 | async-start | bytes 7864320
  2369.9 213.1 %reduce-scatter.23.cloned.1.call-start = ((), (), s32[]{:S(2)}) async-start(), calls=%async_computation.25 | async-start | bytes 9437184 | tf_op jit(solution)/shard_map/reduce_scatter | solution.py:303
  2379.9 355.6 %reduce-scatter.17.cloned.1.call-start = ((), (), s32[]{:S(2)}) async-start(), calls=%async_computation.22 | async-start | bytes 9437184 | tf_op jit(solution)/shard_map/reduce_scatter | solution.py:294
  2415.5 471.7 %reduce-scatter.21.cloned.1.call-start = ((), (), s32[]{:S(2)}) async-start(), calls=%async_computation.24 | async-start | bytes 9437184 | tf_op jit(solution)/shard_map/reduce_scatter | solution.py:300
  2425.2 613.9 %reduce-scatter.19.cloned.1.call-start = ((), (), s32[]{:S(2)}) async-start(), calls=%async_computation.23 | async-start | bytes 9437184 | tf_op jit(solution)/shard_map/reduce_scatter | solution.py:297
  2449.5 662.8 %reduce-scatter.29.cloned.1.call-start = ((), (), s32[]{:S(2)}) async-start(), calls=%async_computation.28 | async-start | bytes 10485760 | tf_op jit(solution)/shard_map/reduce_scatter | solution.py:202
  2473.6 767.4 %reduce-scatter.27.cloned.1.call-start = ((), (), s32[]{:S(2)}) async-start(), calls=%async_computation.27 | async-start | bytes 20971520 | tf_op jit(solution)/shard_map/reduce_scatter | solution.py:196
  2526.9 778.0 %reduce-scatter.35.cloned.1.call-start = ((), (), s32[]{:S(2)}) async-start(), calls=%async_computation.31 | async-start | bytes 589824
  2551.7 809.4 %reduce-scatter.25.cloned.1.call-start = ((), (), s32[]{:S(2)}) async-start(), calls=%async_computation.26 | async-start | bytes 73728 | tf_op jit(solution)/shard_map/reduce_scatter | solution.py:306
  2552.8 898.3 %all-reduce.10.cloned.1.call-start = ((), (), s32[]{:S(2)}) async-start(), calls=%async_computation.32 | async-start | bytes 8388608 | tf_op jit(solution)/shard_map/psum | solution.py:314
  (98 other events, 3239.3 us)
Sparse Core Ops, SparseCore 0:
  10.2 126.8 all-gather.12
  139.2 123.1 all-gather.14
  264.5 123.1 all-gather.8
  389.6 45.3 all-gather.16
  437.0 46.3 all-gather.10
  485.4 124.0 all-gather.18
  669.2 110.2 all-gather.20
  1014.2 62.4 all-gather.22
  2284.9 60.2 reduce-scatter.32
  2370.0 60.2 reduce-scatter.30
  2433.9 149.0 reduce-scatter.22
  2587.5 147.9 reduce-scatter.16
  2739.1 147.9 reduce-scatter.20
  2891.1 148.0 reduce-scatter.18
  3041.6 70.6 reduce-scatter.28
  3114.9 126.1 reduce-scatter.26
  3244.8 60.0 reduce-scatter.34
  3308.7 52.3 reduce-scatter.24
  3363.8 87.1 all-reduce.9
where the time goes:
time: 3480 us; the launch traced here: 3470 us
  waiting for transfers between devices  2450 us (70%)
  matrix products  427 us (12%)
  local copies, waits for them, and re-layouts  305 us (9%)
  other arithmetic  182 us (5%)
  blocking collectives  60.5 us (2%)
    all_to_all x1, waiting for transfers between devices, per_device(): lax.all_to_all(send_rows, 'exp', split_axis=0, concat_axis=1, tiled=True)  324 us
    all_to_all x1, waiting for transfers between devices, per_device(): lax.all_to_all(send_grad, 'exp', split_axis=0, concat_axis=1, tiled=True)  298 us
    all_to_all x1, waiting for transfers between devices, per_device(): lax.all_to_all(arrived_grad, 'exp', split_axis=1, concat_axis=0, tiled=True)  273 us
    all_to_all x1, waiting for transfers between devices, per_device(): lax.all_to_all(expert_out, 'exp', split_axis=1, concat_axis=0, tiled=True)  257 us
    reduce_scatter x1, waiting for transfers between devices, per_device(): lax.psum_scatter(query_w_grad.astype(jnp.bfloat16), 'exp', scatter_dimens...  153 us
    reduce_scatter x1, waiting for transfers between devices, per_device(): lax.psum_scatter(key_w_grad.astype(jnp.bfloat16), 'exp', scatter_dimensio...  152 us
    reduce_scatter x1, waiting for transfers between devices, per_device(): lax.psum_scatter(value_w_grad.astype(jnp.bfloat16), 'exp', scatter_dimens...  152 us
    reduce_scatter x1, waiting for transfers between devices, per_device(): lax.psum_scatter(jnp.concatenate([gate_w_grad, up_w_grad], axis=1).astype...  125 us
  transfers between devices with their start and end apart: 23, of which 20 were waited for; matrix products, arithmetic and copies ran while one was open for 19% of the time, Pallas kernels for 0%

commit v1 on v0

v1 whole, which is shorter than its diff:
```python
import functools

import jax
import jax.numpy as jnp
from jax import lax
from jax.experimental import pallas as pl
from jax.experimental.pallas import tpu as pltpu
from jax.sharding import PartitionSpec as P

HEAD_DIM = 128
CORES = 2
ROWS_Z = 4

epsilon = 1e-05
rope_theta = 10000.0
BF = jnp.bfloat16
F32 = jnp.float32


def dot(a, b, dims):
    return lax.dot_general(a, b, (dims, ((), ())), preferred_element_type=F32)


def ring_order(count):
    rows = ROWS_Z if count % ROWS_Z == 0 else 1
    across = count // rows
    walk = [(0, 0)]
    for z in range(rows):
        xs = range(1, across)
        walk += [(z, x) for x in (xs if z % 2 == 0 else reversed(xs))]
    walk += [(z, 0) for z in range(rows - 1, 0, -1)]
    return [z * across + x for z, x in walk]


class Ring:
    def __init__(self, axis, rings):
        self.axis = axis
        self.size = len(rings[0])
        self.right = [
            (r[i], r[(i + 1) % self.size]) for r in rings for i in range(self.size)
        ]
        self.left = [(b, a) for a, b in self.right]

    def go_right(self, v):
        return lax.ppermute(v, self.axis, self.right)

    def go_left(self, v):
        return lax.ppermute(v, self.axis, self.left)

    def gather(self, v):
        n = self.size
        got = [None] * n
        got[0] = v
        right = left = v
        for s in range(1, n // 2):
            right = self.go_right(right)
            left = self.go_left(left)
            got[s], got[n - s] = right, left
        half = v.shape[0] // 2
        got[n // 2] = jnp.concatenate(
            [self.go_right(right[:half]), self.go_left(left[half:])], axis=0
        )
        return got

    def scatter(self, part, dtype=BF):
        n = self.size
        far = part(n // 2).astype(dtype)
        half = far.shape[0] // 2
        from_left = self.go_right(far[:half]).astype(F32)
        from_right = self.go_left(far[half:]).astype(F32)
        from_left = jnp.concatenate([from_left, jnp.zeros_like(from_left)], axis=0)
        from_right = jnp.concatenate([jnp.zeros_like(from_right), from_right], axis=0)
        for s in range(n // 2 - 1, 0, -1):
            to_right = (part(s) + from_left).astype(dtype)
            to_left = (part(n - s) + from_right).astype(dtype)
            from_left = self.go_right(to_right).astype(F32)
            from_right = self.go_left(to_left).astype(F32)
        return part(0) + from_left + from_right


def _sorted_copy(dst, src, place, half, blocks):
    for b in range(blocks):
        at = pl.multiple_of(place[b] * half, half)
        dst[b * half : (b + 1) * half, :] = src[pl.ds(at, half), :]


def _scores(q, k, row0, width, scale):
    raw = dot(q, k, (((1,), (1,)))) * scale
    rows = lax.broadcasted_iota(jnp.int32, raw.shape, 0) + row0
    cols = lax.broadcasted_iota(jnp.int32, raw.shape, 1)
    return jnp.where(cols <= rows, raw, -1e30)


def _attend_kernel(place, q_ref, k_ref, v_ref, o_ref, lse_ref, q_s, k_s, v_s, o_s, *, half, blocks, tile, scale):
    for dst, src in ((q_s, q_ref), (k_s, k_ref), (v_s, v_ref)):
        _sorted_copy(dst, src, place, half, blocks)
    for i in range(half * blocks // tile):
        width = (i + 1) * tile
        s = _scores(q_s[i * tile : width, :], k_s[:width, :], i * tile, width, scale)
        top = jnp.max(s, axis=-1, keepdims=True)
        total = top + jnp.log(jnp.sum(jnp.exp(s - top), axis=-1, keepdims=True))
        p = jnp.exp(s - total).astype(BF)
        o_s[i * tile : width, :] = dot(p, v_s[:width, :], ((1,), (0,))).astype(BF)
        lse_ref[0, i * tile : width, :] = total
    for b in range(blocks):
        at = pl.multiple_of(place[b] * half, half)
        o_ref[pl.ds(at, half), :] = o_s[b * half : (b + 1) * half, :]


def _attend_back_kernel(place, q_ref, k_ref, v_ref, d_ref, lse_ref, dq_ref, dk_ref, dv_ref,
                        q_s, k_s, v_s, d_s, dq_s, dk_s, dv_s, *, half, blocks, tile, scale):
    for dst, src in ((q_s, q_ref), (k_s, k_ref), (v_s, v_ref), (d_s, d_ref)):
        _sorted_copy(dst, src, place, half, blocks)
    count = half * blocks // tile
    for i in reversed(range(count)):
        width = (i + 1) * tile
        here = slice(i * tile, width)
        q, d, k, v = q_s[here, :], d_s[here, :], k_s[:width, :], v_s[:width, :]
        p = jnp.exp(_scores(q, k, i * tile, width, scale) - lse_ref[0, here, :])
        dp = dot(d, v, ((1,), (1,)))
        row = jnp.sum(p * dp, axis=-1, keepdims=True)
        ds = (p * (dp - row)).astype(BF)
        dq_s[here, :] = dot(ds, k, ((1,), (0,))) * scale
        dk = dot(ds, q, ((0,), (0,))) * scale
        dv = dot(p.astype(BF), d, ((0,), (0,)))
        if i == count - 1:
            dk_s[:width, :] = dk
            dv_s[:width, :] = dv
        else:
            dk_s[:width, :] += dk
            dv_s[:width, :] += dv
    for b in range(blocks):
        at = pl.multiple_of(place[b] * half, half)
        for dst, src in ((dq_ref, dq_s), (dk_ref, dk_s), (dv_ref, dv_s)):
            dst[pl.ds(at, half), :] = src[b * half : (b + 1) * half, :].astype(dst.dtype)


def _head_specs(rows):
    head = pl.BlockSpec((rows, HEAD_DIM), lambda h, place: (0, h))
    lse = pl.BlockSpec((1, rows, 1), lambda h, place: (h, 0, 0))
    return head, lse


def attend(place, q, k, v, half):
    rows, width = q.shape
    heads = width // HEAD_DIM
    head, lse = _head_specs(rows)
    body = functools.partial(_attend_kernel, half=half, blocks=rows // half, tile=min(384, rows), scale=HEAD_DIM**-0.5)
    return pl.pallas_call(
        body,
        grid_spec=pltpu.PrefetchScalarGridSpec(
            num_scalar_prefetch=1,
            grid=(heads,),
            in_specs=[head] * 3,
            out_specs=[head, lse],
            scratch_shapes=[pltpu.VMEM((rows, HEAD_DIM), BF)] * 4,
        ),
        out_shape=[
            jax.ShapeDtypeStruct((rows, width), BF),
            jax.ShapeDtypeStruct((heads, rows, 1), F32),
        ],
        compiler_params=pltpu.CompilerParams(vmem_limit_bytes=48 << 20),
        cost_estimate=pl.CostEstimate(flops=2 * rows * rows * width * 2, bytes_accessed=8 * rows * width, transcendentals=heads * rows * rows),
    )(place, q, k, v)


def attend_back(place, q, k, v, d, lse_in, half):
    rows, width = q.shape
    heads = width // HEAD_DIM
    head, lse = _head_specs(rows)
    body = functools.partial(_attend_back_kernel, half=half, blocks=rows // half, tile=min(384, rows), scale=HEAD_DIM**-0.5)
    return pl.pallas_call(
        body,
        grid_spec=pltpu.PrefetchScalarGridSpec(
            num_scalar_prefetch=1,
            grid=(heads,),
            in_specs=[head] * 4 + [lse],
            out_specs=[head] * 3,
            scratch_shapes=[pltpu.VMEM((rows, HEAD_DIM), BF)] * 4
            + [pltpu.VMEM((rows, HEAD_DIM), F32)] * 3,
        ),
        out_shape=[
            jax.ShapeDtypeStruct((rows, width), F32),
            jax.ShapeDtypeStruct((rows, width), F32),
            jax.ShapeDtypeStruct((rows, width), BF),
        ],
        compiler_params=pltpu.CompilerParams(vmem_limit_bytes=48 << 20),
        cost_estimate=pl.CostEstimate(flops=5 * rows * rows * width * 2, bytes_accessed=18 * rows * width, transcendentals=heads * rows * rows),
    )(place, q, k, v, d, lse_in)


def inv_rms(matrix):
    return lax.rsqrt(jnp.mean(matrix * matrix, axis=-1, keepdims=True) + epsilon)


def norm_back(value, gain, grad):
    r = inv_rms(value)
    weighted = gain * grad
    inside = jnp.mean(value * weighted, axis=-1, keepdims=True)
    return r * weighted - value * (r * r * r * inside), jnp.sum(grad * value * r, axis=0)


def angle_tables(positions):
    half_width = HEAD_DIM // 2
    inverse = rope_theta ** (-(jnp.arange(half_width, dtype=F32) * 2.0) / HEAD_DIM)
    angles = positions.astype(F32)[:, None] * inverse[None, :]
    angles = jnp.concatenate([angles, angles], axis=-1)
    return jnp.cos(angles), jnp.sin(angles)


def rope(matrix, cosine, sine, back=False):
    rows, width = matrix.shape
    split = matrix.reshape(rows, width // HEAD_DIM, HEAD_DIM)
    first, second = split[..., : HEAD_DIM // 2], split[..., HEAD_DIM // 2 :]
    turned = [second, -first] if back else [-second, first]
    turned = jnp.concatenate(turned, axis=-1)
    result = split * cosine[:, None, :] + turned * sine[:, None, :]
    return result.reshape(rows, width)


def per_device(
    exp_walk,
    layer_input,
    block_ids,
    routes,
    w_query,
    w_key,
    w_value,
    w_output,
    w_router,
    norm_gains,
    w_gate_up,
    w_down,
    d_out,
):
    C, E = lax.axis_size("ctx"), lax.axis_size("exp")
    c, e = lax.axis_index("ctx"), lax.axis_index("exp")
    Y = C // CORES
    ring = Ring("exp", [exp_walk])
    ctx_ring = Ring("ctx", [[y * CORES + k for y in range(Y)] for k in range(CORES)])
    sibling = [(i, i ^ 1) for i in range(C)]

    def swap(v):
        return lax.ppermute(v, "ctx", sibling)

    def ctx_gather(v):
        got = []
        for block in ctx_ring.gather(v):
            got += [block, swap(block)]
        return got

    def ctx_scatter(part):
        mine = []
        for dy in range(Y):
            sent = swap(part(dy * CORES + 1).astype(BF))
            mine.append(part(dy * CORES) + sent.astype(F32))
        return ctx_ring.scatter(lambda s: mine[(Y - s) % Y])

    def ctx_of(r):
        return lax.rem(c // CORES + Y - r // CORES, Y) * CORES + jnp.bitwise_xor(lax.rem(c, CORES), r % CORES)

    def entry_of(i):
        return lax.rem(c // CORES + Y - i // CORES, Y) * CORES + jnp.bitwise_xor(lax.rem(c, CORES), i % CORES)

    def ctx_sum(rows):
        blocks = rows.reshape(rows.shape[0], C, -1)
        whole = lax.psum(jnp.stack([lax.dynamic_index_in_dim(blocks, entry_of(i), 1, False) for i in range(C)]), "ctx")
        return jnp.concatenate([lax.dynamic_index_in_dim(whole, ctx_of(r), 0, False) for r in range(C)], axis=1)

    walk = jnp.array(exp_walk, jnp.int32)
    place_in_walk = [0] * E
    for i, d in enumerate(exp_walk):
        place_in_walk[d] = i
    my_place = jnp.array(place_in_walk, jnp.int32)[e]
    left_of = [walk[lax.rem(my_place + E - s, E)] for s in range(E)]

    T, D = layer_input.shape[1:]
    rows_e = w_query.shape[0]
    cols_c = D // C
    S = T * C
    half = T // 2
    NE = w_router.shape[1]
    K = routes.shape[2]
    J = w_gate_up.shape[0]
    cap = (5 * T * K + 4 * NE - 1) // (4 * NE)
    x = layer_input[0]
    grad_out = d_out[0]

    x_all = jnp.concatenate(ctx_gather(x), axis=0)

    small = jnp.concatenate(
        [w_router.reshape(-1), norm_gains.reshape(-1), routes.astype(BF).reshape(-1)]
    )
    small_len = small.shape[0]
    small = jnp.pad(small, (0, -small_len % 256)).reshape(-1, 128)
    smalls = [v.reshape(-1) for v in ring.gather(small)]
    cut = rows_e * NE, rows_e * NE + rows_e * norm_gains.shape[1]
    router_full = jnp.zeros((E, rows_e, NE), BF)
    gains_full = jnp.zeros((E, rows_e, norm_gains.shape[1]), BF)
    for s in range(E):
        router_full = lax.dynamic_update_slice(
            router_full, smalls[s][: cut[0]].reshape(1, rows_e, NE), (left_of[s], 0, 0)
        )
        gains_full = lax.dynamic_update_slice(
            gains_full,
            smalls[s][cut[0] : cut[1]].reshape(1, rows_e, -1),
            (left_of[s], 0, 0),
        )
    router_full = router_full.reshape(D, NE)
    gains = gains_full.reshape(D, -1).astype(F32).T
    routes_all = jnp.stack([v[cut[1] : small_len] for v in smalls]).astype(jnp.int32)
    routes_all = routes_all.reshape(E, T, K)

    def my_columns(w):
        return lax.dynamic_slice_in_dim(w, c * cols_c, cols_c, axis=1)

    def assemble(blocks):
        full = jnp.zeros((E * rows_e, blocks[0].shape[1]), BF)
        for s in range(E):
            full = lax.dynamic_update_slice_in_dim(full, blocks[s], left_of[s] * rows_e, axis=0)
        return full

    w_qkv = assemble(ring.gather(jnp.concatenate([my_columns(w) for w in (w_query, w_key, w_value)], axis=1)))
    w_out_cols = assemble(ring.gather(my_columns(w_output)))
    w_out_rows = lax.all_to_all(
        w_out_cols.reshape(C, cols_c, cols_c), "ctx", split_axis=0, concat_axis=0, tiled=True
    )
    w_out_rows = jnp.transpose(w_out_rows, (1, 0, 2)).reshape(cols_c, D)
    w_gu = jnp.concatenate(ctx_gather(w_gate_up), axis=2)
    w_dn = jnp.concatenate(ctx_gather(w_down), axis=2)
    H = w_dn.shape[2]
    shard = H // C
    d_all = ring.gather(grad_out)

    blocks_rel = jnp.stack([lax.dynamic_slice_in_dim(block_ids[0], ctx_of(r) * 2, 2) for r in range(C)]).reshape(-1)
    positions = (blocks_rel[:, None] * half + jnp.arange(half, dtype=jnp.int32)[None, :]).reshape(-1)
    place = jnp.argsort(blocks_rel).astype(jnp.int32)
    cosine, sine = angle_tables(positions)
    gain_q = lax.dynamic_slice_in_dim(gains[1], c * cols_c, cols_c)
    gain_k = lax.dynamic_slice_in_dim(gains[2], c * cols_c, cols_c)

    x_all32 = x_all.astype(F32)
    n1 = (x_all32 * inv_rms(x_all32) * gains[0]).astype(BF)
    qkv = dot(n1, w_qkv, ((1,), (0,)))
    qp, kp = qkv[:, :cols_c], qkv[:, cols_c : 2 * cols_c]
    v = qkv[:, 2 * cols_c :].astype(BF)
    squares = ctx_sum(jnp.stack([jnp.sum(qp * qp, axis=1), jnp.sum(kp * kp, axis=1)]))
    scales = lax.rsqrt(squares / D + epsilon)
    r_q, r_k = scales[0][:, None], scales[1][:, None]
    q = rope(qp * r_q * gain_q, cosine, sine).astype(BF)
    k = rope(kp * r_k * gain_k, cosine, sine).astype(BF)
    attn, lse = attend(place, q, k, v, half)
    branch = dot(attn, w_out_rows, ((1,), (0,)))
    hidden = x.astype(F32) + ctx_scatter(lambda r: branch[r * T : (r + 1) * T])
    n2 = (hidden * inv_rms(hidden) * gains[3]).astype(BF)

    mine = e * J + jnp.arange(J, dtype=jnp.int32)
    chosen = jnp.any(routes_all[:, None] == mine[None, :, None, None], axis=-1)
    before = (jnp.arange(T)[:, None] < jnp.arange(T)[None, :]).astype(BF)
    rank = dot(chosen.astype(BF).reshape(E * J, T), before, ((1,), (0,))).reshape(E, J, T).astype(jnp.int32)
    slot = jnp.where(chosen & (rank < cap), rank, -1)
    pick = (slot[:, :, None, :] == jnp.arange(cap, dtype=jnp.int32)[None, None, :, None]).astype(BF)

    def take(rows):
        return jnp.stack(
            [jnp.einsum("jrt,td->jrd", pick[s], rows[s], preferred_element_type=F32).astype(BF) for s in range(E)], axis=1
        ).reshape(J, E * cap, D)

    xd = take(d_all)
    dw = jnp.einsum("jrd,jdf->jrf", xd, w_dn, preferred_element_type=F32)

    n2_all = ring.gather(n2)
    logits = [dot(n2_all[s], router_full, ((1,), (0,))) for s in range(E)]
    router = [jax.nn.softmax(v, axis=-1) for v in logits]
    is_mine = (jnp.arange(NE, dtype=jnp.int32)[None, :] == mine[:, None]).astype(F32)
    gate = jnp.stack([jnp.sum(router[s][None] * is_mine[:, None, :], axis=-1) for s in range(E)])
    gate_slot = jnp.sum(pick.astype(F32) * gate[:, :, None, :], axis=-1)
    gate_slot = jnp.transpose(gate_slot, (1, 0, 2)).reshape(J, E * cap, 1)
    xin = take(n2_all)
    g = jnp.einsum("jrd,jdf->jrf", xin, w_gu[:, :D], preferred_element_type=F32)
    u = jnp.einsum("jrd,jdf->jrf", xin, w_gu[:, D:], preferred_element_type=F32)
    sig = jax.nn.sigmoid(g)
    act = g * sig
    inner32 = act * u
    inner = inner32.astype(BF)
    dgate_slot = jnp.sum(inner32 * dw, axis=-1).reshape(J, E, cap)
    dinner = gate_slot * dw
    dg = (dinner * u * sig * (1.0 + g * (1.0 - sig))).astype(BF)
    du = (dinner * act).astype(BF)
    inner_gated = (gate_slot * inner32).astype(BF)

    dxin = jnp.einsum("jrf,jdf->jrd", dg, w_gu[:, :D], preferred_element_type=F32)
    dxin = (dxin + jnp.einsum("jrf,jdf->jrd", du, w_gu[:, D:], preferred_element_type=F32)).astype(BF)

    def put(rows):
        rows = rows.reshape(J, E, cap, D)

        def part(s):
            left = (E - s) % E
            return jnp.einsum("jrt,jrd->td", pick[left], rows[:, left], preferred_element_type=F32)

        return part

    dgate = jnp.einsum("sjrt,jsr->sjt", pick.astype(F32), dgate_slot, precision=lax.Precision.HIGHEST)
    dgate_cols = jnp.einsum("sjt,jn->snt", dgate, is_mine, precision=lax.Precision.HIGHEST)
    drouter = ring.scatter(lambda s: dgate_cols[(E - s) % E], F32).T
    router_own = router[0]
    dlogits = (router_own * (drouter - jnp.sum(drouter * router_own, axis=-1, keepdims=True))).astype(BF)
    dn2 = ring.scatter(put(dxin)) + dot(dlogits, router_full, ((1,), (1,)))
    hidden_part, d_gain3 = norm_back(hidden, gains[3], dn2)
    dhidden = grad_out.astype(F32) + hidden_part
    dhidden_all = jnp.concatenate(ctx_gather(dhidden.astype(BF)), axis=0)

    y = jnp.einsum("jrf,jdf->jrd", inner_gated, w_dn, preferred_element_type=F32).astype(BF)
    output = (hidden + ring.scatter(put(y))).astype(BF)[None]

    def weight_grad(rows, cols):
        def part(r):
            return jnp.einsum("jrd,jrf->jdf", rows, cols[..., r * shard : (r + 1) * shard], preferred_element_type=F32)

        return part

    part_g, part_u = weight_grad(xin, dg), weight_grad(xin, du)
    g_gate_up = jnp.concatenate(
        [ctx_scatter(part_g), ctx_scatter(part_u)], axis=1
    )
    g_down = ctx_scatter(weight_grad(xd, inner_gated))

    dattn = dot(dhidden_all, w_out_rows, ((1,), (1,))).astype(BF)
    g_out = dot(attn, dhidden_all, ((0,), (0,))).astype(BF)
    g_out = jnp.transpose(g_out.reshape(cols_c, C, cols_c), (1, 0, 2))
    g_out = lax.all_to_all(g_out, "ctx", split_axis=0, concat_axis=0, tiled=True).reshape(D, cols_c)
    dq, dk, dv = attend_back(place, q, k, v, dattn, lse, half)
    tq, tk = rope(dq, cosine, sine, True), rope(dk, cosine, sine, True)
    wq, wk = tq * gain_q, tk * gain_k
    inside = ctx_sum(jnp.stack([jnp.sum(qp * wq, axis=1), jnp.sum(kp * wk, axis=1)])) / D
    dqp = r_q * wq - qp * (r_q * r_q * r_q * inside[0][:, None])
    dkp = r_k * wk - kp * (r_k * r_k * r_k * inside[1][:, None])
    d_gain1 = jnp.sum(tq * qp * r_q, axis=0)
    d_gain2 = jnp.sum(tk * kp * r_k, axis=0)
    dqkv = jnp.concatenate([dqp.astype(BF), dkp.astype(BF), dv], axis=1)
    dn1_part = dot(dqkv, w_qkv, ((1,), (1,)))
    dn1 = ctx_scatter(lambda r: dn1_part[r * T : (r + 1) * T])
    x32 = x.astype(F32)
    token_part, d_gain0 = norm_back(x32, gains[0], dn1)
    d_x = (dhidden + token_part)[None]

    g_qkv = dot(n1, dqkv, ((0,), (0,))).astype(BF)
    right_of = [walk[lax.rem(my_place + s, E)] for s in range(E)]

    def row_sum(full):
        return ring.scatter(lambda s: lax.dynamic_slice_in_dim(full, right_of[s] * rows_e, rows_e, axis=0).astype(F32))

    g_out_mine = row_sum(g_out)
    g_qkv_mine = row_sum(g_qkv)

    def all_columns(block):
        full = jnp.zeros((rows_e, D), F32)
        for r, piece in enumerate(ctx_gather(block.astype(BF))):
            full = lax.dynamic_update_slice_in_dim(full, piece.astype(F32), ctx_of(r) * cols_c, axis=1)
        return full

    g_query, g_key, g_value = (all_columns(g_qkv_mine[:, i * cols_c : (i + 1) * cols_c]) for i in range(3))
    g_output = all_columns(g_out_mine)

    g_router = dot(n2, dlogits, ((0,), (0,)))
    spread = jnp.zeros((2, D), F32)
    spread = lax.dynamic_update_slice(spread, jnp.stack([d_gain1, d_gain2]), (0, c * cols_c))
    g_small = jnp.concatenate([g_router.T, d_gain0[None], spread, d_gain3[None]], axis=0)
    g_small = lax.psum(g_small, ("ctx", "exp"))
    g_small = lax.dynamic_slice_in_dim(g_small, e * rows_e, rows_e, axis=1).T
    return (
        output,
        d_x,
        g_query,
        g_key,
        g_value,
        g_output,
        g_small[:, :NE],
        g_small[:, NE:],
        g_gate_up,
        g_down,
    )


def solution(mesh):
    exp_walk = ring_order(mesh.shape["exp"])
    tokens = P("exp", "ctx", None)
    rows = P("exp", None)
    hidden_units = P("exp", None, "ctx")
    in_specs = (tokens, rows, tokens) + (rows,) * 6 + (hidden_units, hidden_units, tokens)
    out_specs = (tokens, tokens) + (rows,) * 6 + (hidden_units, hidden_units)
    return jax.shard_map(
        functools.partial(per_device, exp_walk),
        mesh=mesh,
        in_specs=in_specs,
        out_specs=out_specs,
        check_vma=False,
    )
```

time: 3480 us -> 1720 us (0.49)
  waiting for transfers between devices: 2450 us -> 612 us
  local copies, waits for them, and re-layouts: 305 us -> 159 us
  starting transfers between devices: 25.3 us -> 155 us
  matrix products: 427 us -> 474 us
  Pallas kernels: 0 us -> 45.1 us
    all_to_all x4 -> x2, waiting for transfers between devices: 1150 us -> 1.72 us  [the longest x1 1.71 us: per_device(): lax.all_to_all(g_out, 'ctx', split_axis=0, concat_axis=0, tiled=True)]
    reduce_scatter x7 -> x0, waiting for transfers between devices: 740 us -> none  [the longest x1 153 us: per_device(): lax.psum_scatter(query_w_grad.astype(jnp.bfloat16), 'exp', scatter_dimens...]
    ppermute x0 -> x132, waiting for transfers between devices: none -> 507 us  [the longest x53 287 us: go_right(): return lax.ppermute(v, self.axis, self.right)]
    all_gather x8 -> x0, waiting for transfers between devices: 419 us -> none  [the longest x1 116 us: per_device(): lax.all_gather(w_key, 'exp', axis=0, tiled=True)]
    ppermute x0 -> x132, starting transfers between devices: none -> 147 us  [the longest x53 61.5 us: go_right(): return lax.ppermute(v, self.axis, self.right)]
    unnamed x22 -> x1, waiting for transfers between devices: 64.1 us -> 0.02 us
    gather x2 -> x0, local copies, waits for them, and re-layouts: 62.8 us -> none  [the longest x1 31.5 us: per_device(): padded_out[pair_slot].astype(jnp.float32)]
    convert_element_type x2, local copies, waits for them, and re-layouts: 58.3 us -> 0.23 us  [the longest x1 0.16 us: per_device(): routes.astype(BF).reshape(-1)]
  transfers between devices with their start and end apart: 23 -> 135, of which waited for: 20 -> 54; matrix products, arithmetic and copies ran while one was open for 19% -> 32% of each run, Pallas kernels for 0% -> 3%
where the time goes in v1:
time: 1720 us; the launch traced here: 1710 us
  waiting for transfers between devices  612 us (36%)
  matrix products  474 us (28%)
  other arithmetic  181 us (11%)
  local copies, waits for them, and re-layouts  159 us (9%)
  starting transfers between devices  155 us (9%)
  between operations  45.3 us (3%)
  Pallas kernels  45.1 us (3%)
  blocking collectives  35.4 us (2%)
    ppermute x53, waiting for transfers between devices, go_right(): return lax.ppermute(v, self.axis, self.right)  287 us
    ppermute x53, waiting for transfers between devices, go_left(): return lax.ppermute(v, self.axis, self.left)  219 us
    dot_general x12, matrix products, part(): jnp.einsum('jrd,jrf->jdf', rows, cols[..., r * shard:(r + 1) * shard], pr...  139 us
    psum x1, waiting for transfers between devices, per_device(): g_small = lax.psum(g_small, ('ctx', 'exp'))  104 us
    dot_general x17, matrix products, dot(): return lax.dot_general(a, b, (dims, ((), ())), preferred_element_type=F32)  74.6 us
    ppermute x53, starting transfers between devices, go_right(): return lax.ppermute(v, self.axis, self.right)  61.5 us
    dot_general x16, matrix products, part(): jnp.einsum('jrt,jrd->td', pick[left], rows[:, left], preferred_element_ty...  52.9 us
    ppermute x26, starting transfers between devices, swap(): return lax.ppermute(v, 'ctx', sibling)  52.1 us
  transfers between devices with their start and end apart: 135, of which 54 were waited for; matrix products, arithmetic and copies ran while one was open for 32% of the time, Pallas kernels for 3%

profile of v1, /device:TPU:1, one launch (start us, length us, event | category | flops | bytes accessed | tf_op | source)
XLA Modules:
  0.0 1707.5 jit_solution(12251210800616820659)
XLA Ops:
  157.4 33.8 %collective-permute-done.13 = bf16[256,1536]{1,0:T(8,128)(2,1)S(1)} collective-permute-done((bf16[256,1536]{1,0:T(8,128)(2,1)}, bf16[256,1536]{1,0:T(8,128)(2,1)S(1)}, u32[]{:S(2)}, u32[]{:S(2)}) %collective-permute-start.13) | collective-permute-done | bytes 786464 | tf_op jit(solution)/shard_map/ppermute | solution.py:45
  240.9 25.9 %psum.21 = f32[4,2,384]{2,0,1:T(4,128)S(1)} all-reduce(f32[4,2,384]{2,0,1:T(4,128)S(1)} %pad_maximum_fusion.13), channel_id=1, replica_groups=mesh['ctx'=4,'exp'=8] {'ctx'}, use_global_device_ids=true, to_apply=%region_4.5 | all-reduce | flops 3072 | bytes 24576 | tf_op jit(solution)/shard_map/psum | solution.py:267
  310.1 19.9 %shard_map.213 = (bf16[1536,512]{1,0:T(8,128)(2,1)S(1)}, f32[4,1536,1]{2,1,0:T(8,128)}) custom-call(s32[8]{0:T(128)S(1)} %get-tuple-element.16.place, bf16[1536,512]{1,0:T(8,128)(2,1)S(1)} %get-tuple-element.85.q_ref, bf16[1536,512]{1,0:T(8,128)(2,1)S(1)} %get-tuple-element.84.k_ref, bf16[1536,512]{1,0:T(8,128)(2,1)} %slice.1002.v_ref), custom_call_target="tpu_custom_call" | custom-call | flops 4831838208 | bytes 6291456 | tf_op jit(solution)/shard_map/pallas_call | solution.py:149
  341.5 57.5 %collective-permute-done.46 = bf16[1,2048,256]{2,1,0:T(8,128)(2,1)} collective-permute-done((bf16[1,2048,256]{2,1,0:T(8,128)(2,1)S(1)}, bf16[1,2048,256]{2,1,0:T(8,128)(2,1)}, u32[]{:S(2)}, u32[]{:S(2)}) %collective-permute-start.46) | collective-permute-done | bytes 1048608 | tf_op jit(solution)/shard_map/ppermute | solution.py:48
  419.2 29.1 %collective-permute-done.58 = bf16[384,2048]{1,0:T(8,128)(2,1)S(1)} collective-permute-done((bf16[384,2048]{1,0:T(8,128)(2,1)}, bf16[384,2048]{1,0:T(8,128)(2,1)S(1)}, u32[]{:S(2)}, u32[]{:S(2)}) %collective-permute-start.58) | collective-permute-done | bytes 1572896 | tf_op jit(solution)/shard_map/ppermute | solution.py:45
  466.9 16.1 collective-permute-done.30
  535.9 21.4 %collective-permute-done.33 = bf16[384,2048]{1,0:T(8,128)(2,1)} collective-permute-done((bf16[384,2048]{1,0:T(8,128)(2,1)}, bf16[384,2048]{1,0:T(8,128)(2,1)}, u32[]{:S(2)}, u32[]{:S(2)}) %collective-permute-start.33) | collective-permute-done | bytes 1572896 | tf_op jit(solution)/shard_map/ppermute | solution.py:45
  564.0 27.5 %collective-permute-done.34 = bf16[384,2048]{1,0:T(8,128)(2,1)S(1)} collective-permute-done((bf16[384,2048]{1,0:T(8,128)(2,1)}, bf16[384,2048]{1,0:T(8,128)(2,1)S(1)}, u32[]{:S(2)}, u32[]{:S(2)}) %collective-permute-start.34) | collective-permute-done | bytes 1572896 | tf_op jit(solution)/shard_map/ppermute | solution.py:45
  620.7 24.6 %fusion.6 = f32[2,1920,1024]{1,2,0:T(8,128)} fusion(bf16[2,1920,2048]{2,1,0:T(8,128)(2,1)} %bitcast.600, bf16[2,4096,1024]{1,2,0:T(8,128)(2,1)} %pad_maximum_fusion), kind=kOutput, calls=%fused_computation.19 | convolution fusion | flops 16106127360 | bytes 39845888 | tf_op jit(solution)/shard_map/jrd,jdf->jrf/dot_general | solution.py:381
  645.4 24.6 %fusion.9 = f32[2,1920,1024]{1,2,0:T(8,128)} fusion(bf16[2,1920,2048]{2,1,0:T(8,128)(2,1)} %bitcast.601, bf16[2,4096,1024]{1,2,0:T(8,128)(2,1)} %pad_maximum_fusion), kind=kOutput, calls=%fused_computation.22 | convolution fusion | flops 16106127360 | bytes 39845888 | tf_op jit(solution)/shard_map/jrd,jdf->jrf/dot_general | solution.py:380
  670.0 32.5 %multiply_reduce_fusion = (f32[2,1920]{1,0:T(2,128)S(1)}, f32[2,1920,1024]{1,2,0:T(8,128)}) fusion(f32[2,1920,1024]{1,2,0:T(8,128)} %fusion.6, f32[2,1920,1024]{1,2,0:T(8,128)} %fusion.9, bf16[2,1920,2048]{2,1,0:T(8,128)(2,1)} %bitcast.595, bf16[2,2048,256]{2,1,0:T(8,128)(2,1)} %collective-permute-done.47, ...), kind=kOutput, calls=%fused_computation.2 | convolution fusion | flops 16167202816 | bytes 71318528 | tf_op jit(solution)/shard_map/jrd,jdf->jrf/dot_general | solution.py:370
  723.4 22.2 %multiply_convert_fusion.1 = (bf16[2,1920,1024]{1,2,0:T(8,128)(2,1)}, bf16[2,1920,1024]{1,2,0:T(8,128)(2,1)S(1)}, bf16[2,1920,1024]{1,2,0:T(8,128)(2,1)}) fusion(f32[2,1920,1024]{1,2,0:T(8,128)} %fusion.9, f32[2,1920,1024]{1,2,0:T(8,128)} %fusion.6, f32[2,1920,1024]{1,2,0:T(8,128)} %get-tuple-element.176, f32[2,1920]{1,0:T(2,128)S(1)} %mul.794), kind=kLoop, calls=%fused_computation.4 | loop fusion | flops 66846720 | bytes 70794240 | tf_op jit(solution)/shard_map/convert_element_type | solution.py:388
  817.0 25.4 %fusion.4 = f32[2,1920,2048]{2,1,0:T(8,128)} fusion(bf16[2,1920,1024]{1,2,0:T(8,128)(2,1)} %copy-done.33, bf16[2,4096,1024]{1,2,0:T(8,128)(2,1)} %pad_maximum_fusion), kind=kOutput, calls=%fused_computation.17 | convolution fusion | flops 16106127360 | bytes 47710208 | tf_op jit(solution)/shard_map/jrf,jdf->jrd/dot_general | solution.py:393
  842.3 28.1 %add_convert_fusion = bf16[2,1920,2048]{2,1,0:T(8,128)(2,1)} fusion(f32[2,1920,2048]{2,1,0:T(8,128)} %fusion.4, bf16[2,1920,1024]{1,2,0:T(8,128)(2,1)} %get-tuple-element.61, bf16[2,4096,1024]{1,2,0:T(8,128)(2,1)} %pad_maximum_fusion), kind=kOutput, calls=%fused_computation | convolution fusion | flops 16121856000 | bytes 63438848 | tf_op jit(solution)/shard_map/jrf,jdf->jrd/dot_general | solution.py:392
  894.6 27.9 %convolution_convert_fusion = bf16[2,1920,2048]{2,1,0:T(8,128)(2,1)} fusion(bf16[2,1920,1024]{1,2,0:T(8,128)(2,1)} %get-tuple-element.63, bf16[2,2048,256]{2,1,0:T(8,128)(2,1)} %collective-permute-done.47, bf16[2,2048,256]{2,1,0:T(8,128)(2,1)} %constant_dynamic-update-slice_fusion.27, bf16[2,2048,256]{2,1,0:T(8,128)(2,1)} %collective-permute-done.44, ...), kind=kOutput, calls=%fused_computation.13 | convolution fusion | flops 16147546112 | bytes 31981568 | tf_op jit(solution)/shard_map/jrf,jdf->jrd/dot_general | solution.py:414
  1035.7 21.0 %collective-permute-done.49 = bf16[384,2048]{1,0:T(8,128)(2,1)} collective-permute-done((bf16[384,2048]{1,0:T(8,128)(2,1)}, bf16[384,2048]{1,0:T(8,128)(2,1)}, u32[]{:S(2)}, u32[]{:S(2)}) %collective-permute-start.49) | collective-permute-done | bytes 1572896 | tf_op jit(solution)/shard_map/ppermute | solution.py:45
  1060.6 29.7 %collective-permute-done.66 = bf16[384,2048]{1,0:T(8,128)(2,1)S(1)} collective-permute-done((bf16[384,2048]{1,0:T(8,128)(2,1)S(1)}, bf16[384,2048]{1,0:T(8,128)(2,1)S(1)}, u32[]{:S(2)}, u32[]{:S(2)}) %collective-permute-start.66) | collective-permute-done | bytes 1572896 | tf_op jit(solution)/shard_map/ppermute | solution.py:45
  1142.7 18.2 %collective-permute-done.123 = bf16[1,2048,256]{2,1,0:T(8,128)(2,1)S(1)} collective-permute-done((bf16[1,2048,256]{2,1,0:T(8,128)(2,1)}, bf16[1,2048,256]{2,1,0:T(8,128)(2,1)S(1)}, u32[]{:S(2)}, u32[]{:S(2)}) %collective-permute-start.123) | collective-permute-done | bytes 1048608 | tf_op jit(solution)/shard_map/ppermute | solution.py:48
  1173.4 49.4 %collective-permute-done.81 = bf16[192,2048]{1,0:T(8,128)(2,1)S(1)} collective-permute-done((bf16[192,2048]{1,0:T(8,128)(2,1)S(1)}, bf16[192,2048]{1,0:T(8,128)(2,1)S(1)}, u32[]{:S(2)}, u32[]{:S(2)}) %collective-permute-start.81) | collective-permute-done | bytes 786464 | tf_op jit(solution)/shard_map/ppermute | solution.py:45
  1224.0 15.7 collective-permute-done.82
  1276.8 25.2 %shard_map.214 = (f32[1536,512]{1,0:T(8,128)}, f32[1536,512]{1,0:T(8,128)}, bf16[1536,512]{1,0:T(8,128)(2,1)S(1)}) custom-call(s32[8]{0:T(128)S(1)} %get-tuple-element.16.place, bf16[1536,512]{1,0:T(8,128)(2,1)S(1)} %copy-done.7, bf16[1536,512]{1,0:T(8,128)(2,1)S(1)} %copy-done.5, bf16[1536,512]{1,0:T(8,128)(2,1)} %slice.1002.v_ref, ...), custom_call_target="tpu_custom_call" | custom-call | flops 12079595520 | bytes 14155776 | tf_op jit(solution)/shard_map/pallas_call | solution.py:172
  1355.4 16.4 fusion.243
  1486.3 27.9 %collective-permute-done.113 = bf16[256,512]{1,0:T(8,128)(2,1)S(1)} collective-permute-done((bf16[256,512]{1,0:T(8,128)(2,1)S(1)}, bf16[256,512]{1,0:T(8,128)(2,1)S(1)}, u32[]{:S(2)}, u32[]{:S(2)}) %collective-permute-start.113) | collective-permute-done | bytes 262176 | tf_op jit(solution)/shard_map/ppermute | solution.py:48
  1543.7 103.7 %all-reduce.22.cloned.1.call-done = f32[20,2048]{1,0:T(8,128)} async-done(((f32[20,2048]{1,0:T(8,128)}), f32[20,2048]{1,0:T(8,128)}) %all-reduce.22.cloned.1.call-update) | async-done | bytes 163856 | tf_op jit(solution)/shard_map/psum | solution.py:470
  (911 shorter events, 938.3 us)
Async XLA Ops:
  23.5 95.0 %collective-permute-start.11 = (bf16[256,1536]{1,0:T(8,128)(2,1)}, bf16[256,1536]{1,0:T(8,128)(2,1)}, u32[]{:S(2)}, u32[]{:S(2)}) collective-permute-start(bf16[256,1536]{1,0:T(8,128)(2,1)} %get-tuple-element.130), channel_id=1, source_target_pairs={{0,1},{1,3},{3,5},{5,7},{7,6},{6,4},{4,2},{2,0},{8,9},{9,11},{11,1... | collective-permute-start | bytes 2359304 | tf_op jit(solution)/shard_map/ppermute | solution.py:45
  25.5 94.4 %collective-permute-start.15 = (bf16[256,1536]{1,0:T(8,128)(2,1)}, bf16[256,1536]{1,0:T(8,128)(2,1)}, u32[]{:S(2)}, u32[]{:S(2)}) collective-permute-start(bf16[256,1536]{1,0:T(8,128)(2,1)} %get-tuple-element.130), channel_id=1, source_target_pairs={{1,0},{3,1},{5,3},{7,5},{6,7},{4,6},{2,4},{0,2},{9,8},{11,9},{13,1... | collective-permute-start | bytes 2359304 | tf_op jit(solution)/shard_map/ppermute | solution.py:48
  137.7 200.2 %collective-permute-start.56 = (bf16[384,2048]{1,0:T(8,128)(2,1)}, bf16[384,2048]{1,0:T(8,128)(2,1)}, u32[]{:S(2)}, u32[]{:S(2)}) collective-permute-start(bf16[384,2048]{1,0:T(8,128)(2,1)} %bitcast.80), channel_id=1, source_target_pairs={{0,1},{1,3},{3,5},{5,7},{7,6},{6,4},{4,2},{2,0},{8,9},{9,11},{11,1... | collective-permute-start | bytes 4718600 | tf_op jit(solution)/shard_map/ppermute | solution.py:45
  147.1 191.7 %collective-permute-start.60 = (bf16[384,2048]{1,0:T(8,128)(2,1)}, bf16[384,2048]{1,0:T(8,128)(2,1)}, u32[]{:S(2)}, u32[]{:S(2)}) collective-permute-start(bf16[384,2048]{1,0:T(8,128)(2,1)} %bitcast.80), channel_id=1, source_target_pairs={{1,0},{3,1},{5,3},{7,5},{6,7},{4,6},{2,4},{0,2},{9,8},{11,9},{13,1... | collective-permute-start | bytes 4718600 | tf_op jit(solution)/shard_map/ppermute | solution.py:48
  191.2 219.7 %collective-permute-start.41 = (bf16[1,4096,256]{1,2,0:T(8,128)(2,1)}, bf16[1,4096,256]{1,2,0:T(8,128)(2,1)}, u32[]{:S(2)}, u32[]{:S(2)}) collective-permute-start(bf16[1,4096,256]{1,2,0:T(8,128)(2,1)} %get-tuple-element.77), channel_id=1, source_target_pairs={{0,16},{16,0},{8,24},{24,8},{1,17},{17,1},{9,25},{25,9},{2,18},{18... | collective-permute-start | bytes 6291464 | tf_op jit(solution)/shard_map/ppermute | solution.py:45
  215.0 115.3 %collective-permute-start.45 = (bf16[1,2048,256]{2,1,0:T(8,128)(2,1)}, bf16[1,2048,256]{2,1,0:T(8,128)(2,1)}, u32[]{:S(2)}, u32[]{:S(2)}) collective-permute-start(bf16[1,2048,256]{2,1,0:T(8,128)(2,1)} %get-tuple-element.101), channel_id=1, source_target_pairs={{0,16},{16,0},{8,24},{24,8},{1,17},{17,1},{9,25},{25,9},{2,18},{18... | collective-permute-start | bytes 3145736 | tf_op jit(solution)/shard_map/ppermute | solution.py:45
  215.6 114.5 %collective-permute-start.31 = (bf16[32,128]{1,0:T(8,128)(2,1)S(1)}, bf16[32,128]{1,0:T(8,128)(2,1)S(1)}, u32[]{:S(2)}, u32[]{:S(2)}) collective-permute-start(bf16[32,128]{1,0:T(8,128)(2,1)S(1)} %slice.698), channel_id=1, source_target_pairs={{0,1},{1,3},{3,5},{5,7},{7,6},{6,4},{4,2},{2,0},{8,9},{9,11},{11,1... | collective-permute-start | bytes 24584 | tf_op jit(solution)/shard_map/ppermute | solution.py:45
  330.0 84.2 %collective-permute-start.42 = (bf16[1,4096,256]{1,2,0:T(8,128)(2,1)}, bf16[1,4096,256]{1,2,0:T(8,128)(2,1)}, u32[]{:S(2)}, u32[]{:S(2)}) collective-permute-start(bf16[1,4096,256]{1,2,0:T(8,128)(2,1)} %get-tuple-element.76), channel_id=1, source_target_pairs={{16,0},{0,16},{24,8},{8,24},{17,1},{1,17},{25,9},{9,25},{18,2},{2,... | collective-permute-start | bytes 6291464 | tf_op jit(solution)/shard_map/ppermute | solution.py:48
  410.9 111.0 %collective-permute-start.40 = (bf16[2,4096,256]{1,2,0:T(8,128)(2,1)}, bf16[2,4096,256]{1,2,0:T(8,128)(2,1)S(1)}, u32[]{:S(2)}, u32[]{:S(2)}) collective-permute-start(bf16[2,4096,256]{1,2,0:T(8,128)(2,1)} %copy.496), channel_id=1, source_target_pairs={{0,8},{8,0},{16,24},{24,16},{1,9},{9,1},{17,25},{25,17},{2,10},{10... | collective-permute-start | bytes 12582920 | tf_op jit(solution)/shard_map/ppermute | solution.py:244
  415.9 107.6 %collective-permute-start.43 = (bf16[2,4096,256]{1,2,0:T(8,128)(2,1)S(1)}, bf16[2,4096,256]{1,2,0:T(8,128)(2,1)S(1)}, u32[]{:S(2)}, u32[]{:S(2)}) collective-permute-start(bf16[2,4096,256]{1,2,0:T(8,128)(2,1)S(1)} %constant_dynamic-update-slice_fusion.25), channel_id=1, source_target_pairs={{0,8},{8,0},{16,24},{24,16},{1,9},{9,1},{17,25},{25,17},{2,10},{10... | collective-permute-start | bytes 12582920 | tf_op jit(solution)/shard_map/ppermute | solution.py:244
  491.0 178.9 %collective-permute-start.44 = (bf16[2,2048,256]{2,1,0:T(8,128)(2,1)}, bf16[2,2048,256]{2,1,0:T(8,128)(2,1)}, u32[]{:S(2)}, u32[]{:S(2)}) collective-permute-start(bf16[2,2048,256]{2,1,0:T(8,128)(2,1)} %param.24), channel_id=1, source_target_pairs={{0,8},{8,0},{16,24},{24,16},{1,9},{9,1},{17,25},{25,17},{2,10},{10... | collective-permute-start | bytes 6291464 | tf_op jit(solution)/shard_map/ppermute | solution.py:244
  521.9 148.0 %collective-permute-start.47 = (bf16[2,2048,256]{2,1,0:T(8,128)(2,1)}, bf16[2,2048,256]{2,1,0:T(8,128)(2,1)}, u32[]{:S(2)}, u32[]{:S(2)}) collective-permute-start(bf16[2,2048,256]{2,1,0:T(8,128)(2,1)} %constant_dynamic-update-slice_fusion.27), channel_id=1, source_target_pairs={{0,8},{8,0},{16,24},{24,16},{1,9},{9,1},{17,25},{25,17},{2,10},{10... | collective-permute-start | bytes 6291464 | tf_op jit(solution)/shard_map/ppermute | solution.py:244
  947.4 153.5 %collective-permute-start.128 = (bf16[2,2048,256]{2,1,0:T(8,128)(2,1)}, bf16[2,2048,256]{2,1,0:T(8,128)(2,1)}, u32[]{:S(2)}, u32[]{:S(2)}) collective-permute-start(bf16[2,2048,256]{2,1,0:T(8,128)(2,1)} %convolution_convert_fusion.5), channel_id=1, source_target_pairs={{0,8},{8,0},{16,24},{24,16},{1,9},{9,1},{17,25},{25,17},{2,10},{10... | collective-permute-start | bytes 6291464 | tf_op jit(solution)/shard_map/ppermute | solution.py:244
  1017.2 80.5 %collective-permute-start.53 = (bf16[384,2048]{1,0:T(8,128)(2,1)}, bf16[384,2048]{1,0:T(8,128)(2,1)}, u32[]{:S(2)}, u32[]{:S(2)}) collective-permute-start(bf16[384,2048]{1,0:T(8,128)(2,1)} %fusion.34), channel_id=1, source_target_pairs={{1,0},{3,1},{5,3},{7,5},{6,7},{4,6},{2,4},{0,2},{9,8},{11,9},{13,1... | collective-permute-start | bytes 4718600 | tf_op jit(solution)/shard_map/ppermute | solution.py:48
  1102.6 138.1 %collective-permute-start.124 = (bf16[2,2048,256]{2,1,0:T(8,128)(2,1)}, bf16[2,2048,256]{2,1,0:T(8,128)(2,1)}, u32[]{:S(2)}, u32[]{:S(2)}) collective-permute-start(bf16[2,2048,256]{2,1,0:T(8,128)(2,1)} %convolution_convert_fusion.7), channel_id=1, source_target_pairs={{0,8},{8,0},{16,24},{24,16},{1,9},{9,1},{17,25},{25,17},{2,10},{10... | collective-permute-start | bytes 6291464 | tf_op jit(solution)/shard_map/ppermute | solution.py:244
  1132.6 111.0 %collective-permute-start.126 = (bf16[1,2048,256]{2,1,0:T(8,128)(2,1)}, bf16[1,2048,256]{2,1,0:T(8,128)(2,1)}, u32[]{:S(2)}, u32[]{:S(2)}) collective-permute-start(bf16[1,2048,256]{2,1,0:T(8,128)(2,1)} %get-tuple-element.94), channel_id=1, source_target_pairs={{0,16},{16,0},{8,24},{24,8},{1,17},{17,1},{9,25},{25,9},{2,18},{18... | collective-permute-start | bytes 3145736 | tf_op jit(solution)/shard_map/ppermute | solution.py:45
  1141.3 102.4 %collective-permute-start.127 = (bf16[1,2048,256]{2,1,0:T(8,128)(2,1)S(1)}, bf16[1,2048,256]{2,1,0:T(8,128)(2,1)}, u32[]{:S(2)}, u32[]{:S(2)}) collective-permute-start(bf16[1,2048,256]{2,1,0:T(8,128)(2,1)S(1)} %copy-done.62), channel_id=1, source_target_pairs={{16,0},{0,16},{24,8},{8,24},{17,1},{1,17},{25,9},{9,25},{18,2},{2,... | collective-permute-start | bytes 3145736 | tf_op jit(solution)/shard_map/ppermute | solution.py:48
  1141.9 80.8 %collective-permute-start.81 = (bf16[192,2048]{1,0:T(8,128)(2,1)S(1)}, bf16[192,2048]{1,0:T(8,128)(2,1)S(1)}, u32[]{:S(2)}, u32[]{:S(2)}) collective-permute-start(bf16[192,2048]{1,0:T(8,128)(2,1)S(1)} %get-tuple-element.105), channel_id=1, source_target_pairs={{0,16},{16,0},{8,24},{24,8},{1,17},{17,1},{9,25},{25,9},{2,18},{18... | collective-permute-start | bytes 2359304 | tf_op jit(solution)/shard_map/ppermute | solution.py:45
  1222.7 184.0 %collective-permute-start.50 = (bf16[384,2048]{1,0:T(8,128)(2,1)}, bf16[384,2048]{1,0:T(8,128)(2,1)}, u32[]{:S(2)}, u32[]{:S(2)}) collective-permute-start(bf16[384,2048]{1,0:T(8,128)(2,1)} %fusion.38), channel_id=1, source_target_pairs={{0,1},{1,3},{3,5},{5,7},{7,6},{6,4},{4,2},{2,0},{8,9},{9,11},{11,1... | collective-permute-start | bytes 4718600 | tf_op jit(solution)/shard_map/ppermute | solution.py:45
  1239.7 171.1 %collective-permute-start.54 = (bf16[384,2048]{1,0:T(8,128)(2,1)}, bf16[384,2048]{1,0:T(8,128)(2,1)}, u32[]{:S(2)}, u32[]{:S(2)}) collective-permute-start(bf16[384,2048]{1,0:T(8,128)(2,1)} %fusion.35), channel_id=1, source_target_pairs={{1,0},{3,1},{5,3},{7,5},{6,7},{4,6},{2,4},{0,2},{9,8},{11,9},{13,1... | collective-permute-start | bytes 4718600 | tf_op jit(solution)/shard_map/ppermute | solution.py:48
  1403.7 243.7 %all-reduce.22.cloned.1.call-start = ((), (), s32[]{:S(2)}) async-start(), calls=%async_computation.2 | async-start | bytes 393216 | tf_op jit(solution)/shard_map/psum | solution.py:470
  1465.7 194.1 %collective-permute-start.91 = (bf16[256,1536]{1,0:T(8,128)(2,1)}, bf16[256,1536]{1,0:T(8,128)(2,1)}, u32[]{:S(2)}, u32[]{:S(2)}) collective-permute-start(bf16[256,1536]{1,0:T(8,128)(2,1)} %get-tuple-element.68), channel_id=1, source_target_pairs={{0,1},{1,3},{3,5},{5,7},{7,6},{6,4},{4,2},{2,0},{8,9},{9,11},{11,1... | collective-permute-start | bytes 2359304 | tf_op jit(solution)/shard_map/ppermute | solution.py:45
  1528.1 123.8 %collective-permute-start.94 = (bf16[256,1536]{1,0:T(8,128)(2,1)}, bf16[256,1536]{1,0:T(8,128)(2,1)}, u32[]{:S(2)}, u32[]{:S(2)}) collective-permute-start(bf16[256,1536]{1,0:T(8,128)(2,1)} %add_convert_fusion.6), channel_id=1, source_target_pairs={{1,0},{3,1},{5,3},{7,5},{6,7},{4,6},{2,4},{0,2},{9,8},{11,9},{13,1... | collective-permute-start | bytes 2359304 | tf_op jit(solution)/shard_map/ppermute | solution.py:48
  1535.5 116.3 %collective-permute-start.117 = (bf16[128,512]{1,0:T(8,128)(2,1)}, bf16[128,512]{1,0:T(8,128)(2,1)S(1)}, u32[]{:S(2)}, u32[]{:S(2)}) collective-permute-start(bf16[128,512]{1,0:T(8,128)(2,1)} %get-tuple-element.133), channel_id=1, source_target_pairs={{0,16},{16,0},{8,24},{24,8},{1,17},{17,1},{9,25},{25,9},{2,18},{18... | collective-permute-start | bytes 393224 | tf_op jit(solution)/shard_map/ppermute | solution.py:45
  (239 other events, 5756.1 us)
Sparse Core Ops, SparseCore 0:
  1515.9 131.5 all-reduce.21

commit v2 on v1

v2 whole, which is shorter than its diff:
```python
import functools

import jax
import jax.numpy as jnp
from jax import lax
from jax.experimental import pallas as pl
from jax.experimental.pallas import tpu as pltpu
from jax.sharding import PartitionSpec as P

HEAD_DIM = 128
CORES = 2
ROWS_Z = 4
VMEM_BYTES = 56 << 20

epsilon = 1e-05
rope_theta = 10000.0
BF = jnp.bfloat16
F32 = jnp.float32


def dot(a, b, dims):
    return lax.dot_general(a, b, (dims, ((), ())), preferred_element_type=F32)


def after(v, *others):
    return lax.optimization_barrier((v, *others))[0]


def zero_of(*arrays):
    return sum(a[(0,) * a.ndim].astype(F32) for a in arrays) * 0.0


def ring_order(count):
    rows = ROWS_Z if count % ROWS_Z == 0 else 1
    across = count // rows
    walk = [(0, 0)]
    for z in range(rows):
        xs = range(1, across)
        walk += [(z, x) for x in (xs if z % 2 == 0 else reversed(xs))]
    walk += [(z, 0) for z in range(rows - 1, 0, -1)]
    return [z * across + x for z, x in walk]


class Ring:
    def __init__(self, axis, rings):
        self.axis = axis
        self.size = len(rings[0])
        self.right = [
            (r[i], r[(i + 1) % self.size]) for r in rings for i in range(self.size)
        ]
        self.left = [(b, a) for a, b in self.right]

    def go_right(self, v):
        return lax.ppermute(v, self.axis, self.right)

    def go_left(self, v):
        return lax.ppermute(v, self.axis, self.left)

    def gather(self, v):
        if self.size == 2:
            return [v, self.go_right(v)]
        walk = Gather(self, v)
        for _ in range(self.size // 2):
            walk.hop()
        return walk.got

    def scatter(self, part, dtype=BF):
        n = self.size
        far = part(n // 2).astype(dtype)
        if n == 2:
            return part(0) + self.go_right(far).astype(F32)
        half = far.shape[0] // 2
        from_left = self.go_right(far[:half]).astype(F32)
        from_right = self.go_left(far[half:]).astype(F32)
        from_left = jnp.concatenate([from_left, jnp.zeros_like(from_left)], axis=0)
        from_right = jnp.concatenate([jnp.zeros_like(from_right), from_right], axis=0)
        for s in range(n // 2 - 1, 0, -1):
            to_right = (part(s) + from_left).astype(dtype)
            to_left = (part(n - s) + from_right).astype(dtype)
            from_left = self.go_right(to_right).astype(F32)
            from_right = self.go_left(to_left).astype(F32)
        return part(0) + from_left + from_right

class Home:
    def __init__(self, ring, far):
        half = far.shape[0] // 2
        self.ring, self.near, self.half = ring, ring.size // 2, half
        self.arrived = ring.go_right(far[:half]), ring.go_left(far[half:])

    def hop(self, to_left, to_right):
        left, right = self.arrived
        if self.near == self.ring.size // 2:
            to_right = jnp.concatenate([to_right[: self.half] + left, to_right[self.half :]], axis=0)
            to_left = jnp.concatenate([to_left[: self.half], to_left[self.half :] + right], axis=0)
        else:
            to_right, to_left = to_right + left, to_left + right
        self.near -= 1
        self.arrived = self.ring.go_right(to_right), self.ring.go_left(to_left)


class Line:
    def __init__(self):
        self.last = ()

    def mark(self, *arrays):
        self.last = arrays

    def tie(self, v):
        return after(v, *self.last) if self.last else v

    def zero(self):
        return zero_of(*self.last).astype(jnp.int32).reshape(1)


class Gather:
    def __init__(self, ring, v):
        self.ring, self.count = ring, 0
        self.got = [v] + [None] * (ring.size - 1)
        self.latest = (v, v)

    def hop(self):
        n, (right, left) = self.ring.size, self.latest
        self.count += 1
        s = self.count
        if s < n // 2:
            self.latest = self.ring.go_right(right), self.ring.go_left(left)
            self.got[s], self.got[n - s] = self.latest
        elif s == n // 2:
            half = right.shape[0] // 2
            self.latest = self.ring.go_right(right[:half]), self.ring.go_left(left[half:])
            self.got[s] = jnp.concatenate(self.latest, axis=0)


def _scores(q, k, row0, scale):
    raw = dot(q, k, ((1,), (1,))) * scale
    rows = lax.broadcasted_iota(jnp.int32, raw.shape, 0) + row0
    cols = lax.broadcasted_iota(jnp.int32, raw.shape, 1)
    return jnp.where(cols <= rows, raw, -1e30)


def _turn(v, cosine, sine):
    return v * cosine + pltpu.roll(v, HEAD_DIM // 2, 1) * sine


def _attend_kernel(place, qp, kp, vp, rq, rk, cosine, sine, gq, gk, o_ref, q_s, k_s, v_s, lse_ref, o_s, *, half, blocks, tile, scale):
    for b in range(blocks):
        at, to = pl.ds(pl.multiple_of(place[b] * half, half), half), slice(b * half, (b + 1) * half)
        c, s = cosine[at, :], sine[at, :]
        q_s[to, :] = _turn(qp[at, :] * rq[at, :] * gq[...], c, s).astype(BF)
        k_s[to, :] = _turn(kp[at, :] * rk[at, :] * gk[...], c, s).astype(BF)
        v_s[to, :] = vp[at, :].astype(BF)
    for i in range(half * blocks // tile):
        width = (i + 1) * tile
        s = _scores(q_s[i * tile : width, :], k_s[:width, :], i * tile, scale)
        top = jnp.max(s, axis=-1, keepdims=True)
        total = top + jnp.log(jnp.sum(jnp.exp(s - top), axis=-1, keepdims=True))
        p = jnp.exp(s - total).astype(BF)
        o_s[i * tile : width, :] = dot(p, v_s[:width, :], ((1,), (0,))).astype(BF)
        lse_ref[0, i * tile : width, :] = total
    for b in range(blocks):
        at = pl.multiple_of(place[b] * half, half)
        o_ref[pl.ds(at, half), :] = o_s[b * half : (b + 1) * half, :]


def _attend_back_kernel(place, q_s, k_s, v_s, d_ref, lse_ref, qp, kp, rq, rk, cosine, sine, gq, gk, wq_ref, wk_ref, dv_ref, in_ref, gain_ref,
                        d_s, dq_s, dk_s, dv_s, *, half, blocks, tile, scale):
    for b in range(blocks):
        at = pl.ds(pl.multiple_of(place[b] * half, half), half)
        d_s[b * half : (b + 1) * half, :] = d_ref[at, :]
    count = half * blocks // tile
    for i in reversed(range(count)):
        width = (i + 1) * tile
        here = slice(i * tile, width)
        q, d, k, v = q_s[here, :], d_s[here, :], k_s[:width, :], v_s[:width, :]
        p = jnp.exp(_scores(q, k, i * tile, scale) - lse_ref[0, here, :])
        dp = dot(d, v, ((1,), (1,)))
        row = jnp.sum(p * dp, axis=-1, keepdims=True)
        ds = (p * (dp - row)).astype(BF)
        dq_s[here, :] = dot(ds, k, ((1,), (0,)))
        dk = dot(ds, q, ((0,), (0,)))
        dv = dot(p.astype(BF), d, ((0,), (0,)))
        if i == count - 1:
            dk_s[:width, :] = dk
            dv_s[:width, :] = dv
        else:
            dk_s[:width, :] += dk
            dv_s[:width, :] += dv

    @pl.when(pl.program_id(0) == 0)
    def _():
        in_ref[...] = jnp.zeros_like(in_ref)

    sums = [jnp.zeros((1, HEAD_DIM), F32)] * 2
    lane = lax.broadcasted_iota(jnp.int32, (1, in_ref.shape[1]), 1)
    for b in range(blocks):
        at, here = pl.ds(pl.multiple_of(place[b] * half, half), half), slice(b * half, (b + 1) * half)
        c, s = cosine[at, :], sine[at, :]
        for n, (grad, pre, r, gain, out) in enumerate(((dq_s, qp, rq, gq, wq_ref), (dk_s, kp, rk, gk, wk_ref))):
            t = _turn(grad[here, :] * scale, c, -s)
            value = pre[at, :]
            w = t * gain[...]
            out[at, :] = w
            in_ref[at, :] += jnp.where(lane == n, jnp.sum(value * w, axis=-1, keepdims=True), 0.0)
            sums[n] = sums[n] + jnp.sum(t * value * r[at, :], axis=0, keepdims=True)
        dv_ref[at, :] = dv_s[here, :].astype(BF)
    gain_ref[0:1, :] = sums[0]
    gain_ref[1:2, :] = sums[1]


def _head_specs(rows, heads):
    head = lambda k: pl.BlockSpec((rows, HEAD_DIM), lambda h, place: (0, k * heads + h))
    lse = pl.BlockSpec((1, rows, 1), lambda h, place: (h, 0, 0))
    col = pl.BlockSpec((rows, 1), lambda h, place: (0, 0))
    table = pl.BlockSpec((rows, HEAD_DIM), lambda h, place: (0, 0))
    gain = pl.BlockSpec((1, HEAD_DIM), lambda h, place: (0, h))
    return head, lse, col, table, gain


def _sizes(rows, half):
    return dict(half=half, blocks=rows // half, tile=min(384, rows), scale=HEAD_DIM**-0.5)


def attend(place, qkv, rq, rk, cosine, sine, gq, gk, half):
    rows, width = qkv.shape[0], qkv.shape[1] // 3
    heads = width // HEAD_DIM
    head, lse, col, table, gain = _head_specs(rows, heads)
    return pl.pallas_call(
        functools.partial(_attend_kernel, **_sizes(rows, half)),
        grid_spec=pltpu.PrefetchScalarGridSpec(
            num_scalar_prefetch=1,
            grid=(heads,),
            in_specs=[head(0), head(1), head(2), col, col, table, table, gain, gain],
            out_specs=[head(0)] * 4 + [lse],
            scratch_shapes=[pltpu.VMEM((rows, HEAD_DIM), BF)],
        ),
        out_shape=[jax.ShapeDtypeStruct((rows, width), BF)] * 4 + [jax.ShapeDtypeStruct((heads, rows, 1), F32)],
        compiler_params=pltpu.CompilerParams(vmem_limit_bytes=VMEM_BYTES),
        cost_estimate=pl.CostEstimate(flops=2 * rows * rows * width * 2, bytes_accessed=20 * rows * width, transcendentals=heads * rows * rows),
        name="attend",
    )(place, qkv, qkv, qkv, rq, rk, cosine, sine, gq, gk)


def attend_back(place, q, k, v, d, lse_in, qkv, rq, rk, cosine, sine, gq, gk, half):
    rows, width = q.shape
    heads = width // HEAD_DIM
    head, lse, col, table, gain = _head_specs(rows, heads)
    return pl.pallas_call(
        functools.partial(_attend_back_kernel, **_sizes(rows, half)),
        grid_spec=pltpu.PrefetchScalarGridSpec(
            num_scalar_prefetch=1,
            grid=(heads,),
            in_specs=[head(0)] * 4 + [lse, head(0), head(1), col, col, table, table, gain, gain],
            out_specs=[head(0)] * 3
            + [pl.BlockSpec((rows, 8), lambda h, place: (0, 0)), pl.BlockSpec((2, HEAD_DIM), lambda h, place: (0, h))],
            scratch_shapes=[pltpu.VMEM((rows, HEAD_DIM), BF)] + [pltpu.VMEM((rows, HEAD_DIM), F32)] * 3,
        ),
        out_shape=[
            jax.ShapeDtypeStruct((rows, width), F32),
            jax.ShapeDtypeStruct((rows, width), F32),
            jax.ShapeDtypeStruct((rows, width), BF),
            jax.ShapeDtypeStruct((rows, 8), F32),
            jax.ShapeDtypeStruct((2, width), F32),
        ],
        compiler_params=pltpu.CompilerParams(vmem_limit_bytes=VMEM_BYTES),
        cost_estimate=pl.CostEstimate(flops=5 * rows * rows * width * 2, bytes_accessed=28 * rows * width, transcendentals=heads * rows * rows),
        name="attend_back",
    )(place, q, k, v, d, lse_in, qkv, qkv, rq, rk, cosine, sine, gq, gk)


def _columns_kernel(place, *refs, pieces, weights, cols):
    for r in range(pieces):
        at = pl.ds(pl.multiple_of(place[r] * cols, cols), cols)
        for w in range(weights):
            refs[pieces + w][:, at] = refs[r][:, w * cols : (w + 1) * cols].astype(F32)


def columns(place, blocks, rows, cols):
    n, tile = len(blocks), min(rows, 64)
    weights = blocks[0].shape[1] // cols
    return pl.pallas_call(
        functools.partial(_columns_kernel, pieces=n, weights=weights, cols=cols),
        grid_spec=pltpu.PrefetchScalarGridSpec(
            num_scalar_prefetch=1,
            grid=(rows // tile,),
            in_specs=[pl.BlockSpec((tile, weights * cols), lambda i, place: (i, 0))] * n,
            out_specs=[pl.BlockSpec((tile, n * cols), lambda i, place: (i, 0))] * weights,
        ),
        out_shape=[jax.ShapeDtypeStruct((rows, n * cols), F32)] * weights,
        compiler_params=pltpu.CompilerParams(vmem_limit_bytes=VMEM_BYTES),
        name="columns",
    )(place, *blocks)


PAD=128

def pick_rows(slot_row, cap):
    return (lax.broadcasted_iota(jnp.int32, (cap, slot_row.shape[1]), 0) == slot_row).astype(BF)

def pick_back(slot_col, cap):
    return (lax.broadcasted_iota(jnp.int32, (slot_col.shape[0], cap), 1) == slot_col).astype(BF)

def _dispatch_kernel(*refs, count, cap):
    slot, rows, w, out_x, out_w = refs[0], refs[1:1+count], refs[1+count], refs[2+count], refs[3+count]
    @pl.when(pl.program_id(1) == 0)
    def _():
        for s in range(count):
            out_x[0, s*cap:(s+1)*cap, :] = dot(pick_rows(slot[s], cap), rows[s][...], ((1,),(0,))).astype(BF)
    out_w[0] = dot(out_x[0], w[0], ((1,),(0,))).astype(BF)

def dispatch(slots, at, rows, w, cap, tile=512):
    n, (J, D, F), T = len(rows), w.shape, rows[0].shape[0]
    M = n * cap
    return pl.pallas_call(
        functools.partial(_dispatch_kernel, count=n, cap=cap),
        grid=(J, F // tile),
        in_specs=[pl.BlockSpec((n, None, 1, T), lambda j, f: (at, j, 0, 0))]
        + [pl.BlockSpec((T, D), lambda j, f: (0, 0), pipeline_mode=pl.Buffered(1))] * n
        + [pl.BlockSpec((1, D, tile), lambda j, f: (j, 0, f))],
        out_specs=[pl.BlockSpec((1, M, D), lambda j, f: (j, 0, 0)), pl.BlockSpec((1, M, tile), lambda j, f: (j, 0, f))],
        out_shape=[jax.ShapeDtypeStruct((J, M, D), BF), jax.ShapeDtypeStruct((J, M, F), BF)],
        compiler_params=pltpu.CompilerParams(vmem_limit_bytes=VMEM_BYTES),
        cost_estimate=pl.CostEstimate(flops=2 * J * M * D * (F + T), bytes_accessed=2 * (J * D * F + n * T * D + J * M * (D + F)), transcendentals=0),
        name="dispatch",
    )(slots, *rows, w)


def _expert_kernel(first, slot, *refs, count, cap, experts):
    rows = refs[:count]
    wg, wu, dw, out_x, out_dg, out_du, out_in, out_dgate, gate = refs[count:]
    D = wg.shape[1]
    f = pl.program_id(1)
    @pl.when(f == 0)
    def _():
        mine = lax.broadcasted_iota(jnp.int32, (1, PAD), 1)
        me = first[0] + pl.program_id(0)
        mask = ((mine == me) | (mine == me + experts)).astype(F32)
        for s in range(count):
            at = slice(s*cap,(s+1)*cap)
            got = dot(pick_rows(slot[s], cap), rows[s][...], ((1,),(0,)))
            out_x[0, at, :] = got[:, :D].astype(BF)
            gate[at, :] = jnp.sum(got[:, D:]*mask, axis=-1, keepdims=True)
        out_dgate[...] = jnp.zeros_like(out_dgate)
    x = out_x[0]
    g = dot(x, wg[0], ((1,),(0,)))
    u = dot(x, wu[0], ((1,),(0,)))
    sig = 1.0/(1.0+jnp.exp(-g))
    act = g*sig
    inner = act*u
    d = dw[0].astype(F32)
    out_dgate[0] += jnp.sum(inner*d, axis=-1, keepdims=True)
    scaled = gate[...]
    d = d*scaled
    out_in[0] = (inner*scaled).astype(BF)
    out_du[0] = (d*act).astype(BF)
    out_dg[0] = (d*u*(sig + act*(1.0-sig))).astype(BF)

def expert(first, slots, at, rows, w_gu, dw, cap, experts, tile=512):
    n=len(rows); J, D2, F = w_gu.shape; D=D2//2; T=rows[0].shape[0]; M=n*cap
    return pl.pallas_call(
        functools.partial(_expert_kernel, count=n, cap=cap, experts=experts),
        grid=(J, F//tile),
        in_specs=[pl.BlockSpec(memory_space=pltpu.SMEM), pl.BlockSpec((n, None, 1, T), lambda j,f:(at,j,0,0))]
          +[pl.BlockSpec((T,D+PAD), lambda j,f:(0,0), pipeline_mode=pl.Buffered(1))]*n
          +[pl.BlockSpec((1,D,tile), lambda j,f:(j,0,f)), pl.BlockSpec((1,D,tile), lambda j,f:(j,1,f)), pl.BlockSpec((1,M,tile), lambda j,f:(j,0,f))],
        out_specs=[pl.BlockSpec((1,M,D), lambda j,f:(j,0,0))]+[pl.BlockSpec((1,M,tile), lambda j,f:(j,0,f))]*3+[pl.BlockSpec((1,M,1), lambda j,f:(j,0,0))],
        out_shape=[jax.ShapeDtypeStruct((J,M,D),BF)]+[jax.ShapeDtypeStruct((J,M,F),BF)]*3+[jax.ShapeDtypeStruct((J,M,1),F32)],
        scratch_shapes=[pltpu.VMEM((M,1),F32)],
        compiler_params=pltpu.CompilerParams(vmem_limit_bytes=VMEM_BYTES),
        cost_estimate=pl.CostEstimate(flops=2*J*M*D*(2*F+T), bytes_accessed=2*(J*D2*F+n*T*D+J*M*(D+4*F)), transcendentals=J*M*F),
        name="expert",
    )(first, slots, *rows, w_gu, w_gu, dw)

def _plus(part, which, more, cols):
    if which is None:
        return part
    more = more[:, cols].astype(F32)
    half = part.shape[0] // 2
    if which == "top":
        return jnp.concatenate([part[:half] + more, part[half:]], axis=0)
    if which == "low":
        return jnp.concatenate([part[:half], part[half:] + more], axis=0)
    return part + more

def _combine_kernel(*refs, terms, count, cap, tile, extra, adds, experts):
    it = iter(refs)
    first = next(it) if extra else None
    slot = next(it)
    factors = [(next(it), next(it)) for _ in range(terms)]
    dgate = next(it) if extra else None
    adds_in = [next(it) if a is not None else None for a in adds]
    outs = [next(it) for _ in range(count)]
    acc = next(it)
    n, j, last = pl.program_id(0), pl.program_id(1), pl.num_programs(1) - 1
    total = None
    for a, w in factors:
        part = dot(a[j], w[0], ((1,),(1,)))
        total = part if total is None else total + part
    total = total.astype(BF)
    cols = pl.ds(pl.multiple_of(n*tile, tile), tile)
    for s in range(count):
        back = pick_back(slot[s, j], cap)
        part = dot(back, total[s*cap:(s+1)*cap], ((1,),(0,)))
        @pl.when(j == 0)
        def _(): acc[s] = _plus(part, adds[s], adds_in[s], cols)
        @pl.when((j > 0) & (j < last))
        def _(): acc[s] += part
        @pl.when(j == last)
        def _(): outs[s][:, cols] = (acc[s] + part).astype(outs[s].dtype)
    if extra:
        D = outs[0].shape[1] - PAD
        @pl.when(n == 0)
        def _():
            lane = lax.broadcasted_iota(jnp.int32, (1, PAD), 1)
            me = first[0] + j
            for s in range(count):
                v = dgate[j, s*cap:(s+1)*cap, :]
                hi = v.astype(BF).astype(F32)
                spread = jnp.where(lane == me, hi, 0.0) + jnp.where(lane == me + experts, v - hi, 0.0)
                part = dot(pick_back(slot[s, j], cap), spread.astype(BF), ((1,),(0,)))
                @pl.when(j == 0)
                def _(): outs[s][:, D:] = _plus(part, adds[s], adds_in[s], slice(D, D + PAD)).astype(outs[s].dtype)
                @pl.when(j > 0)
                def _(): outs[s][:, D:] = (outs[s][:, D:].astype(F32) + part).astype(outs[s].dtype)

def combine(slots, at, factors, cap, adds, first=None, dgate=None, experts=0, tile=1024, out_dtype=BF):
    n = len(adds)
    _, J, T, _ = slots.shape
    M, F = factors[0][0].shape[1:]
    D = factors[-1][1].shape[1] // (factors[-1][2] + 1)
    extra = dgate is not None
    width = D + (PAD if extra else 0)
    steps = D // tile
    one = pl.Buffered(1)
    ops, specs = [], []
    if extra:
        ops.append(first)
        specs.append(pl.BlockSpec(memory_space=pltpu.SMEM))
    ops.append(slots)
    specs.append(pl.BlockSpec((n, J, T, 1), lambda i, j: (at, 0, 0, 0), pipeline_mode=one))
    for a, w, block in factors:
        ops += [a, w]
        specs += [
            pl.BlockSpec((J, M, F), lambda i, j: (0, 0, 0), pipeline_mode=one),
            pl.BlockSpec((1, tile, F), lambda i, j, block=block: (j, block * steps + i, 0)),
        ]
    if extra:
        ops.append(dgate)
        specs.append(pl.BlockSpec((J, M, 1), lambda i, j: (0, 0, 0), pipeline_mode=one))
    for a in adds:
        if a is not None:
            ops.append(a[1])
            specs.append(pl.BlockSpec(a[1].shape, lambda i, j: (0, 0), pipeline_mode=one))
    return pl.pallas_call(
        functools.partial(_combine_kernel, terms=len(factors), count=n, cap=cap, tile=tile, extra=extra, adds=[a and a[0] for a in adds], experts=experts),
        grid=(steps, J),
        in_specs=specs,
        out_specs=[pl.BlockSpec((T, width), lambda i, j: (0, 0))] * n,
        out_shape=[jax.ShapeDtypeStruct((T, width), out_dtype)] * n,
        scratch_shapes=[pltpu.VMEM((n, T, tile), F32)],
        compiler_params=pltpu.CompilerParams(vmem_limit_bytes=VMEM_BYTES),
        cost_estimate=pl.CostEstimate(flops=2 * J * M * D * (len(factors) * F + T), bytes_accessed=2 * len(factors) * J * F * (D + M) + 4 * n * T * D, transcendentals=0),
        name="combine",
    )(*ops)


def _wgrad_kernel(_, *refs, count, pieces):
    xs, gs, outs = refs[:count], refs[count : 2 * count], refs[2 * count :]
    total = None
    for x, g in zip(xs, gs):
        part = dot(x[0], g[0], ((0,), (0,)))
        total = part if total is None else total + part
    for p in range(pieces):

        @pl.when(pl.program_id(2) == p)
        def _(p=p):
            outs[p][0] = total.astype(BF)


def wgrad(order, xs, gs, pieces, tile=2048):
    J, _, D = xs[0].shape
    F = gs[0].shape[2]
    p, n, rows = F // pieces, len(xs), sum(g.shape[1] for g in gs)
    tile = min(tile, D)
    return pl.pallas_call(
        functools.partial(_wgrad_kernel, count=n, pieces=pieces),
        grid=(J, D // tile, pieces),
        in_specs=[pl.BlockSpec(memory_space=pltpu.SMEM)]
        + [pl.BlockSpec((1, x.shape[1], tile), lambda j, i, c: (j, 0, i)) for x in xs]
        + [pl.BlockSpec((1, g.shape[1], p), lambda j, i, c: (j, 0, c)) for g in gs],
        out_specs=[pl.BlockSpec((1, tile, p), lambda j, i, c: (j, i, 0))] * pieces,
        out_shape=[jax.ShapeDtypeStruct((J, D, p), BF)] * pieces,
        compiler_params=pltpu.CompilerParams(vmem_limit_bytes=VMEM_BYTES),
        cost_estimate=pl.CostEstimate(flops=2 * J * rows * D * F, bytes_accessed=2 * J * (rows * (D + F) + D * F), transcendentals=0),
        name="wgrad",
    )(order, *xs, *gs)


def inv_rms(matrix):
    return lax.rsqrt(jnp.mean(matrix * matrix, axis=-1, keepdims=True) + epsilon)


def norm_back(value, gain, grad):
    r = inv_rms(value)
    weighted = gain * grad
    inside = jnp.mean(value * weighted, axis=-1, keepdims=True)
    return r * weighted - value * (r * r * r * inside), jnp.sum(grad * value * r, axis=0)


def angle_tables(positions):
    half_width = HEAD_DIM // 2
    inverse = rope_theta ** (-(jnp.arange(half_width, dtype=F32) * 2.0) / HEAD_DIM)
    angles = positions.astype(F32)[:, None] * inverse[None, :]
    angles = jnp.concatenate([angles, angles], axis=-1)
    sign = jnp.where(jnp.arange(HEAD_DIM) < half_width, -1.0, 1.0)
    return jnp.cos(angles), jnp.sin(angles) * sign


def per_device(
    exp_walk,
    layer_input,
    block_ids,
    routes,
    w_query,
    w_key,
    w_value,
    w_output,
    w_router,
    norm_gains,
    w_gate_up,
    w_down,
    d_out,
):
    C, E = lax.axis_size("ctx"), lax.axis_size("exp")
    c, e = lax.axis_index("ctx"), lax.axis_index("exp")
    Y = C // CORES
    ring = Ring("exp", [exp_walk])
    ctx_ring = Ring("ctx", [[y * CORES + k for y in range(Y)] for k in range(CORES)])
    sibling = [(i, i ^ 1) for i in range(C)]

    def swap(v):
        return lax.ppermute(v, "ctx", sibling)

    def ctx_gather(v):
        got = []
        for block in ctx_ring.gather(v):
            got += [block, swap(block)]
        return got

    def chip_sums(part):
        return [part(dy * CORES).astype(F32) + swap(part(dy * CORES + 1).astype(BF)).astype(F32) for dy in range(Y)]

    def y_sum(mine):
        return ctx_ring.scatter(lambda s: mine[(Y - s) % Y])

    def ctx_sum(rows):
        n = rows.shape[0]
        blocks = jnp.transpose(rows.reshape(n, C, -1), (1, 0, 2))
        whole = jnp.zeros_like(blocks)
        for r in range(C):
            whole = lax.dynamic_update_slice(whole, blocks[r : r + 1], (other_u[r], zero, zero))
        whole = lax.psum(whole, "ctx")
        return jnp.concatenate([lax.dynamic_index_in_dim(whole, other_u[r], 0, False) for r in range(C)], axis=1)

    zero = jnp.uint32(0)
    where = {d: i for i, d in enumerate(exp_walk)}
    left_table = [[exp_walk[(where[i] - s) % E] for s in range(E)] for i in range(E)]
    left_now = lax.dynamic_index_in_dim(jnp.array(left_table, jnp.uint32), e.astype(jnp.uint32), 0, False)
    left_of = [left_now[s] for s in range(E)]

    def put_rows(blocks):
        full = jnp.zeros((E, *blocks[0].shape), BF)
        for s in range(E):
            full = lax.dynamic_update_slice(full, blocks[s][None], (left_of[s], zero, zero))
        return full
    ctx_table = [
        [(i // CORES - r // CORES) % Y * CORES + (i % CORES ^ r % CORES) for r in range(C)] for i in range(C)
    ]
    others = lax.dynamic_index_in_dim(jnp.array(ctx_table, jnp.int32), c.astype(jnp.uint32), 0, False)
    other_u = [others[r].astype(jnp.uint32) for r in range(C)]

    T, D = layer_input.shape[1:]
    rows_e = w_query.shape[0]
    cols_c = D // C
    S = T * C
    half = T // 2
    c_col = (c * cols_c).astype(jnp.uint32)
    NE = w_router.shape[1]
    K = routes.shape[2]
    J = w_gate_up.shape[0]
    cap = (5 * T * K + 4 * NE - 1) // (4 * NE)
    room = -(-cap // 16) * 16
    x = layer_input[0]
    grad_out = d_out[0]

    x_blocks = ctx_gather(x)
    x_all = jnp.concatenate(x_blocks, axis=0)

    small = jnp.concatenate([w_router.reshape(-1), norm_gains.reshape(-1), routes.astype(BF).reshape(-1)])
    small_len = small.shape[0]
    small = jnp.pad(small, (0, -small_len % 4096)).reshape(-1, 128)
    w_qkv_mine = jnp.concatenate(
        [lax.dynamic_slice_in_dim(w, c_col, cols_c, axis=1) for w in (w_query, w_key, w_value)], axis=1
    )
    qkv_walk, small_walk = Gather(ring, w_qkv_mine), Gather(ring, small)
    for _ in range(E // 2):
        small_walk.hop()
        qkv_walk.hop()
        if qkv_walk.count == 2:
            qkv_walk.latest = [v + zero_of(x_blocks[-CORES]).astype(BF) for v in qkv_walk.latest]
        small_walk.latest = [after(v, *qkv_walk.latest) for v in small_walk.latest]
    order = [E // 2, 0] + [i for s in range(1, E // 2) for i in (s, E - s)]
    small_all = jnp.stack([small_walk.got[i] for i in order])
    by_owner = put_rows(small_walk.got)
    cut = rows_e * NE // 128, rows_e * (NE + norm_gains.shape[1]) // 128, small_len // 128
    router_full = by_owner[:, : cut[0]].reshape(D, NE)
    gains = by_owner[:, cut[0] : cut[1]].reshape(D, -1).astype(F32).T
    routes_all = small_all[:, cut[1] : cut[2]].reshape(E, T * K)

    def my_columns(w):
        return lax.dynamic_slice_in_dim(w, c_col, cols_c, axis=1)

    qkv_blocks = qkv_walk.got
    w_qkv = put_rows(qkv_blocks).reshape(D, 3 * cols_c)
    qkv_there = qkv_blocks[E // 2]
    w_out_cols = lax.all_gather(my_columns(w_output), "exp", axis=0, tiled=True)
    w_out_rows = lax.all_to_all(w_out_cols.reshape(C, cols_c, cols_c), "ctx", split_axis=0, concat_axis=0, tiled=True)
    w_out_rows = jnp.transpose(w_out_rows, (1, 0, 2)).reshape(cols_c, D)

    d_walk = Gather(ring, after(grad_out, qkv_there))
    d_walk.hop()
    dn_blocks = ctx_gather(w_down)
    w_dn = jnp.concatenate(dn_blocks, axis=2)

    def hold(v, *others):
        return v + zero_of(*others).astype(v.dtype)

    gu_first = ctx_gather(hold(w_gate_up[: J // 2], dn_blocks[-CORES]))

    blocks_rel = jnp.stack([lax.dynamic_slice_in_dim(block_ids[0], other_u[r] * 2, 2) for r in range(C)]).reshape(-1)
    positions = (blocks_rel[:, None] * half + jnp.arange(half, dtype=jnp.int32)[None, :]).reshape(-1)
    count = jnp.arange(2 * C, dtype=jnp.int32)
    place = jnp.sum(jnp.where(blocks_rel[None, :] == count[:, None], count[None, :], 0), axis=1)
    cosine, sine = angle_tables(positions)
    gain_q = lax.dynamic_slice_in_dim(gains[1:2], c_col, cols_c, axis=1)
    gain_k = lax.dynamic_slice_in_dim(gains[2:3], c_col, cols_c, axis=1)

    groups = [([0], 1)] + [([s, E - s], s) for s in range(1, E // 2)] + [([E // 2], 0)]
    first = (e * J).astype(jnp.int32).reshape(1)
    mine = first[0] + jnp.arange(J, dtype=jnp.int32)
    pairs = (routes_all[:, None, :] == mine[None, :, None].astype(BF)).astype(BF).reshape(E * J, T * K)
    token = jnp.arange(T * K)[:, None] // K
    chosen = dot(pairs, (token == jnp.arange(T)[None, :]).astype(BF), ((1,), (0,)))
    rank = dot(pairs, (token < jnp.arange(T)[None, :]).astype(BF), ((1,), (0,)))
    slot = jnp.where((chosen > 0.5) & (rank < cap), rank, -1.0).astype(jnp.int32).reshape(E, J, T)
    slot_row, slot_col = slot[:, :, None, :], slot[:, :, :, None]

    line, d_slots = Line(), {}

    def fetch(g):
        members, at = groups[g]
        d_slots[g] = dispatch(line.tie(slot_row), at, [d_walk.got[i] for i in members], w_dn, room)
        line.mark(d_slots[g][1])

    fetch(0)
    x_all32 = x_all.astype(F32)
    n1 = (x_all32 * inv_rms(x_all32) * gains[0]).astype(BF)
    qkv = dot(n1, w_qkv, ((1,), (0,)))
    qp, kp = qkv[:, :cols_c], qkv[:, cols_c : 2 * cols_c]
    squares = hold(jnp.stack([jnp.sum(qp * qp, axis=1), jnp.sum(kp * kp, axis=1)]), gu_first[-CORES], d_slots[0][1])
    scales = lax.rsqrt(ctx_sum(squares) / D + epsilon)
    r_q, r_k = scales[0][:, None], scales[1][:, None]
    d_walk.latest = [hold(v, scales) for v in d_walk.latest]
    d_walk.hop()
    gu_last = ctx_gather(hold(w_gate_up[J // 2 :], scales))
    w_gu = jnp.concatenate([jnp.concatenate(b, axis=2) for b in (gu_first, gu_last)], axis=0)
    attn, q, k, v, lse = attend(place, qkv, r_q, r_k, cosine, sine, gain_q, gain_k, half)
    branch_part = dot(attn, w_out_rows, ((1,), (0,))).astype(BF)
    chips = chip_sums(lambda r: branch_part[r * T : (r + 1) * T])
    branch = y_sum([hold(v, gu_last[-CORES]) for v in chips])
    d_walk.latest = [hold(v, branch_part) for v in d_walk.latest]
    while d_walk.count < E // 2 - 1:
        d_walk.hop()
    line.mark(branch_part)
    fetch(1)
    branch = hold(branch, w_gu, d_slots[1][1])
    hidden = x.astype(F32) + branch
    n2 = (hidden * inv_rms(hidden) * gains[3]).astype(BF)
    router_own = jax.nn.softmax(dot(n2, router_full, ((1,), (0,))), axis=-1)
    router_high = router_own.astype(BF)
    router_low = (router_own - router_high.astype(F32)).astype(BF)
    n2_wide = jnp.concatenate([n2, router_high, router_low, jnp.zeros((T, PAD - 2 * NE), BF)], axis=1)

    line, n2_walk, done = Line(), Gather(ring, n2_wide), {}

    def work(g):
        members, at = groups[g]
        done[g] = expert(first, line.tie(slot_row), at, [n2_walk.got[i] for i in members], w_gu, d_slots[g][1], room, NE)
        line.mark(done[g][1])

    def back(g):
        members, at = groups[g]
        _, dg, du, _, dgate = done[g]
        kind = F32 if members == [0] else BF
        got = combine(line.tie(slot_col), at, [(dg, w_gu, 0), (du, w_gu, 1)], room, [None] * len(members), first, dgate, NE, out_dtype=kind)
        line.mark(got[0])
        return got

    def mix(g):
        members, at = groups[g]
        kind = F32 if members == [0] else BF
        got = combine(line.tie(slot_col), at, [(done[g][3], w_dn, 0)], room, [None] * len(members), out_dtype=kind)
        line.mark(got[0])
        return got

    def grads(left, right):
        parts = wgrad(line.zero(), left, right, C)
        line.mark(parts[0])
        return chip_sums(lambda r: parts[r])

    far = E // 2
    n2_walk.hop()
    d_walk.latest = [hold(v, n2_wide) for v in d_walk.latest]
    d_walk.hop()
    line.mark(n2_wide)
    work(0)
    fetch(2)
    for g in range(1, far + 1):
        line.mark(*n2_walk.latest, line.last[0])
        if g < far:
            n2_walk.hop()
        work(g)
        if g + 1 < far:
            fetch(g + 2)
    home = Home(ring, back(far)[0])
    for g in range(far - 1, 0, -1):
        terms = back(g)
        line.mark(*home.arrived, line.last[0])
        home.hop(*terms)
    [own] = back(0)
    chips_g = grads([done[i][0] for i in done], [done[i][1] for i in done])
    [mix_far] = mix(far)
    line.mark(*home.arrived, line.last[0])
    rows_back = own + home.arrived[0].astype(F32) + home.arrived[1].astype(F32)
    mixed = Home(ring, after(mix_far, *home.arrived))
    drouter = rows_back[:, D : D + NE] + rows_back[:, D + NE : D + 2 * NE]
    dlogits = (router_own * (drouter - jnp.sum(drouter * router_own, axis=-1, keepdims=True))).astype(BF)
    dn2 = rows_back[:, :D] + dot(dlogits, router_full, ((1,), (1,)))
    hidden_part, d_gain3 = norm_back(hidden, gains[3], dn2)
    dhidden = grad_out.astype(F32) + hidden_part
    dhidden_low = dhidden.astype(BF)
    dhidden_blocks = ctx_gather(dhidden_low)
    dhidden_all = jnp.concatenate(dhidden_blocks, axis=0)
    line.mark(dhidden_low)
    terms = {}
    for g in range(far - 1, -1, -1):
        terms[g] = mix(g)
        if g == far - 1:
            line.mark(*mixed.arrived, line.last[0])
            mixed.hop(*terms[g])
            line.mark(*terms[g])
            chips_u = grads([done[i][0] for i in done], [done[i][2] for i in done])
    sum_g = y_sum([hold(v, dhidden_blocks[-CORES]) for v in chips_g])

    def pump():
        if mixed.near > 1:
            line.mark(*mixed.arrived, *line.last)
            mixed.hop(*terms[mixed.near - 1])

    dattn = dot(after(dhidden_all, *line.last), w_out_rows, ((1,), (1,))).astype(BF)
    g_out = dot(attn, dhidden_all, ((0,), (0,))).astype(BF)
    line.mark(g_out, dattn)
    pump()
    wq, wk, dv, inside, d_gain_qk = attend_back(line.tie(place), q, k, v, dattn, lse, qkv, r_q, r_k, cosine, sine, gain_q, gain_k, half)
    line.mark(dv)
    pump()
    def next_hop(walk, of):
        if walk.near > 1:
            line.mark(*walk.arrived, *line.last)
            walk.hop(of(walk.near - 1), of(E - walk.near + 1))

    g_out = jnp.transpose(g_out.reshape(cols_c, C, cols_c), (1, 0, 2))
    g_out = lax.all_to_all(g_out, "ctx", split_axis=0, concat_axis=0, tiled=True).reshape(E, rows_e, cols_c)
    g_router = dot(dlogits, n2, ((0,), (0,)))
    spread = lax.dynamic_update_slice(jnp.zeros((2, D), F32), d_gain_qk, (zero, c_col))
    g_small = jnp.concatenate([g_router, spread, d_gain3[None]], axis=0)
    count = g_small.shape[0]
    g_small = jnp.transpose(g_small.reshape(count, E, rows_e), (1, 0, 2)).reshape(E, -1)
    unit = 3 * 16
    small_rows = -(-(rows_e * cols_c + count * rows_e) // (cols_c * unit)) * unit - rows_e
    g_small = jnp.pad(g_small, ((0, 0), (0, small_rows * cols_c - count * rows_e))).reshape(E, small_rows, cols_c)
    more = jnp.concatenate([g_out, g_small.astype(BF)], axis=1).reshape(E, -1, 3 * cols_c)
    more = lax.optimization_barrier(more)

    inside = ctx_sum(hold(line.tie(inside)[:, :2].T, sum_g, more)) / D
    dqp = r_q * wq - qp * (r_q * r_q * r_q * inside[0][:, None])
    dkp = r_k * wk - kp * (r_k * r_k * r_k * inside[1][:, None])
    dqkv = jnp.concatenate([dqp.astype(BF), dkp.astype(BF), dv], axis=1)
    g_qkv = dot(n1, dqkv, ((0,), (0,))).astype(BF).reshape(E, rows_e, 3 * cols_c)

    def of_qkv(s):
        return jnp.concatenate([lax.dynamic_index_in_dim(a, left_of[s], 0, False) for a in (g_qkv, more)], axis=0)

    qkv_home = Home(ring, of_qkv(far))
    sum_u = y_sum([hold(v, inside) for v in chips_u])
    line.mark(g_qkv)
    dn1_part = dot(line.tie(dqkv), w_qkv, ((1,), (1,))).astype(BF)
    line.mark(dn1_part)
    next_hop(qkv_home, lambda s: hold(of_qkv(s), sum_u))
    chips_n1 = chip_sums(lambda r: dn1_part[r * T : (r + 1) * T])
    dn1 = y_sum(chips_n1)
    line.mark(dn1_part)
    chips_d = grads([d_slots[i][0] for i in done], [done[i][3] for i in done])
    next_hop(qkv_home, of_qkv)
    sum_d = y_sum(chips_d)

    def arrived_sum(walk, own):
        return own.astype(F32) + walk.arrived[0].astype(F32) + walk.arrived[1].astype(F32)

    while qkv_home.near > 1:
        next_hop(qkv_home, lambda s: hold(of_qkv(s), sum_d))
    x32 = x.astype(F32)
    token_part, _ = norm_back(x32, gains[0], dn1)
    d_x = (dhidden + token_part)[None]
    g_gate_up = jnp.concatenate([sum_g, sum_u], axis=1)
    g_down = sum_d
    while mixed.near > 1:
        pump()
    output = (hidden + terms[0][0] + mixed.arrived[0].astype(F32) + mixed.arrived[1].astype(F32)).astype(BF)[None]

    dense_mine = arrived_sum(qkv_home, of_qkv(0))
    g_qkv_mine = dense_mine[:rows_e]
    own_gain = norm_gains[:, 0].astype(F32)
    d_gain0 = jnp.sum(w_qkv_mine.astype(F32) * g_qkv_mine, axis=1) / own_gain
    gain_rows = -(-rows_e // (3 * cols_c * 16)) * 16
    d_gain0 = jnp.pad(d_gain0, (0, gain_rows * 3 * cols_c - rows_e)).reshape(gain_rows, 3 * cols_c)
    pieces = ctx_gather(jnp.concatenate([dense_mine, d_gain0], axis=0).astype(BF))
    g_query, g_key, g_value = columns(others, pieces, rows_e, cols_c)
    last = dense_mine.shape[0]
    out_pieces = [p[rows_e:last].reshape(-1, cols_c) for p in pieces]
    [g_output] = columns(others, out_pieces, rows_e, cols_c)
    g_small = sum(p[rows_e:].astype(F32) for p in out_pieces).reshape(-1)[: count * rows_e].reshape(count, rows_e)
    d_gain0 = sum(p[last:].astype(F32) for p in pieces).reshape(-1)[:rows_e]
    g_gains = jnp.concatenate([d_gain0[None], g_small[NE:]], axis=0).T
    return (output, d_x, g_query, g_key, g_value, g_output, g_small[:NE].T, g_gains, g_gate_up, g_down)


def solution(mesh):
    exp_walk = ring_order(mesh.shape["exp"])
    tokens = P("exp", "ctx", None)
    rows = P("exp", None)
    hidden_units = P("exp", None, "ctx")
    in_specs = (tokens, rows, tokens) + (rows,) * 6 + (hidden_units, hidden_units, tokens)
    out_specs = (tokens, tokens) + (rows,) * 6 + (hidden_units, hidden_units)
    return jax.shard_map(
        functools.partial(per_device, exp_walk),
        mesh=mesh,
        in_specs=in_specs,
        out_specs=out_specs,
        check_vma=False,
    )
```

time: 1720 us -> 1220 us (0.71)
  matrix products: 474 us -> 67 us
  Pallas kernels: 45.1 us -> 427 us
  waiting for transfers between devices: 612 us -> 231 us
  starting transfers between devices: 155 us -> 127 us
  other arithmetic: 181 us -> 159 us
    dot_general x52 -> x0, matrix products: 400 us -> none  [the longest x12 139 us: part(): jnp.einsum('jrd,jrf->jdf', rows, cols[..., r * shard:(r + 1) * shard], pr...]
    pallas_call x2 -> x27, Pallas kernels: 45.1 us -> 427 us  [the longest x10 136 us: combine(): pl.pallas_call(functools.partial(_combine_kernel, terms=len(factors), cou...]
    ppermute x53 -> x39, waiting for transfers between devices: 287 us -> 94.5 us  [go_right(): return lax.ppermute(v, self.axis, self.right)]
    psum x1 -> x0, waiting for transfers between devices: 104 us -> none  [per_device(): g_small = lax.psum(g_small, ('ctx', 'exp'))]
    ppermute x53 -> x28, waiting for transfers between devices: 219 us -> 137 us  [go_left(): return lax.ppermute(v, self.axis, self.left)]
    add x6 -> x34, other arithmetic: 0.03 us -> 59.4 us  [the longest x12 28.8 us: hop(): to_right, to_left = (to_right + left, to_left + right)]
    convert_element_type x22 -> x5, other arithmetic: 62.2 us -> 5.1 us  [the longest x1 4.12 us: per_device(): dhidden_low = dhidden.astype(BF)]
    ppermute x53 -> x39, starting transfers between devices: 61.5 us -> 24.3 us  [go_right(): return lax.ppermute(v, self.axis, self.right)]
  transfers between devices with their start and end apart: 135 -> 92, of which waited for: 54 -> 25; matrix products, arithmetic and copies ran while one was open for 32% -> 28% of each run, Pallas kernels for 3% -> 32%
where the time goes in v2:
time: 1220 us; the launch traced here: 1210 us
  Pallas kernels  427 us (35%)
  waiting for transfers between devices  231 us (19%)
  other arithmetic  159 us (13%)
  local copies, waits for them, and re-layouts  144 us (12%)
  starting transfers between devices  127 us (10%)
  matrix products  67 us (5%)
  between operations  32 us (3%)
  blocking collectives  25.7 us (2%)
    ppermute x28, waiting for transfers between devices, go_left(): return lax.ppermute(v, self.axis, self.left)  137 us
    pallas_call x10, Pallas kernels, combine(): pl.pallas_call(functools.partial(_combine_kernel, terms=len(factors), cou...  136 us
    ppermute x39, waiting for transfers between devices, go_right(): return lax.ppermute(v, self.axis, self.right)  94.5 us
    pallas_call x5, Pallas kernels, expert(): pl.pallas_call(functools.partial(_expert_kernel, count=n, cap=cap, expert...  85.5 us
    pallas_call x3, Pallas kernels, wgrad(): pl.pallas_call(functools.partial(_wgrad_kernel, count=n, pieces=pieces),...  83.4 us
    dot_general x11, matrix products, dot(): return lax.dot_general(a, b, (dims, ((), ())), preferred_element_type=F32)  67 us
    pallas_call x5, Pallas kernels, dispatch(): pl.pallas_call(functools.partial(_dispatch_kernel, count=n, cap=cap), gri...  53.4 us
    ppermute x22, starting transfers between devices, swap(): return lax.ppermute(v, 'ctx', sibling)  48.5 us
  transfers between devices with their start and end apart: 92, of which 25 were waited for; matrix products, arithmetic and copies ran while one was open for 28% of the time, Pallas kernels for 32%

profile of v2, /device:TPU:1, one launch (start us, length us, event | category | flops | bytes accessed | tf_op | source)
XLA Modules:
  0.0 1213.6 jit_solution(3697690925478954445)
XLA Ops:
  82.3 16.5 %collective-permute-done.19 = bf16[2,2048,256]{2,1,0:T(8,128)(2,1)S(1)} collective-permute-done((bf16[2,2048,256]{2,1,0:T(8,128)(2,1)}, bf16[2,2048,256]{2,1,0:T(8,128)(2,1)S(1)}, u32[]{:S(2)}, u32[]{:S(2)}) %collective-permute-start.19) | collective-permute-done | bytes 2097184 | tf_op jit(solution)/shard_map/ppermute | solution.py:54
  146.2 16.0 %fusion.13.qp.kp.vp = f32[1536,1536]{1,0:T(8,128)S(1)} fusion(bf16[2048,1536]{1,0:T(8,128)(2,1)} %bitcast.33, f32[2048]{0:T(1024)S(1)} %bitcast.231, f32[1536]{0:T(1024)S(1)} %add_rsqrt_fusion, bf16[384,2048]{1,0:T(8,128)(2,1)} %collective-permute-done.2, bf16[384,2048]{1,0:T(8,128)(2,1)} %collective-permute-done.1, ...), kind=kOutput, calls=%fused_computation.57 | convolution fusion | flops 9698279424 | bytes 22034432 | tf_op jit(solution)/shard_map/dot_general | solution.py:22
  186.5 15.4 %psum.14 = f32[4,2,384]{2,1,0:T(2,128)S(1)} all-reduce(f32[4,2,384]{2,1,0:T(2,128)S(1)} %constant_dynamic-update-slice_fusion.19), channel_id=1, replica_groups=mesh['ctx'=4,'exp'=8] {'ctx'}, use_global_device_ids=true, to_apply=%region_4.5 | all-reduce | flops 3072 | bytes 24576 | tf_op jit(solution)/shard_map/psum | solution.py:561
  209.3 23.5 %attend.1 = (bf16[1536,512]{1,0:T(8,128)(2,1)}, bf16[1536,512]{1,0:T(8,128)(2,1)}, bf16[1536,512]{1,0:T(8,128)(2,1)}, bf16[1536,512]{1,0:T(8,128)(2,1)}, f32[4,1536,1]{2,1,0:T(8,128)}) custom-call(s32[8]{0:T(128)} %select_reduce_fusion.place, f32[1536,1536]{1,0:T(8,128)} %copy-done.2, f32[1536,1536]{1,0:T(8,128)} %copy-done.2, f32[1536,1536]{1,0:T(8,128)} %copy-done.2, ...), custom_call_target="tpu_custom_call" | custom-call | flops 4831838208 | bytes 15728640 | tf_op jit(solution)/shard_map/attend/pallas_call | solution.py:227
  264.8 23.0 %collective-permute-done.42.refs_2_ = bf16[384,2048]{1,0:T(8,128)(2,1)} collective-permute-done((bf16[384,2048]{1,0:T(8,128)(2,1)}, bf16[384,2048]{1,0:T(8,128)(2,1)}, u32[]{:S(2)}, u32[]{:S(2)}) %collective-permute-start.42) | collective-permute-done | bytes 1572896 | tf_op jit(solution)/shard_map/ppermute | solution.py:57
  290.4 13.4 %collective-permute-start.44 = (bf16[384,2048]{1,0:T(8,128)(2,1)}, bf16[384,2048]{1,0:T(8,128)(2,1)}, u32[]{:S(2)}, u32[]{:S(2)}) collective-permute-start(bf16[384,2048]{1,0:T(8,128)(2,1)} %broadcast_add_fusion), channel_id=1, source_target_pairs={{1,0},{3,1},{5,3},{7,5},{6,7},{4,6},{2,4},{0,2},{9,8},{11,9},{13,1... | collective-permute-start | bytes 4718600 | tf_op jit(solution)/shard_map/ppermute | solution.py:57
  324.6 13.4 %collective-permute-done.44.refs_2_ = bf16[384,2048]{1,0:T(8,128)(2,1)} collective-permute-done((bf16[384,2048]{1,0:T(8,128)(2,1)}, bf16[384,2048]{1,0:T(8,128)(2,1)}, u32[]{:S(2)}, u32[]{:S(2)}) %collective-permute-start.44) | collective-permute-done | bytes 1572896 | tf_op jit(solution)/shard_map/ppermute | solution.py:57
  361.0 13.9 %maximum_maximum_fusion.refs_1_.refs_2_.refs_3_.refs_5_ = bf16[2,4096,1024]{2,1,0:T(8,128)(2,1)} fusion(bf16[1,4096,256]{2,1,0:T(8,128)(2,1)} %collective-permute-done.40, bf16[1,4096,256]{2,1,0:T(8,128)(2,1)} %collective-permute-done.24, bf16[1,4096,256]{2,1,0:T(8,128)(2,1)} %collective-permute-done.39, bf16[1,4096,256]{2,1,0:T(8,128)(2,1)} %slice_add_fusion.1, ...), kind=kLoop, calls=%fused_computation | loop fusion | flops 134217728 | bytes 33554432 | tf_op jit(solution)/shard_map/concatenate | solution.py:675
  374.9 13.4 %expert.5 = (bf16[2,240,2048]{2,1,0:T(8,128)(2,1)}, bf16[2,240,1024]{2,1,0:T(8,128)(2,1)}, bf16[2,240,1024]{2,1,0:T(8,128)(2,1)}, bf16[2,240,1024]{2,1,0:T(8,128)(2,1)}, f32[2,240,1]{2,1,0:T(8,128)}) custom-call(s32[1]{0:T(128)} %bitcast.51.first.refs_0_, s32[8,2,1,384]{3,2,1,0:T(1,128)} %broadcast_in_dim_reshape.13.refs_0_.slot, ...), custom_call_target="tpu_custom_call" | custom-call | flops 4781506560 | bytes 24248320 | tf_op jit(solution)/shard_map/expert/pallas_call | solution.py:359
  415.5 19.6 %expert.6 = (bf16[2,480,2048]{2,1,0:T(8,128)(2,1)}, bf16[2,480,1024]{2,1,0:T(8,128)(2,1)}, bf16[2,480,1024]{2,1,0:T(8,128)(2,1)}, bf16[2,480,1024]{2,1,0:T(8,128)(2,1)}, f32[2,480,1]{2,1,0:T(8,128)}) custom-call(s32[1]{0:T(128)} %bitcast.51.first.refs_0_, s32[8,2,1,384]{3,2,1,0:T(1,128)} %broadcast_in_dim_reshape.13.refs_0_.slot, ...), custom_call_target="tpu_custom_call" | custom-call | flops 9563013120 | bytes 31719424 | tf_op jit(solution)/shard_map/expert/pallas_call | solution.py:359
  461.1 19.5 %expert.7 = (bf16[2,480,2048]{2,1,0:T(8,128)(2,1)}, bf16[2,480,1024]{2,1,0:T(8,128)(2,1)}, bf16[2,480,1024]{2,1,0:T(8,128)(2,1)}, bf16[2,480,1024]{2,1,0:T(8,128)(2,1)}, f32[2,480,1]{2,1,0:T(8,128)}) custom-call(s32[1]{0:T(128)} %bitcast.51.first.refs_0_, s32[8,2,1,384]{3,2,1,0:T(1,128)} %broadcast_in_dim_reshape.13.refs_0_.slot, ...), custom_call_target="tpu_custom_call" | custom-call | flops 9563013120 | bytes 31719424 | tf_op jit(solution)/shard_map/expert/pallas_call | solution.py:359
  491.4 19.6 %expert.8 = (bf16[2,480,2048]{2,1,0:T(8,128)(2,1)}, bf16[2,480,1024]{2,1,0:T(8,128)(2,1)}, bf16[2,480,1024]{2,1,0:T(8,128)(2,1)}, bf16[2,480,1024]{2,1,0:T(8,128)(2,1)}, f32[2,480,1]{2,1,0:T(8,128)}) custom-call(s32[1]{0:T(128)} %bitcast.51.first.refs_0_, s32[8,2,1,384]{3,2,1,0:T(1,128)} %broadcast_in_dim_reshape.13.refs_0_.slot, ...), custom_call_target="tpu_custom_call" | custom-call | flops 9563013120 | bytes 31719424 | tf_op jit(solution)/shard_map/expert/pallas_call | solution.py:359
  544.9 19.0 %combine.11 = (bf16[384,2176]{1,0:T(8,128)(2,1)}, bf16[384,2176]{1,0:T(8,128)(2,1)}) custom-call(s32[1]{0:T(128)} %bitcast.51.first.refs_0_, s32[8,2,384,1]{3,2,1,0:T(8,128)} %copy.179.refs_1_, bf16[2,480,1024]{2,1,0:T(8,128)(2,1)} %get-tuple-element.137.refs_2_.refs_8_, bf16[2,4096,1024]{2,1,0:T(8,128)(2,1)} %maximum_maximum_fusion.refs_1_.refs_2_.refs_3_.refs_5_, ...), custom_call_target="tpu_custom_call" | custom-call | flops 9563013120 | bytes 27000832 | tf_op jit(solution)/shard_map/combine/pallas_call | solution.py:453
  573.2 19.0 %combine.12 = (bf16[384,2176]{1,0:T(8,128)(2,1)}, bf16[384,2176]{1,0:T(8,128)(2,1)}) custom-call(s32[1]{0:T(128)} %bitcast.51.first.refs_0_, s32[8,2,384,1]{3,2,1,0:T(8,128)} %copy.180.refs_1_, bf16[2,480,1024]{2,1,0:T(8,128)(2,1)} %get-tuple-element.133.refs_2_.refs_7_, bf16[2,4096,1024]{2,1,0:T(8,128)(2,1)} %maximum_maximum_fusion.refs_1_.refs_2_.refs_3_.refs_5_, ...), custom_call_target="tpu_custom_call" | custom-call | flops 9563013120 | bytes 27000832 | tf_op jit(solution)/shard_map/combine/pallas_call | solution.py:453
  611.7 19.0 %combine.13 = (bf16[384,2176]{1,0:T(8,128)(2,1)}, bf16[384,2176]{1,0:T(8,128)(2,1)}) custom-call(s32[1]{0:T(128)} %bitcast.51.first.refs_0_, s32[8,2,384,1]{3,2,1,0:T(8,128)} %copy.181.refs_1_, bf16[2,480,1024]{2,1,0:T(8,128)(2,1)} %get-tuple-element.129.refs_2_.refs_6_, bf16[2,4096,1024]{2,1,0:T(8,128)(2,1)} %maximum_maximum_fusion.refs_1_.refs_2_.refs_3_.refs_5_, ...), custom_call_target="tpu_custom_call" | custom-call | flops 9563013120 | bytes 27000832 | tf_op jit(solution)/shard_map/combine/pallas_call | solution.py:453
  666.6 27.7 %wgrad.4 = (bf16[2,2048,256]{2,1,0:T(8,128)(2,1)}, bf16[2,2048,256]{2,1,0:T(8,128)(2,1)}, bf16[2,2048,256]{2,1,0:T(8,128)(2,1)}, bf16[2,2048,256]{2,1,0:T(8,128)(2,1)}) custom-call(s32[1]{0:T(128)} %bitcast.55._, bf16[2,240,2048]{2,1,0:T(8,128)(2,1)} %get-tuple-element.165.refs_0_, bf16[2,480,2048]{2,1,0:T(8,128)(2,1)} %get-tuple-element.166.refs_1_, ...), custom_call_target="tpu_custom_call" | custom-call | flops 16106127360 | bytes 31981568 | tf_op jit(solution)/shard_map/wgrad/pallas_call | solution.py:484
  738.7 27.7 %wgrad.3 = (bf16[2,2048,256]{2,1,0:T(8,128)(2,1)}, bf16[2,2048,256]{2,1,0:T(8,128)(2,1)}, bf16[2,2048,256]{2,1,0:T(8,128)(2,1)}, bf16[2,2048,256]{2,1,0:T(8,128)(2,1)}) custom-call(s32[1]{0:T(128)} %bitcast.54._, bf16[2,240,2048]{2,1,0:T(8,128)(2,1)} %get-tuple-element.165.refs_0_, bf16[2,480,2048]{2,1,0:T(8,128)(2,1)} %get-tuple-element.166.refs_1_, ...), custom_call_target="tpu_custom_call" | custom-call | flops 16106127360 | bytes 31981568 | tf_op jit(solution)/shard_map/wgrad/pallas_call | solution.py:484
  853.9 36.0 %attend_back.1 = (f32[1536,512]{1,0:T(8,128)}, f32[1536,512]{1,0:T(8,128)}, bf16[1536,512]{1,0:T(8,128)(2,1)}, f32[1536,8]{1,0:T(8,128)}, f32[2,512]{1,0:T(2,128)}) custom-call(s32[8]{0:T(128)} %select_reduce_fusion.place, bf16[1536,512]{1,0:T(8,128)(2,1)} %get-tuple-element.187.q_s, bf16[1536,512]{1,0:T(8,128)(2,1)} %get-tuple-element.188.k_s, ...), custom_call_target="tpu_custom_call" | custom-call | flops 12079595520 | bytes 22020096 | tf_op jit(solution)/shard_map/attend_back/pallas_call | solution.py:247
  928.0 14.4 %convolution_convert_fusion.1 = bf16[2048,1536]{1,0:T(8,128)(2,1)} fusion(f32[2048]{0:T(1024)S(1)} %bitcast.232, f32[1536]{0:T(1024)S(1)} %copy-done.84, bf16[1536,512]{1,0:T(8,128)(2,1)S(1)} %copy-done.52, bf16[1536,512]{1,0:T(8,128)(2,1)S(1)} %get-tuple-element.233, bf16[1536,512]{1,0:T(8,128)(2,1)S(1)} %get-tuple-element.232, ...), kind=kOutput, calls=%fused_computation.8 | convolution fusion | flops 9715580928 | bytes 17315840 | tf_op jit(solution)/shard_map/dot_general | solution.py:22
  942.5 13.5 %convolution_convert_fusion = bf16[1536,2048]{1,0:T(8,128)(2,1)S(1)} fusion(bf16[1536,1536]{1,0:T(8,128)(2,1)} %pad_maximum_fusion.3, bf16[2048,1536]{1,0:T(8,128)(2,1)} %bitcast.33), kind=kOutput, calls=%fused_computation.7 | convolution fusion | flops 9666822144 | bytes 17301504 | tf_op jit(solution)/shard_map/dot_general | solution.py:22
  959.8 28.0 %wgrad.5 = (bf16[2,2048,256]{2,1,0:T(8,128)(2,1)}, bf16[2,2048,256]{2,1,0:T(8,128)(2,1)}, bf16[2,2048,256]{2,1,0:T(8,128)(2,1)}, bf16[2,2048,256]{2,1,0:T(8,128)(2,1)}) custom-call(s32[1]{0:T(128)} %bitcast.79._, bf16[2,240,2048]{2,1,0:T(8,128)(2,1)} %get-tuple-element.201.refs_0_, bf16[2,480,2048]{2,1,0:T(8,128)(2,1)} %get-tuple-element.202.refs_1_, ...), custom_call_target="tpu_custom_call" | custom-call | flops 16106127360 | bytes 31981568 | tf_op jit(solution)/shard_map/wgrad/pallas_call | solution.py:484
  1010.2 30.8 %collective-permute-done.77 = bf16[2,2048,256]{2,1,0:T(8,128)(2,1)S(1)} collective-permute-done((bf16[2,2048,256]{2,1,0:T(8,128)(2,1)S(1)}, bf16[2,2048,256]{2,1,0:T(8,128)(2,1)S(1)}, u32[]{:S(2)}, u32[]{:S(2)}) %collective-permute-start.77) | collective-permute-done | bytes 2097184 | tf_op jit(solution)/shard_map/ppermute | solution.py:54
  1051.9 19.1 %collective-permute-done.83 = bf16[352,1536]{1,0:T(8,128)(2,1)S(1)} collective-permute-done((bf16[352,1536]{1,0:T(8,128)(2,1)S(1)}, bf16[352,1536]{1,0:T(8,128)(2,1)S(1)}, u32[]{:S(2)}, u32[]{:S(2)}) %collective-permute-start.83) | collective-permute-done | bytes 1081376 | tf_op jit(solution)/shard_map/ppermute | solution.py:57
  1124.7 27.6 %collective-permute-done.62 = bf16[384,2048]{1,0:T(8,128)(2,1)} collective-permute-done((bf16[384,2048]{1,0:T(8,128)(2,1)}, bf16[384,2048]{1,0:T(8,128)(2,1)}, u32[]{:S(2)}, u32[]{:S(2)}) %collective-permute-start.62) | collective-permute-done | bytes 1572896 | tf_op jit(solution)/shard_map/ppermute | solution.py:57
  (639 shorter events, 692.5 us)
Async XLA Ops:
  7.2 159.2 %all-gather.2.cloned.1.call-start = ((), (), s32[]{:S(2)}) async-start(), calls=%async_computation.2 | async-start | bytes 2359296 | tf_op jit(solution)/shard_map/all_gather | solution.py:625
  47.2 94.9 %collective-permute-start = (bf16[384,2048]{1,0:T(8,128)(2,1)S(1)}, bf16[384,2048]{1,0:T(8,128)(2,1)}, u32[]{:S(2)}, u32[]{:S(2)}) collective-permute-start(bf16[384,2048]{1,0:T(8,128)(2,1)S(1)} %bitcast.204), channel_id=1, source_target_pairs={{0,8},{8,0},{16,24},{24,16},{1,9},{9,1},{17,25},{25,17},{2,10},{10... | collective-permute-start | bytes 4718600 | tf_op jit(solution)/shard_map/ppermute | solution.py:541
  108.6 75.4 %collective-permute-start.20 = (bf16[1,4096,256]{2,1,0:T(8,128)(2,1)}, bf16[1,4096,256]{2,1,0:T(8,128)(2,1)}, u32[]{:S(2)}, u32[]{:S(2)}) collective-permute-start(bf16[1,4096,256]{2,1,0:T(8,128)(2,1)} %slice_add_fusion.2), channel_id=1, source_target_pairs={{0,16},{16,0},{8,24},{24,8},{1,17},{17,1},{9,25},{25,9},{2,18},{18... | collective-permute-start | bytes 6291464 | tf_op jit(solution)/shard_map/ppermute | solution.py:54
  133.2 115.6 %collective-permute-start.28 = (bf16[384,2048]{1,0:T(8,128)(2,1)}, bf16[384,2048]{1,0:T(8,128)(2,1)}, u32[]{:S(2)}, u32[]{:S(2)}) collective-permute-start(bf16[384,2048]{1,0:T(8,128)(2,1)} %bitcast.35.refs_1_), channel_id=1, source_target_pairs={{1,0},{3,1},{5,3},{7,5},{6,7},{4,6},{2,4},{0,2},{9,8},{11,9},{13,1... | collective-permute-start | bytes 4718600 | tf_op jit(solution)/shard_map/ppermute | solution.py:57
  142.0 112.5 %collective-permute-start.27 = (bf16[384,2048]{1,0:T(8,128)(2,1)}, bf16[384,2048]{1,0:T(8,128)(2,1)}, u32[]{:S(2)}, u32[]{:S(2)}) collective-permute-start(bf16[384,2048]{1,0:T(8,128)(2,1)} %bitcast.35.refs_1_), channel_id=1, source_target_pairs={{0,1},{1,3},{3,5},{5,7},{7,6},{6,4},{4,2},{2,0},{8,9},{9,11},{11,1... | collective-permute-start | bytes 4718600 | tf_op jit(solution)/shard_map/ppermute | solution.py:54
  166.4 66.5 %all-to-all-start = ((bf16[4,512,512]{2,1,0:T(8,128)(2,1)}), bf16[4,512,512]{2,1,0:T(8,128)(2,1)}, u32[]{:S(2)}, u32[]{:S(2)}) async-start(bf16[4,512,512]{2,1,0:T(8,128)(2,1)} %bitcast.217), calls=%async_computation | async-start | bytes 4194304 | tf_op jit(solution)/shard_map/all_to_all | solution.py:626
  253.8 105.4 %collective-permute-start.37 = (bf16[1,4096,256]{2,1,0:T(8,128)(2,1)}, bf16[1,4096,256]{2,1,0:T(8,128)(2,1)}, u32[]{:S(2)}, u32[]{:S(2)}) collective-permute-start(bf16[1,4096,256]{2,1,0:T(8,128)(2,1)} %slice_add_fusion.2), channel_id=1, source_target_pairs={{0,8},{8,0},{16,24},{24,16},{1,9},{9,1},{17,25},{25,17},{2,10},{10... | collective-permute-start | bytes 6291464 | tf_op jit(solution)/shard_map/ppermute | solution.py:541
  257.4 60.8 %collective-permute-start.41 = (bf16[384,2048]{1,0:T(8,128)(2,1)}, bf16[384,2048]{1,0:T(8,128)(2,1)S(1)}, u32[]{:S(2)}, u32[]{:S(2)}) collective-permute-start(bf16[384,2048]{1,0:T(8,128)(2,1)} %broadcast_add_fusion.3), channel_id=1, source_target_pairs={{0,1},{1,3},{3,5},{5,7},{7,6},{6,4},{4,2},{2,0},{8,9},{9,11},{11,1... | collective-permute-start | bytes 4718600 | tf_op jit(solution)/shard_map/ppermute | solution.py:54
  259.7 61.0 %collective-permute-start.23 = (bf16[384,2048]{1,0:T(8,128)(2,1)S(1)}, bf16[384,2048]{1,0:T(8,128)(2,1)}, u32[]{:S(2)}, u32[]{:S(2)}) collective-permute-start(bf16[384,2048]{1,0:T(8,128)(2,1)S(1)} %copy-done.58), channel_id=1, source_target_pairs={{0,8},{8,0},{16,24},{24,16},{1,9},{9,1},{17,25},{25,17},{2,10},{10... | collective-permute-start | bytes 4718600 | tf_op jit(solution)/shard_map/ppermute | solution.py:541
  645.4 65.5 %collective-permute-start.54 = (bf16[384,2176]{1,0:T(8,128)(2,1)}, bf16[384,2176]{1,0:T(8,128)(2,1)S(1)}, u32[]{:S(2)}, u32[]{:S(2)}) collective-permute-start(bf16[384,2176]{1,0:T(8,128)(2,1)} %add.421), channel_id=1, source_target_pairs={{1,0},{3,1},{5,3},{7,5},{6,7},{4,6},{2,4},{0,2},{9,8},{11,9},{13,1... | collective-permute-start | bytes 5013512 | tf_op jit(solution)/shard_map/ppermute | solution.py:57
  648.7 62.2 %collective-permute-start.53 = (bf16[384,2176]{1,0:T(8,128)(2,1)}, bf16[384,2176]{1,0:T(8,128)(2,1)}, u32[]{:S(2)}, u32[]{:S(2)}) collective-permute-start(bf16[384,2176]{1,0:T(8,128)(2,1)} %add.419), channel_id=1, source_target_pairs={{0,1},{1,3},{3,5},{5,7},{7,6},{6,4},{4,2},{2,0},{8,9},{9,11},{11,1... | collective-permute-start | bytes 5013512 | tf_op jit(solution)/shard_map/ppermute | solution.py:54
  694.3 124.6 %collective-permute-start.67 = (bf16[2,2048,256]{2,1,0:T(8,128)(2,1)}, bf16[2,2048,256]{2,1,0:T(8,128)(2,1)}, u32[]{:S(2)}, u32[]{:S(2)}) collective-permute-start(bf16[2,2048,256]{2,1,0:T(8,128)(2,1)} %get-tuple-element.197), channel_id=1, source_target_pairs={{0,8},{8,0},{16,24},{24,16},{1,9},{9,1},{17,25},{25,17},{2,10},{10... | collective-permute-start | bytes 6291464 | tf_op jit(solution)/shard_map/ppermute | solution.py:541
  718.9 70.6 %collective-permute-start.64 = (bf16[384,2048]{1,0:T(8,128)(2,1)S(1)}, bf16[384,2048]{1,0:T(8,128)(2,1)}, u32[]{:S(2)}, u32[]{:S(2)}) collective-permute-start(bf16[384,2048]{1,0:T(8,128)(2,1)S(1)} %get-tuple-element.228), channel_id=1, source_target_pairs={{0,16},{16,0},{8,24},{24,8},{1,17},{17,1},{9,25},{25,9},{2,18},{18... | collective-permute-start | bytes 4718600 | tf_op jit(solution)/shard_map/ppermute | solution.py:54
  719.0 112.0 %collective-permute-start.63 = (bf16[384,2048]{1,0:T(8,128)(2,1)S(1)}, bf16[384,2048]{1,0:T(8,128)(2,1)}, u32[]{:S(2)}, u32[]{:S(2)}) collective-permute-start(bf16[384,2048]{1,0:T(8,128)(2,1)S(1)} %get-tuple-element.228), channel_id=1, source_target_pairs={{0,8},{8,0},{16,24},{24,16},{1,9},{9,1},{17,25},{25,17},{2,10},{10... | collective-permute-start | bytes 4718600 | tf_op jit(solution)/shard_map/ppermute | solution.py:541
  818.9 72.0 %collective-permute-start.66 = (bf16[2,2048,256]{2,1,0:T(8,128)(2,1)}, bf16[2,2048,256]{2,1,0:T(8,128)(2,1)}, u32[]{:S(2)}, u32[]{:S(2)}) collective-permute-start(bf16[2,2048,256]{2,1,0:T(8,128)(2,1)} %get-tuple-element.195), channel_id=1, source_target_pairs={{0,8},{8,0},{16,24},{24,16},{1,9},{9,1},{17,25},{25,17},{2,10},{10... | collective-permute-start | bytes 6291464 | tf_op jit(solution)/shard_map/ppermute | solution.py:541
  822.7 186.4 %collective-permute-start.75 = (bf16[2,2048,256]{2,1,0:T(8,128)(2,1)}, bf16[2,2048,256]{2,1,0:T(8,128)(2,1)}, u32[]{:S(2)}, u32[]{:S(2)}) collective-permute-start(bf16[2,2048,256]{2,1,0:T(8,128)(2,1)} %get-tuple-element.210), channel_id=1, source_target_pairs={{0,8},{8,0},{16,24},{24,16},{1,9},{9,1},{17,25},{25,17},{2,10},{10... | collective-permute-start | bytes 6291464 | tf_op jit(solution)/shard_map/ppermute | solution.py:541
  826.4 64.6 %collective-permute-start.68 = (bf16[2,2048,256]{2,1,0:T(8,128)(2,1)}, bf16[2,2048,256]{2,1,0:T(8,128)(2,1)}, u32[]{:S(2)}, u32[]{:S(2)}) collective-permute-start(bf16[2,2048,256]{2,1,0:T(8,128)(2,1)} %add_convert_fusion.2), channel_id=1, source_target_pairs={{0,16},{16,0},{8,24},{24,8},{1,17},{17,1},{9,25},{25,9},{2,18},{18... | collective-permute-start | bytes 6291464 | tf_op jit(solution)/shard_map/ppermute | solution.py:54
  831.0 66.3 %collective-permute-start.61 = (bf16[384,2048]{1,0:T(8,128)(2,1)}, bf16[384,2048]{1,0:T(8,128)(2,1)}, u32[]{:S(2)}, u32[]{:S(2)}) collective-permute-start(bf16[384,2048]{1,0:T(8,128)(2,1)} %add.433), channel_id=1, source_target_pairs={{1,0},{3,1},{5,3},{7,5},{6,7},{4,6},{2,4},{0,2},{9,8},{11,9},{13,1... | collective-permute-start | bytes 4718600 | tf_op jit(solution)/shard_map/ppermute | solution.py:57
  831.6 65.8 %collective-permute-start.57 = (bf16[384,2048]{1,0:T(8,128)(2,1)}, bf16[384,2048]{1,0:T(8,128)(2,1)}, u32[]{:S(2)}, u32[]{:S(2)}) collective-permute-start(bf16[384,2048]{1,0:T(8,128)(2,1)} %add.429), channel_id=1, source_target_pairs={{0,1},{1,3},{3,5},{5,7},{7,6},{6,4},{4,2},{2,0},{8,9},{9,11},{11,1... | collective-permute-start | bytes 4718600 | tf_op jit(solution)/shard_map/ppermute | solution.py:54
  890.9 100.4 %collective-permute-start.76 = (bf16[2,2048,256]{2,1,0:T(8,128)(2,1)}, bf16[2,2048,256]{2,1,0:T(8,128)(2,1)}, u32[]{:S(2)}, u32[]{:S(2)}) collective-permute-start(bf16[2,2048,256]{2,1,0:T(8,128)(2,1)} %get-tuple-element.212), channel_id=1, source_target_pairs={{0,8},{8,0},{16,24},{24,16},{1,9},{9,1},{17,25},{25,17},{2,10},{10... | collective-permute-start | bytes 6291464 | tf_op jit(solution)/shard_map/ppermute | solution.py:541
  1008.0 65.0 %collective-permute-start.72 = (bf16[2,2048,256]{2,1,0:T(8,128)(2,1)}, bf16[2,2048,256]{2,1,0:T(8,128)(2,1)S(1)}, u32[]{:S(2)}, u32[]{:S(2)}) collective-permute-start(bf16[2,2048,256]{2,1,0:T(8,128)(2,1)} %get-tuple-element.207), channel_id=1, source_target_pairs={{0,8},{8,0},{16,24},{24,16},{1,9},{9,1},{17,25},{25,17},{2,10},{10... | collective-permute-start | bytes 6291464 | tf_op jit(solution)/shard_map/ppermute | solution.py:541
  1009.1 77.0 %collective-permute-start.74 = (bf16[2,2048,256]{2,1,0:T(8,128)(2,1)S(1)}, bf16[2,2048,256]{2,1,0:T(8,128)(2,1)S(1)}, u32[]{:S(2)}, u32[]{:S(2)}) collective-permute-start(bf16[2,2048,256]{2,1,0:T(8,128)(2,1)S(1)} %add_convert_fusion.1), channel_id=1, source_target_pairs={{0,16},{16,0},{8,24},{24,8},{1,17},{17,1},{9,25},{25,9},{2,18},{18... | collective-permute-start | bytes 6291464 | tf_op jit(solution)/shard_map/ppermute | solution.py:54
  1107.4 72.5 %collective-permute-start.69 = (bf16[384,2048]{1,0:T(8,128)(2,1)}, bf16[384,2048]{1,0:T(8,128)(2,1)}, u32[]{:S(2)}, u32[]{:S(2)}) collective-permute-start(bf16[384,2048]{1,0:T(8,128)(2,1)} %get-tuple-element.242), channel_id=1, source_target_pairs={{0,8},{8,0},{16,24},{24,16},{1,9},{9,1},{17,25},{25,17},{2,10},{10... | collective-permute-start | bytes 4718600 | tf_op jit(solution)/shard_map/ppermute | solution.py:541
  1118.6 61.4 %collective-permute-start.71 = (bf16[384,2048]{1,0:T(8,128)(2,1)}, bf16[384,2048]{1,0:T(8,128)(2,1)}, u32[]{:S(2)}, u32[]{:S(2)}) collective-permute-start(bf16[384,2048]{1,0:T(8,128)(2,1)} %add_convert_fusion.3), channel_id=1, source_target_pairs={{0,16},{16,0},{8,24},{24,8},{1,17},{17,1},{9,25},{25,9},{2,18},{18... | collective-permute-start | bytes 4718600 | tf_op jit(solution)/shard_map/ppermute | solution.py:54
  (158 other events, 3246.0 us)
Sparse Core Ops, SparseCore 0:
  19.6 60.7 all-gather.1

commit v3 on v2

--- a/solution.py
+++ b/solution.py
@@ -95,6 +95,7 @@
         else:
             to_right, to_left = to_right + left, to_left + right
         self.near -= 1
+        self.sent = to_right, to_left
         self.arrived = self.ring.go_right(to_right), self.ring.go_left(to_left)
 
 
@@ -672,7 +673,7 @@
     d_walk.latest = [hold(v, scales) for v in d_walk.latest]
     d_walk.hop()
     gu_last = ctx_gather(hold(w_gate_up[J // 2 :], scales))
-    w_gu = jnp.concatenate([jnp.concatenate(b, axis=2) for b in (gu_first, gu_last)], axis=0)
+    w_gu = lax.optimization_barrier(jnp.concatenate([jnp.concatenate(b, axis=2) for b in (gu_first, gu_last)], axis=0))
     attn, q, k, v, lse = attend(place, qkv, r_q, r_k, cosine, sine, gain_q, gain_k, half)
     branch_part = dot(attn, w_out_rows, ((1,), (0,))).astype(BF)
     chips = chip_sums(lambda r: branch_part[r * T : (r + 1) * T])
@@ -682,7 +683,7 @@
         d_walk.hop()
     line.mark(branch_part)
     fetch(1)
-    branch = hold(branch, w_gu, d_slots[1][1])
+    branch = hold(branch, w_gu[-1:, -1:, -1:], d_slots[1][1])
     hidden = x.astype(F32) + branch
     n2 = (hidden * inv_rms(hidden) * gains[3]).astype(BF)
     router_own = jax.nn.softmax(dot(n2, router_full, ((1,), (0,))), axis=-1)
@@ -719,10 +720,10 @@
 
     far = E // 2
     n2_walk.hop()
-    d_walk.latest = [hold(v, n2_wide) for v in d_walk.latest]
-    d_walk.hop()
     line.mark(n2_wide)
     work(0)
+    d_walk.latest = [hold(v, done[0][1]) for v in d_walk.latest]
+    d_walk.hop()
     fetch(2)
     for g in range(1, far + 1):
         line.mark(*n2_walk.latest, line.last[0])
@@ -808,9 +809,9 @@
     next_hop(qkv_home, lambda s: hold(of_qkv(s), sum_u))
     chips_n1 = chip_sums(lambda r: dn1_part[r * T : (r + 1) * T])
     dn1 = y_sum(chips_n1)
-    line.mark(dn1_part)
+    next_hop(qkv_home, of_qkv)
+    line.mark(*qkv_home.sent, *mixed.arrived)
     chips_d = grads([d_slots[i][0] for i in done], [done[i][3] for i in done])
-    next_hop(qkv_home, of_qkv)
     sum_d = y_sum(chips_d)
 
     def arrived_sum(walk, own):

time: 1220 us -> 1170 us (0.959)
  waiting for transfers between devices: 231 us -> 206 us
  starting transfers between devices: 127 us -> 106 us
  other arithmetic: 159 us -> 145 us
    ppermute x28, waiting for transfers between devices: 137 us -> 70.4 us  [go_left(): return lax.ppermute(v, self.axis, self.left)]
    ppermute x39, waiting for transfers between devices: 94.5 us -> 133 us  [go_right(): return lax.ppermute(v, self.axis, self.right)]
    ppermute x22, starting transfers between devices: 48.5 us -> 35.8 us  [swap(): return lax.ppermute(v, 'ctx', sibling)]
  transfers between devices with their start and end apart: 92 -> 92, of which waited for: 25 -> 20; matrix products, arithmetic and copies ran while one was open for 28% -> 29% of each run, Pallas kernels for 32% -> 31%
where the time goes in v3:
time: 1170 us; the launch traced here: 1160 us
  Pallas kernels  427 us (36%)
  waiting for transfers between devices  206 us (18%)
  local copies, waits for them, and re-layouts  150 us (13%)
  other arithmetic  145 us (12%)
  starting transfers between devices  106 us (9%)
  matrix products  66.1 us (6%)
  between operations  33.9 us (3%)
  blocking collectives  27.7 us (2%)
    pallas_call x10, Pallas kernels, combine(): pl.pallas_call(functools.partial(_combine_kernel, terms=len(factors), cou...  136 us
    ppermute x39, waiting for transfers between devices, go_right(): return lax.ppermute(v, self.axis, self.right)  133 us
    pallas_call x5, Pallas kernels, expert(): pl.pallas_call(functools.partial(_expert_kernel, count=n, cap=cap, expert...  85.5 us
    pallas_call x3, Pallas kernels, wgrad(): pl.pallas_call(functools.partial(_wgrad_kernel, count=n, pieces=pieces),...  83.1 us
    ppermute x28, waiting for transfers between devices, go_left(): return lax.ppermute(v, self.axis, self.left)  70.4 us
    dot_general x11, matrix products, dot(): return lax.dot_general(a, b, (dims, ((), ())), preferred_element_type=F32)  66.1 us
    pallas_call x5, Pallas kernels, dispatch(): pl.pallas_call(functools.partial(_dispatch_kernel, count=n, cap=cap), gri...  52.9 us
    ppermute x28, starting transfers between devices, go_left(): return lax.ppermute(v, self.axis, self.left)  38.6 us
  transfers between devices with their start and end apart: 92, of which 20 were waited for; matrix products, arithmetic and copies ran while one was open for 29% of the time, Pallas kernels for 31%

profile of v3, /device:TPU:1, one launch (start us, length us, event | category | flops | bytes accessed | tf_op | source)
XLA Modules:
  0.0 1161.6 jit_solution(12789490873133494091)
XLA Ops:
  82.8 16.1 %collective-permute-done.19 = bf16[2,2048,256]{2,1,0:T(8,128)(2,1)S(1)} collective-permute-done((bf16[2,2048,256]{2,1,0:T(8,128)(2,1)}, bf16[2,2048,256]{2,1,0:T(8,128)(2,1)S(1)}, u32[]{:S(2)}, u32[]{:S(2)}) %collective-permute-start.19) | collective-permute-done | bytes 2097184 | tf_op jit(solution)/shard_map/ppermute | solution.py:54
  147.3 16.0 %fusion.13.qp.kp.vp = f32[1536,1536]{1,0:T(8,128)S(1)} fusion(bf16[2048,1536]{1,0:T(8,128)(2,1)} %bitcast.33, f32[2048]{0:T(1024)S(1)} %bitcast.228, f32[1536]{0:T(1024)S(1)} %add_rsqrt_fusion, bf16[384,2048]{1,0:T(8,128)(2,1)} %collective-permute-done.2, bf16[384,2048]{1,0:T(8,128)(2,1)} %collective-permute-done.1, ...), kind=kOutput, calls=%fused_computation.57 | convolution fusion | flops 9698279424 | bytes 22034432 | tf_op jit(solution)/shard_map/dot_general | solution.py:22
  187.6 16.7 %psum.14 = f32[4,2,384]{2,1,0:T(2,128)S(1)} all-reduce(f32[4,2,384]{2,1,0:T(2,128)S(1)} %constant_dynamic-update-slice_fusion.19), channel_id=1, replica_groups=mesh['ctx'=4,'exp'=8] {'ctx'}, use_global_device_ids=true, to_apply=%region_4.5 | all-reduce | flops 3072 | bytes 24576 | tf_op jit(solution)/shard_map/psum | solution.py:562
  221.2 23.5 %attend.1 = (bf16[1536,512]{1,0:T(8,128)(2,1)}, bf16[1536,512]{1,0:T(8,128)(2,1)}, bf16[1536,512]{1,0:T(8,128)(2,1)}, bf16[1536,512]{1,0:T(8,128)(2,1)}, f32[4,1536,1]{2,1,0:T(8,128)}) custom-call(s32[8]{0:T(128)} %select_reduce_fusion.place, f32[1536,1536]{1,0:T(8,128)} %copy-done.3, f32[1536,1536]{1,0:T(8,128)} %copy-done.3, f32[1536,1536]{1,0:T(8,128)} %copy-done.3, ...), custom_call_target="tpu_custom_call" | custom-call | flops 4831838208 | bytes 15728640 | tf_op jit(solution)/shard_map/attend/pallas_call | solution.py:228
  299.3 19.6 %collective-permute-done.26 = bf16[384,2048]{1,0:T(8,128)(2,1)S(1)} collective-permute-done((bf16[384,2048]{1,0:T(8,128)(2,1)S(1)}, bf16[384,2048]{1,0:T(8,128)(2,1)S(1)}, u32[]{:S(2)}, u32[]{:S(2)}) %collective-permute-start.26) | collective-permute-done | bytes 1572896 | tf_op jit(solution)/shard_map/ppermute | solution.py:54
  326.5 13.4 %expert.5 = (bf16[2,240,2048]{2,1,0:T(8,128)(2,1)}, bf16[2,240,1024]{2,1,0:T(8,128)(2,1)}, bf16[2,240,1024]{2,1,0:T(8,128)(2,1)}, bf16[2,240,1024]{2,1,0:T(8,128)(2,1)}, f32[2,240,1]{2,1,0:T(8,128)}) custom-call(s32[1]{0:T(128)} %bitcast.51.first.refs_0_, s32[8,2,1,384]{3,2,1,0:T(1,128)} %broadcast_in_dim_reshape.13.refs_0_.slot, ...), custom_call_target="tpu_custom_call" | custom-call | flops 4781506560 | bytes 24248320 | tf_op jit(solution)/shard_map/expert/pallas_call | solution.py:360
  345.8 15.7 %collective-permute-done.37.refs_1_ = bf16[384,2176]{1,0:T(8,128)(2,1)} collective-permute-done((bf16[384,2176]{1,0:T(8,128)(2,1)}, bf16[384,2176]{1,0:T(8,128)(2,1)}, u32[]{:S(2)}, u32[]{:S(2)}) %collective-permute-start.37) | collective-permute-done | bytes 1671200 | tf_op jit(solution)/shard_map/ppermute | solution.py:57
  382.1 19.6 %expert.6 = (bf16[2,480,2048]{2,1,0:T(8,128)(2,1)}, bf16[2,480,1024]{2,1,0:T(8,128)(2,1)}, bf16[2,480,1024]{2,1,0:T(8,128)(2,1)}, bf16[2,480,1024]{2,1,0:T(8,128)(2,1)}, f32[2,480,1]{2,1,0:T(8,128)}) custom-call(s32[1]{0:T(128)} %bitcast.51.first.refs_0_, s32[8,2,1,384]{3,2,1,0:T(1,128)} %broadcast_in_dim_reshape.13.refs_0_.slot, ...), custom_call_target="tpu_custom_call" | custom-call | flops 9563013120 | bytes 31719424 | tf_op jit(solution)/shard_map/expert/pallas_call | solution.py:360
  427.6 19.5 %expert.7 = (bf16[2,480,2048]{2,1,0:T(8,128)(2,1)}, bf16[2,480,1024]{2,1,0:T(8,128)(2,1)}, bf16[2,480,1024]{2,1,0:T(8,128)(2,1)}, bf16[2,480,1024]{2,1,0:T(8,128)(2,1)}, f32[2,480,1]{2,1,0:T(8,128)}) custom-call(s32[1]{0:T(128)} %bitcast.51.first.refs_0_, s32[8,2,1,384]{3,2,1,0:T(1,128)} %broadcast_in_dim_reshape.13.refs_0_.slot, ...), custom_call_target="tpu_custom_call" | custom-call | flops 9563013120 | bytes 31719424 | tf_op jit(solution)/shard_map/expert/pallas_call | solution.py:360
  458.0 19.6 %expert.8 = (bf16[2,480,2048]{2,1,0:T(8,128)(2,1)}, bf16[2,480,1024]{2,1,0:T(8,128)(2,1)}, bf16[2,480,1024]{2,1,0:T(8,128)(2,1)}, bf16[2,480,1024]{2,1,0:T(8,128)(2,1)}, f32[2,480,1]{2,1,0:T(8,128)}) custom-call(s32[1]{0:T(128)} %bitcast.51.first.refs_0_, s32[8,2,1,384]{3,2,1,0:T(1,128)} %broadcast_in_dim_reshape.13.refs_0_.slot, ...), custom_call_target="tpu_custom_call" | custom-call | flops 9563013120 | bytes 31719424 | tf_op jit(solution)/shard_map/expert/pallas_call | solution.py:360
  478.9 13.4 %expert.9 = (bf16[2,240,2048]{2,1,0:T(8,128)(2,1)}, bf16[2,240,1024]{2,1,0:T(8,128)(2,1)}, bf16[2,240,1024]{2,1,0:T(8,128)(2,1)}, bf16[2,240,1024]{2,1,0:T(8,128)(2,1)}, f32[2,240,1]{2,1,0:T(8,128)}) custom-call(s32[1]{0:T(128)} %bitcast.51.first.refs_0_, s32[8,2,1,384]{3,2,1,0:T(1,128)} %broadcast_in_dim_reshape.13.refs_0_.slot, ...), custom_call_target="tpu_custom_call" | custom-call | flops 4781506560 | bytes 24248320 | tf_op jit(solution)/shard_map/expert/pallas_call | solution.py:360
  511.6 19.0 %combine.11 = (bf16[384,2176]{1,0:T(8,128)(2,1)}, bf16[384,2176]{1,0:T(8,128)(2,1)}) custom-call(s32[1]{0:T(128)} %bitcast.51.first.refs_0_, s32[8,2,384,1]{3,2,1,0:T(8,128)} %copy.164.refs_1_, bf16[2,480,1024]{2,1,0:T(8,128)(2,1)} %get-tuple-element.137.refs_2_.refs_8_, bf16[2,4096,1024]{2,1,0:T(8,128)(2,1)} %copy-done.2, ...), custom_call_target="tpu_custom_call" | custom-call | flops 9563013120 | bytes 27000832 | tf_op jit(solution)/shard_map/combine/pallas_call | solution.py:454
  539.9 19.0 %combine.12 = (bf16[384,2176]{1,0:T(8,128)(2,1)}, bf16[384,2176]{1,0:T(8,128)(2,1)}) custom-call(s32[1]{0:T(128)} %bitcast.51.first.refs_0_, s32[8,2,384,1]{3,2,1,0:T(8,128)} %copy.165.refs_1_, bf16[2,480,1024]{2,1,0:T(8,128)(2,1)} %get-tuple-element.133.refs_2_.refs_7_, bf16[2,4096,1024]{2,1,0:T(8,128)(2,1)} %copy-done.2, ...), custom_call_target="tpu_custom_call" | custom-call | flops 9563013120 | bytes 27000832 | tf_op jit(solution)/shard_map/combine/pallas_call | solution.py:454
  577.4 19.3 %combine.13 = (bf16[384,2176]{1,0:T(8,128)(2,1)}, bf16[384,2176]{1,0:T(8,128)(2,1)}) custom-call(s32[1]{0:T(128)} %bitcast.51.first.refs_0_, s32[8,2,384,1]{3,2,1,0:T(8,128)} %copy.166.refs_1_, bf16[2,480,1024]{2,1,0:T(8,128)(2,1)} %get-tuple-element.129.refs_2_.refs_6_, bf16[2,4096,1024]{2,1,0:T(8,128)(2,1)} %copy-done.2, ...), custom_call_target="tpu_custom_call" | custom-call | flops 9563013120 | bytes 27000832 | tf_op jit(solution)/shard_map/combine/pallas_call | solution.py:454
  632.5 27.7 %wgrad.4 = (bf16[2,2048,256]{2,1,0:T(8,128)(2,1)}, bf16[2,2048,256]{2,1,0:T(8,128)(2,1)}, bf16[2,2048,256]{2,1,0:T(8,128)(2,1)}, bf16[2,2048,256]{2,1,0:T(8,128)(2,1)}) custom-call(s32[1]{0:T(128)} %bitcast.55._, bf16[2,240,2048]{2,1,0:T(8,128)(2,1)} %get-tuple-element.165.refs_0_, bf16[2,480,2048]{2,1,0:T(8,128)(2,1)} %get-tuple-element.166.refs_1_, ...), custom_call_target="tpu_custom_call" | custom-call | flops 16106127360 | bytes 31981568 | tf_op jit(solution)/shard_map/wgrad/pallas_call | solution.py:485
  689.3 12.7 %combine.15 = (bf16[384,2048]{1,0:T(8,128)(2,1)}, bf16[384,2048]{1,0:T(8,128)(2,1)}) custom-call(s32[8,2,384,1]{3,2,1,0:T(8,128)} %copy.168.refs_0_, bf16[2,480,1024]{2,1,0:T(8,128)(2,1)} %get-tuple-element.162.refs_1_.refs_8_, bf16[2,2048,1024]{2,1,0:T(8,128)(2,1)} %constant_dynamic-update-slice_fusion.11.refs_2_.refs_3_), custom_call_target="tpu_custom_call" | custom-call | flops 5536481280 | bytes 16646144 | tf_op jit(solution)/shard_map/combine/pallas_call | solution.py:454
  707.0 27.7 %wgrad.3 = (bf16[2,2048,256]{2,1,0:T(8,128)(2,1)}, bf16[2,2048,256]{2,1,0:T(8,128)(2,1)}, bf16[2,2048,256]{2,1,0:T(8,128)(2,1)}, bf16[2,2048,256]{2,1,0:T(8,128)(2,1)}) custom-call(s32[1]{0:T(128)} %bitcast.54._, bf16[2,240,2048]{2,1,0:T(8,128)(2,1)} %get-tuple-element.165.refs_0_, bf16[2,480,2048]{2,1,0:T(8,128)(2,1)} %get-tuple-element.166.refs_1_, ...), custom_call_target="tpu_custom_call" | custom-call | flops 16106127360 | bytes 31981568 | tf_op jit(solution)/shard_map/wgrad/pallas_call | solution.py:485
  820.6 36.0 %attend_back.1 = (f32[1536,512]{1,0:T(8,128)}, f32[1536,512]{1,0:T(8,128)}, bf16[1536,512]{1,0:T(8,128)(2,1)}, f32[1536,8]{1,0:T(8,128)}, f32[2,512]{1,0:T(2,128)}) custom-call(s32[8]{0:T(128)} %select_reduce_fusion.place, bf16[1536,512]{1,0:T(8,128)(2,1)} %get-tuple-element.187.q_s, bf16[1536,512]{1,0:T(8,128)(2,1)} %get-tuple-element.188.k_s, ...), custom_call_target="tpu_custom_call" | custom-call | flops 12079595520 | bytes 22020096 | tf_op jit(solution)/shard_map/attend_back/pallas_call | solution.py:248
  901.1 15.0 %convolution_convert_fusion.1 = bf16[2048,1536]{1,0:T(8,128)(2,1)} fusion(f32[2048]{0:T(1024)S(1)} %bitcast.229, f32[1536]{0:T(1024)S(1)} %copy-done.88, bf16[1536,512]{1,0:T(8,128)(2,1)} %get-tuple-element.193, bf16[1536,512]{1,0:T(8,128)(2,1)S(1)} %get-tuple-element.233, bf16[1536,512]{1,0:T(8,128)(2,1)S(1)} %get-tuple-element.232, ...), kind=kOutput, calls=%fused_computation.8 | convolution fusion | flops 9715580928 | bytes 17315840 | tf_op jit(solution)/shard_map/dot_general | solution.py:22
  951.9 18.2 %collective-permute-done.78 = bf16[352,1536]{1,0:T(8,128)(2,1)S(1)} collective-permute-done((bf16[352,1536]{1,0:T(8,128)(2,1)S(1)}, bf16[352,1536]{1,0:T(8,128)(2,1)S(1)}, u32[]{:S(2)}, u32[]{:S(2)}) %collective-permute-start.78) | collective-permute-done | bytes 1081376 | tf_op jit(solution)/shard_map/ppermute | solution.py:57
  975.4 27.7 %wgrad.5 = (bf16[2,2048,256]{2,1,0:T(8,128)(2,1)}, bf16[2,2048,256]{2,1,0:T(8,128)(2,1)}, bf16[2,2048,256]{2,1,0:T(8,128)(2,1)}, bf16[2,2048,256]{2,1,0:T(8,128)(2,1)}) custom-call(s32[1]{0:T(128)} %bitcast.90._, bf16[2,240,2048]{2,1,0:T(8,128)(2,1)} %get-tuple-element.204.refs_0_, bf16[2,480,2048]{2,1,0:T(8,128)(2,1)} %get-tuple-element.205.refs_1_, ...), custom_call_target="tpu_custom_call" | custom-call | flops 16106127360 | bytes 31981568 | tf_op jit(solution)/shard_map/wgrad/pallas_call | solution.py:485
  1028.8 29.6 %collective-permute-done.81 = bf16[2,2048,256]{2,1,0:T(8,128)(2,1)S(1)} collective-permute-done((bf16[2,2048,256]{2,1,0:T(8,128)(2,1)S(1)}, bf16[2,2048,256]{2,1,0:T(8,128)(2,1)S(1)}, u32[]{:S(2)}, u32[]{:S(2)}) %collective-permute-start.81) | collective-permute-done | bytes 2097184 | tf_op jit(solution)/shard_map/ppermute | solution.py:54
  1067.8 17.5 %collective-permute-done.83 = bf16[352,1536]{1,0:T(8,128)(2,1)S(1)} collective-permute-done((bf16[352,1536]{1,0:T(8,128)(2,1)S(1)}, bf16[352,1536]{1,0:T(8,128)(2,1)S(1)}, u32[]{:S(2)}, u32[]{:S(2)}) %collective-permute-start.83) | collective-permute-done | bytes 1081376 | tf_op jit(solution)/shard_map/ppermute | solution.py:54
  1104.5 22.6 %collective-permute-done.87.refs_2_ = bf16[368,1536]{1,0:T(8,128)(2,1)} collective-permute-done((bf16[368,1536]{1,0:T(8,128)(2,1)}, bf16[368,1536]{1,0:T(8,128)(2,1)}, u32[]{:S(2)}, u32[]{:S(2)}) %collective-permute-start.87) | collective-permute-done | bytes 1130528 | tf_op jit(solution)/shard_map/ppermute | solution.py:54
  (641 shorter events, 642.5 us)
Async XLA Ops:
  7.2 160.3 %all-gather.2.cloned.1.call-start = ((), (), s32[]{:S(2)}) async-start(), calls=%async_computation.2 | async-start | bytes 2359296 | tf_op jit(solution)/shard_map/all_gather | solution.py:626
  47.2 94.1 %collective-permute-start = (bf16[384,2048]{1,0:T(8,128)(2,1)S(1)}, bf16[384,2048]{1,0:T(8,128)(2,1)}, u32[]{:S(2)}, u32[]{:S(2)}) collective-permute-start(bf16[384,2048]{1,0:T(8,128)(2,1)S(1)} %bitcast.203), channel_id=1, source_target_pairs={{0,8},{8,0},{16,24},{24,16},{1,9},{9,1},{17,25},{25,17},{2,10},{10... | collective-permute-start | bytes 4718600 | tf_op jit(solution)/shard_map/ppermute | solution.py:542
  108.6 173.6 %collective-permute-start.27 = (bf16[1,4096,256]{2,1,0:T(8,128)(2,1)}, bf16[1,4096,256]{2,1,0:T(8,128)(2,1)}, u32[]{:S(2)}, u32[]{:S(2)}) collective-permute-start(bf16[1,4096,256]{2,1,0:T(8,128)(2,1)} %slice_add_fusion.2), channel_id=1, source_target_pairs={{0,8},{8,0},{16,24},{24,16},{1,9},{9,1},{17,25},{25,17},{2,10},{10... | collective-permute-start | bytes 6291464 | tf_op jit(solution)/shard_map/ppermute | solution.py:542
  141.3 75.7 %collective-permute-start.32 = (bf16[384,2048]{1,0:T(8,128)(2,1)}, bf16[384,2048]{1,0:T(8,128)(2,1)}, u32[]{:S(2)}, u32[]{:S(2)}) collective-permute-start(bf16[384,2048]{1,0:T(8,128)(2,1)} %bitcast.35.refs_1_), channel_id=1, source_target_pairs={{1,0},{3,1},{5,3},{7,5},{6,7},{4,6},{2,4},{0,2},{9,8},{11,9},{13,1... | collective-permute-start | bytes 4718600 | tf_op jit(solution)/shard_map/ppermute | solution.py:57
  142.6 71.4 %collective-permute-start.31 = (bf16[384,2048]{1,0:T(8,128)(2,1)}, bf16[384,2048]{1,0:T(8,128)(2,1)}, u32[]{:S(2)}, u32[]{:S(2)}) collective-permute-start(bf16[384,2048]{1,0:T(8,128)(2,1)} %bitcast.35.refs_1_), channel_id=1, source_target_pairs={{0,1},{1,3},{3,5},{5,7},{7,6},{6,4},{4,2},{2,0},{8,9},{9,11},{11,1... | collective-permute-start | bytes 4718600 | tf_op jit(solution)/shard_map/ppermute | solution.py:54
  167.5 77.2 %all-to-all-start = ((bf16[4,512,512]{2,1,0:T(8,128)(2,1)}), bf16[4,512,512]{2,1,0:T(8,128)(2,1)}, u32[]{:S(2)}, u32[]{:S(2)}) async-start(bf16[4,512,512]{2,1,0:T(8,128)(2,1)} %bitcast.214), calls=%async_computation | async-start | bytes 4194304 | tf_op jit(solution)/shard_map/all_to_all | solution.py:627
  209.2 74.8 %collective-permute-start.29 = (bf16[1,4096,256]{2,1,0:T(8,128)(2,1)}, bf16[1,4096,256]{2,1,0:T(8,128)(2,1)}, u32[]{:S(2)}, u32[]{:S(2)}) collective-permute-start(bf16[1,4096,256]{2,1,0:T(8,128)(2,1)} %slice_add_fusion.1), channel_id=1, source_target_pairs={{0,8},{8,0},{16,24},{24,16},{1,9},{9,1},{17,25},{25,17},{2,10},{10... | collective-permute-start | bytes 6291464 | tf_op jit(solution)/shard_map/ppermute | solution.py:542
  282.3 59.6 %collective-permute-start.43 = (bf16[384,2048]{1,0:T(8,128)(2,1)}, bf16[384,2048]{1,0:T(8,128)(2,1)}, u32[]{:S(2)}, u32[]{:S(2)}) collective-permute-start(bf16[384,2048]{1,0:T(8,128)(2,1)} %broadcast_add_fusion.1), channel_id=1, source_target_pairs={{0,1},{1,3},{3,5},{5,7},{7,6},{6,4},{4,2},{2,0},{8,9},{9,11},{11,1... | collective-permute-start | bytes 4718600 | tf_op jit(solution)/shard_map/ppermute | solution.py:54
  282.6 60.8 %collective-permute-start.44 = (bf16[384,2048]{1,0:T(8,128)(2,1)}, bf16[384,2048]{1,0:T(8,128)(2,1)}, u32[]{:S(2)}, u32[]{:S(2)}) collective-permute-start(bf16[384,2048]{1,0:T(8,128)(2,1)} %broadcast_add_fusion), channel_id=1, source_target_pairs={{1,0},{3,1},{5,3},{7,5},{6,7},{4,6},{2,4},{0,2},{9,8},{11,9},{13,1... | collective-permute-start | bytes 4718600 | tf_op jit(solution)/shard_map/ppermute | solution.py:57
  611.2 66.3 %collective-permute-start.54 = (bf16[384,2176]{1,0:T(8,128)(2,1)}, bf16[384,2176]{1,0:T(8,128)(2,1)S(1)}, u32[]{:S(2)}, u32[]{:S(2)}) collective-permute-start(bf16[384,2176]{1,0:T(8,128)(2,1)} %add.435), channel_id=1, source_target_pairs={{1,0},{3,1},{5,3},{7,5},{6,7},{4,6},{2,4},{0,2},{9,8},{11,9},{13,1... | collective-permute-start | bytes 5013512 | tf_op jit(solution)/shard_map/ppermute | solution.py:57
  615.5 62.0 %collective-permute-start.53 = (bf16[384,2176]{1,0:T(8,128)(2,1)}, bf16[384,2176]{1,0:T(8,128)(2,1)}, u32[]{:S(2)}, u32[]{:S(2)}) collective-permute-start(bf16[384,2176]{1,0:T(8,128)(2,1)} %add.433), channel_id=1, source_target_pairs={{0,1},{1,3},{3,5},{5,7},{7,6},{6,4},{4,2},{2,0},{8,9},{9,11},{11,1... | collective-permute-start | bytes 5013512 | tf_op jit(solution)/shard_map/ppermute | solution.py:54
  660.2 126.5 %collective-permute-start.67 = (bf16[2,2048,256]{2,1,0:T(8,128)(2,1)}, bf16[2,2048,256]{2,1,0:T(8,128)(2,1)}, u32[]{:S(2)}, u32[]{:S(2)}) collective-permute-start(bf16[2,2048,256]{2,1,0:T(8,128)(2,1)} %get-tuple-element.197), channel_id=1, source_target_pairs={{0,8},{8,0},{16,24},{24,16},{1,9},{9,1},{17,25},{25,17},{2,10},{10... | collective-permute-start | bytes 6291464 | tf_op jit(solution)/shard_map/ppermute | solution.py:542
  685.6 71.8 %collective-permute-start.64 = (bf16[384,2048]{1,0:T(8,128)(2,1)S(1)}, bf16[384,2048]{1,0:T(8,128)(2,1)}, u32[]{:S(2)}, u32[]{:S(2)}) collective-permute-start(bf16[384,2048]{1,0:T(8,128)(2,1)S(1)} %get-tuple-element.228), channel_id=1, source_target_pairs={{0,16},{16,0},{8,24},{24,8},{1,17},{17,1},{9,25},{25,9},{2,18},{18... | collective-permute-start | bytes 4718600 | tf_op jit(solution)/shard_map/ppermute | solution.py:54
  686.8 110.9 %collective-permute-start.63 = (bf16[384,2048]{1,0:T(8,128)(2,1)S(1)}, bf16[384,2048]{1,0:T(8,128)(2,1)}, u32[]{:S(2)}, u32[]{:S(2)}) collective-permute-start(bf16[384,2048]{1,0:T(8,128)(2,1)S(1)} %get-tuple-element.228), channel_id=1, source_target_pairs={{0,8},{8,0},{16,24},{24,16},{1,9},{9,1},{17,25},{25,17},{2,10},{10... | collective-permute-start | bytes 4718600 | tf_op jit(solution)/shard_map/ppermute | solution.py:542
  786.7 70.8 %collective-permute-start.66 = (bf16[2,2048,256]{2,1,0:T(8,128)(2,1)}, bf16[2,2048,256]{2,1,0:T(8,128)(2,1)}, u32[]{:S(2)}, u32[]{:S(2)}) collective-permute-start(bf16[2,2048,256]{2,1,0:T(8,128)(2,1)} %get-tuple-element.195), channel_id=1, source_target_pairs={{0,8},{8,0},{16,24},{24,16},{1,9},{9,1},{17,25},{25,17},{2,10},{10... | collective-permute-start | bytes 6291464 | tf_op jit(solution)/shard_map/ppermute | solution.py:542
  790.5 143.2 %collective-permute-start.72 = (bf16[2,2048,256]{2,1,0:T(8,128)(2,1)}, bf16[2,2048,256]{2,1,0:T(8,128)(2,1)}, u32[]{:S(2)}, u32[]{:S(2)}) collective-permute-start(bf16[2,2048,256]{2,1,0:T(8,128)(2,1)} %get-tuple-element.201), channel_id=1, source_target_pairs={{0,8},{8,0},{16,24},{24,16},{1,9},{9,1},{17,25},{25,17},{2,10},{10... | collective-permute-start | bytes 6291464 | tf_op jit(solution)/shard_map/ppermute | solution.py:542
  794.2 63.5 %collective-permute-start.68 = (bf16[2,2048,256]{2,1,0:T(8,128)(2,1)}, bf16[2,2048,256]{2,1,0:T(8,128)(2,1)}, u32[]{:S(2)}, u32[]{:S(2)}) collective-permute-start(bf16[2,2048,256]{2,1,0:T(8,128)(2,1)} %add_convert_fusion.2), channel_id=1, source_target_pairs={{0,16},{16,0},{8,24},{24,8},{1,17},{17,1},{9,25},{25,9},{2,18},{18... | collective-permute-start | bytes 6291464 | tf_op jit(solution)/shard_map/ppermute | solution.py:54
  797.7 64.4 %collective-permute-start.61 = (bf16[384,2048]{1,0:T(8,128)(2,1)}, bf16[384,2048]{1,0:T(8,128)(2,1)}, u32[]{:S(2)}, u32[]{:S(2)}) collective-permute-start(bf16[384,2048]{1,0:T(8,128)(2,1)} %add.447), channel_id=1, source_target_pairs={{1,0},{3,1},{5,3},{7,5},{6,7},{4,6},{2,4},{0,2},{9,8},{11,9},{13,1... | collective-permute-start | bytes 4718600 | tf_op jit(solution)/shard_map/ppermute | solution.py:57
  798.8 68.9 %collective-permute-start.57 = (bf16[384,2048]{1,0:T(8,128)(2,1)}, bf16[384,2048]{1,0:T(8,128)(2,1)}, u32[]{:S(2)}, u32[]{:S(2)}) collective-permute-start(bf16[384,2048]{1,0:T(8,128)(2,1)} %add.443), channel_id=1, source_target_pairs={{0,1},{1,3},{3,5},{5,7},{7,6},{6,4},{4,2},{2,0},{8,9},{9,11},{11,1... | collective-permute-start | bytes 4718600 | tf_op jit(solution)/shard_map/ppermute | solution.py:54
  807.8 63.4 %all-to-all-start.1 = ((bf16[4,512,512]{2,1,0:T(8,128)(2,1)}), bf16[4,512,512]{2,1,0:T(8,128)(2,1)S(1)}, u32[]{:S(2)}, u32[]{:S(2)}) async-start(bf16[4,512,512]{2,1,0:T(8,128)(2,1)} %bitcast.208), calls=%async_computation.1 | async-start | bytes 4194304 | tf_op jit(solution)/shard_map/all_to_all | solution.py:783
  866.2 83.4 %collective-permute-start.62 = (bf16[384,2048]{1,0:T(8,128)(2,1)}, bf16[384,2048]{1,0:T(8,128)(2,1)}, u32[]{:S(2)}, u32[]{:S(2)}) collective-permute-start(bf16[384,2048]{1,0:T(8,128)(2,1)} %add.448), channel_id=1, source_target_pairs={{1,0},{3,1},{5,3},{7,5},{6,7},{4,6},{2,4},{0,2},{9,8},{11,9},{13,1... | collective-permute-start | bytes 4718600 | tf_op jit(solution)/shard_map/ppermute | solution.py:57
  870.8 79.9 %collective-permute-start.58 = (bf16[384,2048]{1,0:T(8,128)(2,1)}, bf16[384,2048]{1,0:T(8,128)(2,1)}, u32[]{:S(2)}, u32[]{:S(2)}) collective-permute-start(bf16[384,2048]{1,0:T(8,128)(2,1)} %add.444), channel_id=1, source_target_pairs={{0,1},{1,3},{3,5},{5,7},{7,6},{6,4},{4,2},{2,0},{8,9},{9,11},{11,1... | collective-permute-start | bytes 4718600 | tf_op jit(solution)/shard_map/ppermute | solution.py:54
  1063.0 64.9 %collective-permute-start.69 = (bf16[384,2048]{1,0:T(8,128)(2,1)}, bf16[384,2048]{1,0:T(8,128)(2,1)}, u32[]{:S(2)}, u32[]{:S(2)}) collective-permute-start(bf16[384,2048]{1,0:T(8,128)(2,1)} %get-tuple-element.242), channel_id=1, source_target_pairs={{0,8},{8,0},{16,24},{24,16},{1,9},{9,1},{17,25},{25,17},{2,10},{10... | collective-permute-start | bytes 4718600 | tf_op jit(solution)/shard_map/ppermute | solution.py:542
  1066.6 61.4 %collective-permute-start.71 = (bf16[384,2048]{1,0:T(8,128)(2,1)}, bf16[384,2048]{1,0:T(8,128)(2,1)}, u32[]{:S(2)}, u32[]{:S(2)}) collective-permute-start(bf16[384,2048]{1,0:T(8,128)(2,1)} %add_convert_fusion.3), channel_id=1, source_target_pairs={{0,16},{16,0},{8,24},{24,8},{1,17},{17,1},{9,25},{25,9},{2,18},{18... | collective-permute-start | bytes 4718600 | tf_op jit(solution)/shard_map/ppermute | solution.py:54
  (160 other events, 3122.0 us)
Sparse Core Ops, SparseCore 0:
  19.6 60.5 all-gather.1

commit v4 on v3

--- a/solution.py
+++ b/solution.py
@@ -384,7 +384,7 @@
 
 def _combine_kernel(*refs, terms, count, cap, tile, extra, adds, experts):
     it = iter(refs)
-    first = next(it) if extra else None
+    first = next(it)
     slot = next(it)
     factors = [(next(it), next(it)) for _ in range(terms)]
     dgate = next(it) if extra else None
@@ -423,7 +423,7 @@
                 @pl.when(j > 0)
                 def _(): outs[s][:, D:] = (outs[s][:, D:].astype(F32) + part).astype(outs[s].dtype)
 
-def combine(slots, at, factors, cap, adds, first=None, dgate=None, experts=0, tile=1024, out_dtype=BF):
+def combine(slots, at, factors, cap, adds, first, dgate=None, experts=0, tile=1024, out_dtype=BF):
     n = len(adds)
     _, J, T, _ = slots.shape
     M, F = factors[0][0].shape[1:]
@@ -432,10 +432,7 @@
     width = D + (PAD if extra else 0)
     steps = D // tile
     one = pl.Buffered(1)
-    ops, specs = [], []
-    if extra:
-        ops.append(first)
-        specs.append(pl.BlockSpec(memory_space=pltpu.SMEM))
+    ops, specs = [first], [pl.BlockSpec(memory_space=pltpu.SMEM)]
     ops.append(slots)
     specs.append(pl.BlockSpec((n, J, T, 1), lambda i, j: (at, 0, 0, 0), pipeline_mode=one))
     for a, w, block in factors:
@@ -702,14 +699,14 @@
         members, at = groups[g]
         _, dg, du, _, dgate = done[g]
         kind = F32 if members == [0] else BF
-        got = combine(line.tie(slot_col), at, [(dg, w_gu, 0), (du, w_gu, 1)], room, [None] * len(members), first, dgate, NE, out_dtype=kind)
+        got = combine(slot_col, at, [(dg, w_gu, 0), (du, w_gu, 1)], room, [None] * len(members), line.tie(first), dgate, NE, out_dtype=kind)
         line.mark(got[0])
         return got
 
     def mix(g):
         members, at = groups[g]
         kind = F32 if members == [0] else BF
-        got = combine(line.tie(slot_col), at, [(done[g][3], w_dn, 0)], room, [None] * len(members), out_dtype=kind)
+        got = combine(slot_col, at, [(done[g][3], w_dn, 0)], room, [None] * len(members), line.tie(first), out_dtype=kind)
         line.mark(got[0])
         return got
 

time: 1170 us -> 1160 us (level)
  local copies, waits for them, and re-layouts: 150 us -> 136 us
  other arithmetic: 145 us -> 132 us
    optimization_barrier x10 -> x0, local copies, waits for them, and re-layouts: 22 us -> none  [after(): return lax.optimization_barrier((v, *others))[0]]
    unnamed x202 -> x201, local copies, waits for them, and re-layouts: 21.5 us -> 28.5 us
  transfers between devices with their start and end apart: 92 -> 92, of which waited for: 20 -> 21; matrix products, arithmetic and copies ran while one was open for 29% -> 27% of each run, Pallas kernels for 31% -> 31%
where the time goes in v4:
time: 1160 us; the launch traced here: 1140 us
  Pallas kernels  427 us (37%)
  waiting for transfers between devices  208 us (18%)
  local copies, waits for them, and re-layouts  136 us (12%)
  other arithmetic  132 us (11%)
  starting transfers between devices  113 us (10%)
  matrix products  66.2 us (6%)
  between operations  33.8 us (3%)
  blocking collectives  27.6 us (2%)
    pallas_call x10, Pallas kernels, combine(): pl.pallas_call(functools.partial(_combine_kernel, terms=len(factors), cou...  136 us
    ppermute x39, waiting for transfers between devices, go_right(): return lax.ppermute(v, self.axis, self.right)  126 us
    pallas_call x5, Pallas kernels, expert(): pl.pallas_call(functools.partial(_expert_kernel, count=n, cap=cap, expert...  85.6 us
    pallas_call x3, Pallas kernels, wgrad(): pl.pallas_call(functools.partial(_wgrad_kernel, count=n, pieces=pieces),...  83.2 us
    ppermute x28, waiting for transfers between devices, go_left(): return lax.ppermute(v, self.axis, self.left)  79.3 us
    dot_general x11, matrix products, dot(): return lax.dot_general(a, b, (dims, ((), ())), preferred_element_type=F32)  66.2 us
    pallas_call x5, Pallas kernels, dispatch(): pl.pallas_call(functools.partial(_dispatch_kernel, count=n, cap=cap), gri...  53 us
    ppermute x22, starting transfers between devices, swap(): return lax.ppermute(v, 'ctx', sibling)  38.7 us
  transfers between devices with their start and end apart: 92, of which 21 were waited for; matrix products, arithmetic and copies ran while one was open for 27% of the time, Pallas kernels for 31%

profile of v4, /device:TPU:1, one launch (start us, length us, event | category | flops | bytes accessed | tf_op | source)
XLA Modules:
  0.0 1144.7 jit_solution(13801603187501676050)
XLA Ops:
  151.9 16.0 %fusion.13.qp.kp.vp = f32[1536,1536]{1,0:T(8,128)S(1)} fusion(bf16[2048,1536]{1,0:T(8,128)(2,1)} %bitcast.33, f32[2048]{0:T(1024)S(1)} %bitcast.226, f32[1536]{0:T(1024)S(1)} %add_rsqrt_fusion, bf16[384,2048]{1,0:T(8,128)(2,1)} %collective-permute-done.2, bf16[384,2048]{1,0:T(8,128)(2,1)} %collective-permute-done.1, ...), kind=kOutput, calls=%fused_computation.57 | convolution fusion | flops 9698279424 | bytes 22034432 | tf_op jit(solution)/shard_map/dot_general | solution.py:22
  192.2 16.7 %psum.14 = f32[4,2,384]{2,1,0:T(2,128)S(1)} all-reduce(f32[4,2,384]{2,1,0:T(2,128)S(1)} %constant_dynamic-update-slice_fusion.19), channel_id=1, replica_groups=mesh['ctx'=4,'exp'=8] {'ctx'}, use_global_device_ids=true, to_apply=%region_4.5 | all-reduce | flops 3072 | bytes 24576 | tf_op jit(solution)/shard_map/psum | solution.py:559
  225.7 23.5 %attend.1 = (bf16[1536,512]{1,0:T(8,128)(2,1)}, bf16[1536,512]{1,0:T(8,128)(2,1)}, bf16[1536,512]{1,0:T(8,128)(2,1)}, bf16[1536,512]{1,0:T(8,128)(2,1)}, f32[4,1536,1]{2,1,0:T(8,128)}) custom-call(s32[8]{0:T(128)} %select_reduce_fusion.place, f32[1536,1536]{1,0:T(8,128)} %copy-done.3, f32[1536,1536]{1,0:T(8,128)} %copy-done.3, f32[1536,1536]{1,0:T(8,128)} %copy-done.3, ...), custom_call_target="tpu_custom_call" | custom-call | flops 4831838208 | bytes 15728640 | tf_op jit(solution)/shard_map/attend/pallas_call | solution.py:228
  303.9 19.7 %collective-permute-done.26 = bf16[384,2048]{1,0:T(8,128)(2,1)S(1)} collective-permute-done((bf16[384,2048]{1,0:T(8,128)(2,1)S(1)}, bf16[384,2048]{1,0:T(8,128)(2,1)S(1)}, u32[]{:S(2)}, u32[]{:S(2)}) %collective-permute-start.26) | collective-permute-done | bytes 1572896 | tf_op jit(solution)/shard_map/ppermute | solution.py:54
  331.2 13.4 %expert.5 = (bf16[2,240,2048]{2,1,0:T(8,128)(2,1)}, bf16[2,240,1024]{2,1,0:T(8,128)(2,1)}, bf16[2,240,1024]{2,1,0:T(8,128)(2,1)}, bf16[2,240,1024]{2,1,0:T(8,128)(2,1)}, f32[2,240,1]{2,1,0:T(8,128)}) custom-call(s32[1]{0:T(128)} %bitcast.50.first.refs_0_, s32[8,2,1,384]{3,2,1,0:T(1,128)} %broadcast_in_dim_reshape.13.refs_0_.slot, ...), custom_call_target="tpu_custom_call" | custom-call | flops 4781506560 | bytes 24248320 | tf_op jit(solution)/shard_map/expert/pallas_call | solution.py:360
  386.8 19.6 %expert.6 = (bf16[2,480,2048]{2,1,0:T(8,128)(2,1)}, bf16[2,480,1024]{2,1,0:T(8,128)(2,1)}, bf16[2,480,1024]{2,1,0:T(8,128)(2,1)}, bf16[2,480,1024]{2,1,0:T(8,128)(2,1)}, f32[2,480,1]{2,1,0:T(8,128)}) custom-call(s32[1]{0:T(128)} %bitcast.50.first.refs_0_, s32[8,2,1,384]{3,2,1,0:T(1,128)} %broadcast_in_dim_reshape.13.refs_0_.slot, ...), custom_call_target="tpu_custom_call" | custom-call | flops 9563013120 | bytes 31719424 | tf_op jit(solution)/shard_map/expert/pallas_call | solution.py:360
  406.4 12.5 %collective-permute-done.38.refs_1_ = bf16[384,2176]{1,0:T(8,128)(2,1)} collective-permute-done((bf16[384,2176]{1,0:T(8,128)(2,1)}, bf16[384,2176]{1,0:T(8,128)(2,1)}, u32[]{:S(2)}, u32[]{:S(2)}) %collective-permute-start.38) | collective-permute-done | bytes 1671200 | tf_op jit(solution)/shard_map/ppermute | solution.py:57
  432.7 19.6 %expert.7 = (bf16[2,480,2048]{2,1,0:T(8,128)(2,1)}, bf16[2,480,1024]{2,1,0:T(8,128)(2,1)}, bf16[2,480,1024]{2,1,0:T(8,128)(2,1)}, bf16[2,480,1024]{2,1,0:T(8,128)(2,1)}, f32[2,480,1]{2,1,0:T(8,128)}) custom-call(s32[1]{0:T(128)} %bitcast.50.first.refs_0_, s32[8,2,1,384]{3,2,1,0:T(1,128)} %broadcast_in_dim_reshape.13.refs_0_.slot, ...), custom_call_target="tpu_custom_call" | custom-call | flops 9563013120 | bytes 31719424 | tf_op jit(solution)/shard_map/expert/pallas_call | solution.py:360
  463.2 19.6 %expert.8 = (bf16[2,480,2048]{2,1,0:T(8,128)(2,1)}, bf16[2,480,1024]{2,1,0:T(8,128)(2,1)}, bf16[2,480,1024]{2,1,0:T(8,128)(2,1)}, bf16[2,480,1024]{2,1,0:T(8,128)(2,1)}, f32[2,480,1]{2,1,0:T(8,128)}) custom-call(s32[1]{0:T(128)} %bitcast.50.first.refs_0_, s32[8,2,1,384]{3,2,1,0:T(1,128)} %broadcast_in_dim_reshape.13.refs_0_.slot, ...), custom_call_target="tpu_custom_call" | custom-call | flops 9563013120 | bytes 31719424 | tf_op jit(solution)/shard_map/expert/pallas_call | solution.py:360
  484.1 13.4 %expert.9 = (bf16[2,240,2048]{2,1,0:T(8,128)(2,1)}, bf16[2,240,1024]{2,1,0:T(8,128)(2,1)}, bf16[2,240,1024]{2,1,0:T(8,128)(2,1)}, bf16[2,240,1024]{2,1,0:T(8,128)(2,1)}, f32[2,240,1]{2,1,0:T(8,128)}) custom-call(s32[1]{0:T(128)} %bitcast.50.first.refs_0_, s32[8,2,1,384]{3,2,1,0:T(1,128)} %broadcast_in_dim_reshape.13.refs_0_.slot, ...), custom_call_target="tpu_custom_call" | custom-call | flops 4781506560 | bytes 24248320 | tf_op jit(solution)/shard_map/expert/pallas_call | solution.py:360
  512.5 19.0 %combine.11 = (bf16[384,2176]{1,0:T(8,128)(2,1)}, bf16[384,2176]{1,0:T(8,128)(2,1)}) custom-call(s32[1]{0:T(128)} %bitcast.50.first.refs_0_, s32[8,2,384,1]{3,2,1,0:T(8,128)} %broadcast_in_dim_reshape.15.refs_1_, bf16[2,480,1024]{2,1,0:T(8,128)(2,1)} %get-tuple-element.137.refs_2_.refs_8_, bf16[2,4096,1024]{2,1,0:T(8,128)(2,1)} %copy-done.2, ...), custom_call_target="tpu_custom_call" | custom-call | flops 9563013120 | bytes 27000832 | tf_op jit(solution)/shard_map/combine/pallas_call | solution.py:451
  535.4 19.0 %combine.12 = (bf16[384,2176]{1,0:T(8,128)(2,1)}, bf16[384,2176]{1,0:T(8,128)(2,1)}) custom-call(s32[1]{0:T(128)} %bitcast.50.first.refs_0_, s32[8,2,384,1]{3,2,1,0:T(8,128)} %broadcast_in_dim_reshape.15.refs_1_, bf16[2,480,1024]{2,1,0:T(8,128)(2,1)} %get-tuple-element.133.refs_2_.refs_7_, bf16[2,4096,1024]{2,1,0:T(8,128)(2,1)} %copy-done.2, ...), custom_call_target="tpu_custom_call" | custom-call | flops 9563013120 | bytes 27000832 | tf_op jit(solution)/shard_map/combine/pallas_call | solution.py:451
  554.4 12.7 %collective-permute-done.51 = bf16[384,2176]{1,0:T(8,128)(2,1)S(1)} collective-permute-done((bf16[384,2176]{1,0:T(8,128)(2,1)S(1)}, bf16[384,2176]{1,0:T(8,128)(2,1)S(1)}, u32[]{:S(2)}, u32[]{:S(2)}) %collective-permute-start.51) | collective-permute-done | bytes 1671200 | tf_op jit(solution)/shard_map/ppermute | solution.py:57
  571.0 19.2 %combine.13 = (bf16[384,2176]{1,0:T(8,128)(2,1)}, bf16[384,2176]{1,0:T(8,128)(2,1)}) custom-call(s32[1]{0:T(128)} %bitcast.50.first.refs_0_, s32[8,2,384,1]{3,2,1,0:T(8,128)} %broadcast_in_dim_reshape.15.refs_1_, bf16[2,480,1024]{2,1,0:T(8,128)(2,1)} %get-tuple-element.129.refs_2_.refs_6_, bf16[2,4096,1024]{2,1,0:T(8,128)(2,1)} %copy-done.2, ...), custom_call_target="tpu_custom_call" | custom-call | flops 9563013120 | bytes 27000832 | tf_op jit(solution)/shard_map/combine/pallas_call | solution.py:451
  603.5 12.6 %combine.14 = f32[384,2176]{1,0:T(8,128)} custom-call(s32[1]{0:T(128)} %bitcast.50.first.refs_0_, s32[8,2,384,1]{3,2,1,0:T(8,128)} %broadcast_in_dim_reshape.15.refs_1_, bf16[2,240,1024]{2,1,0:T(8,128)(2,1)} %get-tuple-element.125.refs_2_.refs_5_, bf16[2,4096,1024]{2,1,0:T(8,128)(2,1)} %copy-done.2, ...), custom_call_target="tpu_custom_call" | custom-call | flops 4781506560 | bytes 21889024 | tf_op jit(solution)/shard_map/combine/pallas_call | solution.py:451
  622.8 27.7 %wgrad.4 = (bf16[2,2048,256]{2,1,0:T(8,128)(2,1)}, bf16[2,2048,256]{2,1,0:T(8,128)(2,1)}, bf16[2,2048,256]{2,1,0:T(8,128)(2,1)}, bf16[2,2048,256]{2,1,0:T(8,128)(2,1)}) custom-call(s32[1]{0:T(128)} %bitcast.55._, bf16[2,240,2048]{2,1,0:T(8,128)(2,1)} %get-tuple-element.165.refs_0_, bf16[2,480,2048]{2,1,0:T(8,128)(2,1)} %get-tuple-element.166.refs_1_, ...), custom_call_target="tpu_custom_call" | custom-call | flops 16106127360 | bytes 31981568 | tf_op jit(solution)/shard_map/wgrad/pallas_call | solution.py:482
  692.5 27.7 %wgrad.3 = (bf16[2,2048,256]{2,1,0:T(8,128)(2,1)}, bf16[2,2048,256]{2,1,0:T(8,128)(2,1)}, bf16[2,2048,256]{2,1,0:T(8,128)(2,1)}, bf16[2,2048,256]{2,1,0:T(8,128)(2,1)}) custom-call(s32[1]{0:T(128)} %bitcast.54._, bf16[2,240,2048]{2,1,0:T(8,128)(2,1)} %get-tuple-element.165.refs_0_, bf16[2,480,2048]{2,1,0:T(8,128)(2,1)} %get-tuple-element.166.refs_1_, ...), custom_call_target="tpu_custom_call" | custom-call | flops 16106127360 | bytes 31981568 | tf_op jit(solution)/shard_map/wgrad/pallas_call | solution.py:482
  803.5 36.1 %attend_back.1 = (f32[1536,512]{1,0:T(8,128)}, f32[1536,512]{1,0:T(8,128)}, bf16[1536,512]{1,0:T(8,128)(2,1)}, f32[1536,8]{1,0:T(8,128)}, f32[2,512]{1,0:T(2,128)}) custom-call(s32[8]{0:T(128)} %select_reduce_fusion.place, bf16[1536,512]{1,0:T(8,128)(2,1)} %get-tuple-element.187.q_s, bf16[1536,512]{1,0:T(8,128)(2,1)} %get-tuple-element.188.k_s, ...), custom_call_target="tpu_custom_call" | custom-call | flops 12079595520 | bytes 22020096 | tf_op jit(solution)/shard_map/attend_back/pallas_call | solution.py:248
  883.9 15.0 %convolution_convert_fusion.1 = bf16[2048,1536]{1,0:T(8,128)(2,1)} fusion(f32[2048]{0:T(1024)S(1)} %bitcast.227, f32[1536]{0:T(1024)S(1)} %copy-done.88, bf16[1536,512]{1,0:T(8,128)(2,1)} %get-tuple-element.193, bf16[1536,512]{1,0:T(8,128)(2,1)S(1)} %get-tuple-element.233, bf16[1536,512]{1,0:T(8,128)(2,1)S(1)} %get-tuple-element.232, ...), kind=kOutput, calls=%fused_computation.8 | convolution fusion | flops 9715580928 | bytes 17315840 | tf_op jit(solution)/shard_map/dot_general | solution.py:22
  935.0 18.0 %collective-permute-done.78 = bf16[352,1536]{1,0:T(8,128)(2,1)S(1)} collective-permute-done((bf16[352,1536]{1,0:T(8,128)(2,1)S(1)}, bf16[352,1536]{1,0:T(8,128)(2,1)S(1)}, u32[]{:S(2)}, u32[]{:S(2)}) %collective-permute-start.78) | collective-permute-done | bytes 1081376 | tf_op jit(solution)/shard_map/ppermute | solution.py:57
  958.6 27.7 %wgrad.5 = (bf16[2,2048,256]{2,1,0:T(8,128)(2,1)}, bf16[2,2048,256]{2,1,0:T(8,128)(2,1)}, bf16[2,2048,256]{2,1,0:T(8,128)(2,1)}, bf16[2,2048,256]{2,1,0:T(8,128)(2,1)}) custom-call(s32[1]{0:T(128)} %bitcast.90._, bf16[2,240,2048]{2,1,0:T(8,128)(2,1)} %get-tuple-element.204.refs_0_, bf16[2,480,2048]{2,1,0:T(8,128)(2,1)} %get-tuple-element.205.refs_1_, ...), custom_call_target="tpu_custom_call" | custom-call | flops 16106127360 | bytes 31981568 | tf_op jit(solution)/shard_map/wgrad/pallas_call | solution.py:482
  1012.1 29.6 %collective-permute-done.81 = bf16[2,2048,256]{2,1,0:T(8,128)(2,1)S(1)} collective-permute-done((bf16[2,2048,256]{2,1,0:T(8,128)(2,1)S(1)}, bf16[2,2048,256]{2,1,0:T(8,128)(2,1)S(1)}, u32[]{:S(2)}, u32[]{:S(2)}) %collective-permute-start.81) | collective-permute-done | bytes 2097184 | tf_op jit(solution)/shard_map/ppermute | solution.py:54
  1051.0 17.5 %collective-permute-done.83 = bf16[352,1536]{1,0:T(8,128)(2,1)S(1)} collective-permute-done((bf16[352,1536]{1,0:T(8,128)(2,1)S(1)}, bf16[352,1536]{1,0:T(8,128)(2,1)S(1)}, u32[]{:S(2)}, u32[]{:S(2)}) %collective-permute-start.83) | collective-permute-done | bytes 1081376 | tf_op jit(solution)/shard_map/ppermute | solution.py:54
  1087.6 22.7 %collective-permute-done.87.refs_2_ = bf16[368,1536]{1,0:T(8,128)(2,1)} collective-permute-done((bf16[368,1536]{1,0:T(8,128)(2,1)}, bf16[368,1536]{1,0:T(8,128)(2,1)}, u32[]{:S(2)}, u32[]{:S(2)}) %collective-permute-start.87) | collective-permute-done | bytes 1130528 | tf_op jit(solution)/shard_map/ppermute | solution.py:54
  (626 shorter events, 632.4 us)
Async XLA Ops:
  7.2 164.9 %all-gather.2.cloned.1.call-start = ((), (), s32[]{:S(2)}) async-start(), calls=%async_computation.2 | async-start | bytes 2359296 | tf_op jit(solution)/shard_map/all_gather | solution.py:623
  42.4 103.5 %collective-permute-start = (bf16[384,2048]{1,0:T(8,128)(2,1)S(1)}, bf16[384,2048]{1,0:T(8,128)(2,1)}, u32[]{:S(2)}, u32[]{:S(2)}) collective-permute-start(bf16[384,2048]{1,0:T(8,128)(2,1)S(1)} %bitcast.203), channel_id=1, source_target_pairs={{0,8},{8,0},{16,24},{24,16},{1,9},{9,1},{17,25},{25,17},{2,10},{10... | collective-permute-start | bytes 4718600 | tf_op jit(solution)/shard_map/ppermute | solution.py:539
  111.3 175.6 %collective-permute-start.27 = (bf16[1,4096,256]{2,1,0:T(8,128)(2,1)}, bf16[1,4096,256]{2,1,0:T(8,128)(2,1)}, u32[]{:S(2)}, u32[]{:S(2)}) collective-permute-start(bf16[1,4096,256]{2,1,0:T(8,128)(2,1)} %slice_add_fusion.2), channel_id=1, source_target_pairs={{0,8},{8,0},{16,24},{24,16},{1,9},{9,1},{17,25},{25,17},{2,10},{10... | collective-permute-start | bytes 6291464 | tf_op jit(solution)/shard_map/ppermute | solution.py:539
  145.9 76.7 %collective-permute-start.32 = (bf16[384,2048]{1,0:T(8,128)(2,1)}, bf16[384,2048]{1,0:T(8,128)(2,1)}, u32[]{:S(2)}, u32[]{:S(2)}) collective-permute-start(bf16[384,2048]{1,0:T(8,128)(2,1)} %bitcast.35.refs_1_), channel_id=1, source_target_pairs={{1,0},{3,1},{5,3},{7,5},{6,7},{4,6},{2,4},{0,2},{9,8},{11,9},{13,1... | collective-permute-start | bytes 4718600 | tf_op jit(solution)/shard_map/ppermute | solution.py:57
  147.2 71.4 %collective-permute-start.31 = (bf16[384,2048]{1,0:T(8,128)(2,1)}, bf16[384,2048]{1,0:T(8,128)(2,1)}, u32[]{:S(2)}, u32[]{:S(2)}) collective-permute-start(bf16[384,2048]{1,0:T(8,128)(2,1)} %bitcast.35.refs_1_), channel_id=1, source_target_pairs={{0,1},{1,3},{3,5},{5,7},{7,6},{6,4},{4,2},{2,0},{8,9},{9,11},{11,1... | collective-permute-start | bytes 4718600 | tf_op jit(solution)/shard_map/ppermute | solution.py:54
  172.1 77.1 %all-to-all-start = ((bf16[4,512,512]{2,1,0:T(8,128)(2,1)}), bf16[4,512,512]{2,1,0:T(8,128)(2,1)}, u32[]{:S(2)}, u32[]{:S(2)}) async-start(bf16[4,512,512]{2,1,0:T(8,128)(2,1)} %bitcast.214), calls=%async_computation | async-start | bytes 4194304 | tf_op jit(solution)/shard_map/all_to_all | solution.py:624
  213.7 74.9 %collective-permute-start.29 = (bf16[1,4096,256]{2,1,0:T(8,128)(2,1)}, bf16[1,4096,256]{2,1,0:T(8,128)(2,1)}, u32[]{:S(2)}, u32[]{:S(2)}) collective-permute-start(bf16[1,4096,256]{2,1,0:T(8,128)(2,1)} %slice_add_fusion.1), channel_id=1, source_target_pairs={{0,8},{8,0},{16,24},{24,16},{1,9},{9,1},{17,25},{25,17},{2,10},{10... | collective-permute-start | bytes 6291464 | tf_op jit(solution)/shard_map/ppermute | solution.py:539
  287.0 59.5 %collective-permute-start.43 = (bf16[384,2048]{1,0:T(8,128)(2,1)}, bf16[384,2048]{1,0:T(8,128)(2,1)}, u32[]{:S(2)}, u32[]{:S(2)}) collective-permute-start(bf16[384,2048]{1,0:T(8,128)(2,1)} %broadcast_add_fusion.1), channel_id=1, source_target_pairs={{0,1},{1,3},{3,5},{5,7},{7,6},{6,4},{4,2},{2,0},{8,9},{9,11},{11,1... | collective-permute-start | bytes 4718600 | tf_op jit(solution)/shard_map/ppermute | solution.py:54
  288.2 60.8 %collective-permute-start.44 = (bf16[384,2048]{1,0:T(8,128)(2,1)}, bf16[384,2048]{1,0:T(8,128)(2,1)}, u32[]{:S(2)}, u32[]{:S(2)}) collective-permute-start(bf16[384,2048]{1,0:T(8,128)(2,1)} %broadcast_add_fusion), channel_id=1, source_target_pairs={{1,0},{3,1},{5,3},{7,5},{6,7},{4,6},{2,4},{0,2},{9,8},{11,9},{13,1... | collective-permute-start | bytes 4718600 | tf_op jit(solution)/shard_map/ppermute | solution.py:57
  650.6 111.7 %collective-permute-start.67 = (bf16[2,2048,256]{2,1,0:T(8,128)(2,1)}, bf16[2,2048,256]{2,1,0:T(8,128)(2,1)}, u32[]{:S(2)}, u32[]{:S(2)}) collective-permute-start(bf16[2,2048,256]{2,1,0:T(8,128)(2,1)} %get-tuple-element.197), channel_id=1, source_target_pairs={{0,8},{8,0},{16,24},{24,16},{1,9},{9,1},{17,25},{25,17},{2,10},{10... | collective-permute-start | bytes 6291464 | tf_op jit(solution)/shard_map/ppermute | solution.py:539
  673.3 64.8 %collective-permute-start.64 = (bf16[384,2048]{1,0:T(8,128)(2,1)S(1)}, bf16[384,2048]{1,0:T(8,128)(2,1)}, u32[]{:S(2)}, u32[]{:S(2)}) collective-permute-start(bf16[384,2048]{1,0:T(8,128)(2,1)S(1)} %get-tuple-element.228), channel_id=1, source_target_pairs={{0,16},{16,0},{8,24},{24,8},{1,17},{17,1},{9,25},{25,9},{2,18},{18... | collective-permute-start | bytes 4718600 | tf_op jit(solution)/shard_map/ppermute | solution.py:54
  674.4 106.3 %collective-permute-start.63 = (bf16[384,2048]{1,0:T(8,128)(2,1)S(1)}, bf16[384,2048]{1,0:T(8,128)(2,1)}, u32[]{:S(2)}, u32[]{:S(2)}) collective-permute-start(bf16[384,2048]{1,0:T(8,128)(2,1)S(1)} %get-tuple-element.228), channel_id=1, source_target_pairs={{0,8},{8,0},{16,24},{24,16},{1,9},{9,1},{17,25},{25,17},{2,10},{10... | collective-permute-start | bytes 4718600 | tf_op jit(solution)/shard_map/ppermute | solution.py:539
  674.9 57.9 %collective-permute-start.55 = (bf16[192,2048]{1,0:T(8,128)(2,1)S(1)}, bf16[192,2048]{1,0:T(8,128)(2,1)S(1)}, u32[]{:S(2)}, u32[]{:S(2)}) collective-permute-start(bf16[192,2048]{1,0:T(8,128)(2,1)S(1)} %get-tuple-element.262), channel_id=1, source_target_pairs={{0,1},{1,3},{3,5},{5,7},{7,6},{6,4},{4,2},{2,0},{8,9},{9,11},{11,1... | collective-permute-start | bytes 2359304 | tf_op jit(solution)/shard_map/ppermute | solution.py:54
  675.2 59.2 %collective-permute-start.59 = (bf16[192,2048]{1,0:T(8,128)(2,1)S(1)}, bf16[192,2048]{1,0:T(8,128)(2,1)S(1)}, u32[]{:S(2)}, u32[]{:S(2)}) collective-permute-start(bf16[192,2048]{1,0:T(8,128)(2,1)S(1)} %get-tuple-element.263), channel_id=1, source_target_pairs={{1,0},{3,1},{5,3},{7,5},{6,7},{4,6},{2,4},{0,2},{9,8},{11,9},{13,1... | collective-permute-start | bytes 2359304 | tf_op jit(solution)/shard_map/ppermute | solution.py:57
  762.3 78.3 %collective-permute-start.66 = (bf16[2,2048,256]{2,1,0:T(8,128)(2,1)}, bf16[2,2048,256]{2,1,0:T(8,128)(2,1)}, u32[]{:S(2)}, u32[]{:S(2)}) collective-permute-start(bf16[2,2048,256]{2,1,0:T(8,128)(2,1)} %get-tuple-element.195), channel_id=1, source_target_pairs={{0,8},{8,0},{16,24},{24,16},{1,9},{9,1},{17,25},{25,17},{2,10},{10... | collective-permute-start | bytes 6291464 | tf_op jit(solution)/shard_map/ppermute | solution.py:539
  772.2 144.6 %collective-permute-start.72 = (bf16[2,2048,256]{2,1,0:T(8,128)(2,1)}, bf16[2,2048,256]{2,1,0:T(8,128)(2,1)}, u32[]{:S(2)}, u32[]{:S(2)}) collective-permute-start(bf16[2,2048,256]{2,1,0:T(8,128)(2,1)} %get-tuple-element.201), channel_id=1, source_target_pairs={{0,8},{8,0},{16,24},{24,16},{1,9},{9,1},{17,25},{25,17},{2,10},{10... | collective-permute-start | bytes 6291464 | tf_op jit(solution)/shard_map/ppermute | solution.py:539
  777.1 63.7 %collective-permute-start.68 = (bf16[2,2048,256]{2,1,0:T(8,128)(2,1)}, bf16[2,2048,256]{2,1,0:T(8,128)(2,1)}, u32[]{:S(2)}, u32[]{:S(2)}) collective-permute-start(bf16[2,2048,256]{2,1,0:T(8,128)(2,1)} %add_convert_fusion.2), channel_id=1, source_target_pairs={{0,16},{16,0},{8,24},{24,8},{1,17},{17,1},{9,25},{25,9},{2,18},{18... | collective-permute-start | bytes 6291464 | tf_op jit(solution)/shard_map/ppermute | solution.py:54
  780.6 64.5 %collective-permute-start.61 = (bf16[384,2048]{1,0:T(8,128)(2,1)}, bf16[384,2048]{1,0:T(8,128)(2,1)}, u32[]{:S(2)}, u32[]{:S(2)}) collective-permute-start(bf16[384,2048]{1,0:T(8,128)(2,1)} %add.447), channel_id=1, source_target_pairs={{1,0},{3,1},{5,3},{7,5},{6,7},{4,6},{2,4},{0,2},{9,8},{11,9},{13,1... | collective-permute-start | bytes 4718600 | tf_op jit(solution)/shard_map/ppermute | solution.py:57
  781.9 63.2 %collective-permute-start.57 = (bf16[384,2048]{1,0:T(8,128)(2,1)}, bf16[384,2048]{1,0:T(8,128)(2,1)}, u32[]{:S(2)}, u32[]{:S(2)}) collective-permute-start(bf16[384,2048]{1,0:T(8,128)(2,1)} %add.443), channel_id=1, source_target_pairs={{0,1},{1,3},{3,5},{5,7},{7,6},{6,4},{4,2},{2,0},{8,9},{9,11},{11,1... | collective-permute-start | bytes 4718600 | tf_op jit(solution)/shard_map/ppermute | solution.py:54
  790.8 63.2 %all-to-all-start.1 = ((bf16[4,512,512]{2,1,0:T(8,128)(2,1)}), bf16[4,512,512]{2,1,0:T(8,128)(2,1)S(1)}, u32[]{:S(2)}, u32[]{:S(2)}) async-start(bf16[4,512,512]{2,1,0:T(8,128)(2,1)} %bitcast.208), calls=%async_computation.1 | async-start | bytes 4194304 | tf_op jit(solution)/shard_map/all_to_all | solution.py:780
  849.2 83.4 %collective-permute-start.62 = (bf16[384,2048]{1,0:T(8,128)(2,1)}, bf16[384,2048]{1,0:T(8,128)(2,1)}, u32[]{:S(2)}, u32[]{:S(2)}) collective-permute-start(bf16[384,2048]{1,0:T(8,128)(2,1)} %add.448), channel_id=1, source_target_pairs={{1,0},{3,1},{5,3},{7,5},{6,7},{4,6},{2,4},{0,2},{9,8},{11,9},{13,1... | collective-permute-start | bytes 4718600 | tf_op jit(solution)/shard_map/ppermute | solution.py:57
  853.8 79.9 %collective-permute-start.58 = (bf16[384,2048]{1,0:T(8,128)(2,1)}, bf16[384,2048]{1,0:T(8,128)(2,1)}, u32[]{:S(2)}, u32[]{:S(2)}) collective-permute-start(bf16[384,2048]{1,0:T(8,128)(2,1)} %add.444), channel_id=1, source_target_pairs={{0,1},{1,3},{3,5},{5,7},{7,6},{6,4},{4,2},{2,0},{8,9},{9,11},{11,1... | collective-permute-start | bytes 4718600 | tf_op jit(solution)/shard_map/ppermute | solution.py:54
  1046.3 64.9 %collective-permute-start.69 = (bf16[384,2048]{1,0:T(8,128)(2,1)}, bf16[384,2048]{1,0:T(8,128)(2,1)}, u32[]{:S(2)}, u32[]{:S(2)}) collective-permute-start(bf16[384,2048]{1,0:T(8,128)(2,1)} %get-tuple-element.242), channel_id=1, source_target_pairs={{0,8},{8,0},{16,24},{24,16},{1,9},{9,1},{17,25},{25,17},{2,10},{10... | collective-permute-start | bytes 4718600 | tf_op jit(solution)/shard_map/ppermute | solution.py:539
  1049.8 61.4 %collective-permute-start.71 = (bf16[384,2048]{1,0:T(8,128)(2,1)}, bf16[384,2048]{1,0:T(8,128)(2,1)}, u32[]{:S(2)}, u32[]{:S(2)}) collective-permute-start(bf16[384,2048]{1,0:T(8,128)(2,1)} %add_convert_fusion.3), channel_id=1, source_target_pairs={{0,16},{16,0},{8,24},{24,8},{1,17},{17,1},{9,25},{25,9},{2,18},{18... | collective-permute-start | bytes 4718600 | tf_op jit(solution)/shard_map/ppermute | solution.py:54
  (159 other events, 3201.2 us)
Sparse Core Ops, SparseCore 0:
  19.6 64.2 all-gather.1
